TPU v7x, 256 devices: a whole 4x4x8 slice. The times are simulated.
256 devices in a mesh: var: 4 (over x_hi, core), ty: 8 (over x_lo, y), tx: 8 (over z).
Axes of the slice: x: 4 (x_hi: 2, x_lo: 2; x = x_hi * 2 + x_lo), y: 4, z: 8, core: 2. Of those that a mesh axis runs over, the one named last changes fastest.
Arguments:
- features: bfloat16 [256, 256, 180], P('ty', 'tx'), may hold values from -6 to 6
- labels: int32 [256, 256], P('ty', 'tx'), may hold values from 1 to 4
- qkv_weight: bfloat16 [2, 180, 540], replicated, may hold values from -0.4375 to 0.4375
- proj_weight: bfloat16 [2, 180, 180], replicated, may hold values from -0.4375 to 0.4375
- up_weight: bfloat16 [2, 180, 360], replicated, may hold values from -0.4375 to 0.4375
- down_weight: bfloat16 [2, 360, 180], replicated, may hold values from -0.3125 to 0.3125
- swin_bias: float32 [2, 6, 225], replicated, may hold values from -340 to 340
- recon_weight: bfloat16 [9, 180, 48], replicated, may hold values from -0.3125 to 0.3125
- refine_qkv: bfloat16 [48, 144], replicated, may hold values from -0.875 to 0.875
- refine_proj: bfloat16 [48, 48], replicated, may hold values from -0.875 to 0.875
- refine_bias: float32 [2, 225], replicated, may hold values from -340 to 340
Outputs:
- restored: float32 [3, 1024, 1024], P(None, 'ty', 'tx')
All inputs are finite; a program needn't handle non-finite values.
Results may differ from a plain program's by a relative error of at most 0.015.
Values may be sent and summed in bfloat16 or wider, within the bound.
A program may use at most 128 MiB of HBM per device.

v0:
```python
import functools

import jax
import jax.numpy as jnp
from jax import lax
from jax.experimental import pallas as pl
from jax.experimental.pallas import tpu as pltpu
from jax.sharding import PartitionSpec as P

MESH = pl.DeviceIdType.MESH

WIN = 8
SHIFT = 4
SCALE = 4
VAR_DEV = 2


EPSILON = 1e-05
MASKED = -1e30


def extended(cells, sides, width):
    for axis, dim in sides:
        count = lax.axis_size(axis)
        ends = count - 1
        head = lax.slice_in_dim(cells, 0, width, axis=dim)
        tail = lax.slice_in_dim(cells, cells.shape[dim] - width, cells.shape[dim], axis=dim)
        cells = jnp.concatenate(
            [
                lax.ppermute(tail, axis, [(i, (i + 1) % count) for i in range(ends)]),
                cells,
                lax.ppermute(head, axis, [((i + 1) % count, i) for i in range(ends)]),
            ],
            axis=dim,
        )
    return cells


def var_sum_kernel(count, part_ref, out_ref, held, send_sem, recv_sem, own_sem):
    me = lax.axis_index("var")
    barrier = pltpu.get_barrier_semaphore()
    for step in range(1, count):
        peer = lax.rem(me + step, count)
        pl.semaphore_signal(barrier, inc=1, device_id={"var": peer}, device_id_type=MESH)
    pl.semaphore_wait(barrier, count - 1)
    own = pltpu.make_async_copy(part_ref, held.at[me], own_sem)
    own.start()
    sends = []
    for step in range(1, count):
        peer = lax.rem(me + step, count)
        copy = pltpu.make_async_remote_copy(
            src_ref=part_ref,
            dst_ref=held.at[me],
            send_sem=send_sem.at[step - 1],
            recv_sem=recv_sem.at[me],
            device_id={"var": peer},
            device_id_type=MESH,
        )
        copy.start()
        sends.append(copy)
    own.wait()
    for copy in sends:
        copy.wait_send()
    for step in range(1, count):
        source = lax.rem(me + count - step, count)
        pltpu.make_async_remote_copy(
            src_ref=part_ref,
            dst_ref=held.at[source],
            send_sem=send_sem.at[step - 1],
            recv_sem=recv_sem.at[source],
            device_id={"var": source},
            device_id_type=MESH,
        ).wait_recv()
    total = held[0].astype(jnp.float32)
    for index in range(1, count):
        total = total + held[index].astype(jnp.float32)
    out_ref[...] = total


def var_sum(part):
    count = lax.axis_size("var")
    return pl.pallas_call(
        functools.partial(var_sum_kernel, count),
        out_shape=jax.ShapeDtypeStruct(part.shape, jnp.float32),
        in_specs=[pl.BlockSpec(memory_space=pltpu.VMEM)],
        out_specs=pl.BlockSpec(memory_space=pltpu.VMEM),
        scratch_shapes=[
            pltpu.VMEM((count,) + part.shape, part.dtype),
            pltpu.SemaphoreType.DMA((count - 1,)),
            pltpu.SemaphoreType.DMA((count,)),
            pltpu.SemaphoreType.DMA(()),
        ],
        compiler_params=pltpu.CompilerParams(collective_id=0, has_side_effects=True),
    )(part)


GROUP = 4
LANE = 128


def block_kernel(
    variants, heads, scale, x_ref, labq_ref, labk_ref, bias_ref, wqkv_ref, wp_ref, wup_ref, wdown_ref, out_ref
):
    inputs = x_ref.shape[0]
    tokens = x_ref.shape[2]
    labq = labq_ref[0]
    labk = labk_ref[0]
    slot_q = lax.broadcasted_iota(jnp.int32, (tokens, tokens), 0) // (WIN * WIN)
    slot_k = lax.broadcasted_iota(jnp.int32, (tokens, tokens), 1) // (WIN * WIN)
    match = (labq == labk) & (slot_q == slot_k)
    projected = []
    for index in range(inputs):
        normed = normalize(x_ref[index, 0]).astype(jnp.bfloat16)
        projected.append(
            jnp.dot(normed, wqkv_ref[...], preferred_element_type=jnp.float32).astype(jnp.bfloat16)
        )
    span = wp_ref.shape[0]
    width = wup_ref.shape[0] // heads
    lane = lax.broadcasted_iota(jnp.int32, (1, span), 1)
    for variant in range(variants):
        source = variant if inputs > 1 else 0
        qkv = projected[source]
        query = qkv[:, :span]
        key = qkv[:, span : 2 * span]
        value = qkv[:, 2 * span :]
        mixed = jnp.zeros((tokens, span), jnp.float32)
        for head in range(heads):
            mine = (lane >= head * width) & (lane < (head + 1) * width)
            scores = lax.dot_general(
                jnp.where(mine, query, jnp.zeros_like(query)),
                key,
                (((1,), (1,)), ((), ())),
                preferred_element_type=jnp.float32,
            )
            scores = scores * scale
            scores = (scores.reshape(GROUP, WIN * WIN, tokens) + bias_ref[variant, head][None]).reshape(
                tokens, tokens
            )
            scores = jnp.where(match, scores, MASKED)
            largest = jnp.max(scores, axis=-1, keepdims=True)
            weights = jnp.exp(scores - largest)
            probabilities = (weights / jnp.sum(weights, axis=-1, keepdims=True)).astype(jnp.bfloat16)
            mixed = mixed + jnp.dot(
                probabilities, jnp.where(mine, value, jnp.zeros_like(value)), preferred_element_type=jnp.float32
            )
        branch = jnp.dot(mixed.astype(jnp.bfloat16), wp_ref[...], preferred_element_type=jnp.float32)
        own = x_ref[source, 0].astype(jnp.float32)
        hidden_in = (own + branch).astype(jnp.bfloat16)
        normed = normalize(hidden_in).astype(jnp.bfloat16)
        hidden = jnp.dot(normed, wup_ref[...], preferred_element_type=jnp.float32)
        hidden = (0.5 * hidden * (1.0 + lax.erf(hidden * (2.0 ** -0.5)))).astype(jnp.bfloat16)
        result = hidden_in.astype(jnp.float32) + jnp.dot(
            hidden, wdown_ref[...], preferred_element_type=jnp.float32
        )
        out_ref[variant, 0] = result.astype(jnp.bfloat16)


def padded_weights(w_qkv, w_proj, heads):
    channels = w_proj.shape[0]
    span = -(-channels // LANE) * LANE
    columns = jnp.pad(w_qkv.reshape(channels, 3, channels), ((0, 0), (0, 0), (0, span - channels)))
    rows = jnp.pad(w_proj, ((0, span - channels), (0, 0)))
    return columns.reshape(channels, 3 * span), rows


def swin_block(windows, region, w_qkv, w_proj, w_up, w_down, bias_grid):
    inputs, count, cells, channels = windows.shape
    variants, heads = bias_grid.shape[:2]
    groups = -(-count // GROUP)
    extra = groups * GROUP - count
    windows = jnp.pad(windows, ((0, 0), (0, extra), (0, 0), (0, 0)))
    region = jnp.pad(region, ((0, extra), (0, 0)))
    tokens = GROUP * cells
    x = windows.reshape(inputs, groups, tokens, channels)
    labq = region.reshape(groups, tokens, 1)
    labk = region.reshape(groups, 1, tokens)
    bias = jnp.tile(bias_grid, (1, 1, 1, GROUP))
    wqkv, wp = padded_weights(w_qkv, w_proj, heads)
    scale = (channels // heads) ** (-0.5)
    whole = lambda shape: pl.BlockSpec(shape, lambda g: (0,) * len(shape))
    out = pl.pallas_call(
        functools.partial(block_kernel, variants, heads, scale),
        out_shape=jax.ShapeDtypeStruct((variants, groups, tokens, channels), jnp.bfloat16),
        grid=(groups,),
        in_specs=[
            pl.BlockSpec((inputs, 1, tokens, channels), lambda g: (0, g, 0, 0)),
            pl.BlockSpec((1, tokens, 1), lambda g: (g, 0, 0)),
            pl.BlockSpec((1, 1, tokens), lambda g: (g, 0, 0)),
            whole(bias.shape),
            whole(wqkv.shape),
            whole(wp.shape),
            whole(w_up.shape),
            whole(w_down.shape),
        ],
        out_specs=pl.BlockSpec((variants, 1, tokens, channels), lambda g: (0, g, 0, 0)),
        compiler_params=pltpu.CompilerParams(vmem_limit_bytes=48 * 1024 * 1024),
    )(x, labq, labk, bias, wqkv, wp, w_up, w_down)
    out = out.reshape(variants, groups * GROUP, cells, channels)
    return out[:, :count]


def block_on_grid(tokens, region, w_qkv, w_proj, w_up, w_down, bias_grid):
    height, breadth = tokens.shape[1], tokens.shape[2]
    windows = to_windows(tokens)
    region_windows = to_windows(region[None, :, :, None])[0, :, :, 0]
    out = swin_block(windows, region_windows, w_qkv, w_proj, w_up, w_down, bias_grid)
    return from_windows(out, height, breadth)


def normalize(values):
    values = values.astype(jnp.float32)
    average = jnp.mean(values, axis=-1, keepdims=True)
    centred = values - average
    spread = jnp.mean(centred * centred, axis=-1, keepdims=True)
    return centred * lax.rsqrt(spread + EPSILON)


def to_windows(grid):
    leading, height, breadth, channels = grid.shape
    grid = grid.reshape(leading, height // WIN, WIN, breadth // WIN, WIN, channels)
    grid = grid.transpose(0, 1, 3, 2, 4, 5)
    return grid.reshape(leading, height // WIN * (breadth // WIN), WIN * WIN, channels)


def from_windows(windows, height, breadth):
    leading, window_count, cells, channels = windows.shape
    windows = windows.reshape(leading, height // WIN, breadth // WIN, WIN, WIN, channels)
    windows = windows.transpose(0, 1, 3, 2, 4, 5)
    return windows.reshape(leading, height, breadth, channels)


def bias_table(offset_table, variant_codes):
    position = jnp.arange(WIN * WIN, dtype=jnp.int32)
    row_step = (position // WIN)[:, None] - (position // WIN)[None, :]
    across = (position % WIN)[:, None] - (position % WIN)[None, :]
    transpose_bit = (variant_codes // 4)[:, None, None]
    flip_rows = (variant_codes // 2 % 2)[:, None, None]
    flip_cols = (variant_codes % 2)[:, None, None]
    row_moved = jnp.where(flip_rows == 1, -row_step, row_step)
    col_moved = jnp.where(flip_cols == 1, -across, across)
    leading_step = jnp.where(transpose_bit == 1, col_moved, row_moved)
    trailing_step = jnp.where(transpose_bit == 1, row_moved, col_moved)
    table_index = (leading_step + WIN - 1) * (2 * WIN - 1) + trailing_step + WIN - 1
    slots = jnp.arange((2 * WIN - 1) * (2 * WIN - 1), dtype=jnp.int32)
    one_hot = (table_index[..., None] == slots).astype(jnp.bfloat16)
    high = lax.reduce_precision(offset_table, exponent_bits=8, mantissa_bits=7)
    rest = offset_table - high
    middle = lax.reduce_precision(rest, exponent_bits=8, mantissa_bits=7)
    low = rest - middle
    parts = jnp.concatenate([high, middle, low], axis=0).astype(jnp.bfloat16)
    picked = jnp.einsum("vqkt,ht->vhqk", one_hot, parts, preferred_element_type=jnp.float32)
    heads = offset_table.shape[0]
    return (picked[:, :heads] + picked[:, heads : 2 * heads]) + picked[:, 2 * heads :]


def variant_kernels(kernel, variant_codes):
    transpose_bit = (variant_codes // 4)[:, None]
    flip_rows = (variant_codes // 2 % 2)[:, None]
    flip_cols = (variant_codes % 2)[:, None]
    kernel_spot = jnp.arange(9, dtype=jnp.int32)
    step_row = (kernel_spot // 3 - 1)[None, :]
    step_col = (kernel_spot % 3 - 1)[None, :]
    row_moved = jnp.where(flip_rows == 1, -step_row, step_row)
    col_moved = jnp.where(flip_cols == 1, -step_col, step_col)
    source_row = jnp.where(transpose_bit == 1, col_moved, row_moved)
    source_col = jnp.where(transpose_bit == 1, row_moved, col_moved)
    source = (source_row + 1) * 3 + source_col + 1
    pick_place = (source[:, :, None] == kernel_spot[None, None, :]).astype(jnp.bfloat16)
    channel = jnp.arange(kernel.shape[-1], dtype=jnp.int32)
    colour = (channel // (SCALE * SCALE))[None, :]
    sub_row = (channel % (SCALE * SCALE) // SCALE)[None, :]
    sub_col = (channel % SCALE)[None, :]
    sub_row_moved = jnp.where(flip_rows == 1, SCALE - 1 - sub_row, sub_row)
    sub_col_moved = jnp.where(flip_cols == 1, SCALE - 1 - sub_col, sub_col)
    anchor_row = jnp.where(transpose_bit == 1, sub_col_moved, sub_row_moved)
    anchor_col = jnp.where(transpose_bit == 1, sub_row_moved, sub_col_moved)
    anchor = colour * SCALE * SCALE + anchor_row * SCALE + anchor_col
    pick_channel = (channel[None, :, None] == anchor[:, None, :]).astype(jnp.bfloat16)
    placed = jnp.einsum(
        "vpq,qcs->vpcs", pick_place, kernel, preferred_element_type=jnp.float32
    ).astype(jnp.bfloat16)
    return jnp.einsum(
        "vpcs,vso->vpco", placed, pick_channel, preferred_element_type=jnp.float32
    ).astype(jnp.bfloat16)


def attend(normed, region, w_qkv, w_proj, bias_grid):
    head_count = bias_grid.shape[1]
    leading, window_count, cells, channels = normed.shape
    head_width = channels // head_count
    projected = jnp.einsum(
        "lnsc,ce->lnse", normed, w_qkv, preferred_element_type=jnp.float32
    ).astype(jnp.bfloat16)
    projected = projected.reshape(leading, window_count, cells, 3, head_count, head_width)
    queries = projected[:, :, :, 0]
    key_part = projected[:, :, :, 1]
    value_part = projected[:, :, :, 2]
    scores = jnp.einsum("lnqhd,lnkhd->lnhqk", queries, key_part, preferred_element_type=jnp.float32)
    scores = scores * head_width ** (-0.5) + bias_grid[:, None]
    matches = region[:, None, :, None] == region[:, None, None, :]
    scores = jnp.where(matches[None], scores, MASKED)
    largest = jnp.max(scores, axis=-1, keepdims=True)
    weights = jnp.exp(scores - largest)
    probabilities = (weights / jnp.sum(weights, axis=-1, keepdims=True)).astype(jnp.bfloat16)
    value_part = jnp.broadcast_to(value_part, (probabilities.shape[0],) + value_part.shape[1:])
    mixed = jnp.einsum(
        "lnhqk,lnkhd->lnqhd", probabilities, value_part, preferred_element_type=jnp.float32
    ).astype(jnp.bfloat16)
    mixed = mixed.reshape(probabilities.shape[0], window_count, cells, channels)
    return jnp.einsum("lnsc,ce->lnse", mixed, w_proj, preferred_element_type=jnp.float32)


def attention_half(tokens, region, w_qkv, w_proj, bias_grid):
    height, breadth = (tokens.shape[1], tokens.shape[2])
    windows = to_windows(tokens)
    region_windows = to_windows(region[None, :, :, None])[0, :, :, 0]
    normed = normalize(windows).astype(jnp.bfloat16)
    branch = attend(normed, region_windows, w_qkv, w_proj, bias_grid)
    result = (windows.astype(jnp.float32) + branch).astype(jnp.bfloat16)
    return from_windows(result, height, breadth)


def feed_forward(tokens, w_up, w_down):
    normed = normalize(tokens).astype(jnp.bfloat16)
    hidden = jnp.einsum("...c,ce->...e", normed, w_up, preferred_element_type=jnp.float32)
    hidden = jax.nn.gelu(hidden, approximate=False).astype(jnp.bfloat16)
    output = tokens.astype(jnp.float32) + jnp.einsum(
        "...e,ec->...c", hidden, w_down, preferred_element_type=jnp.float32
    )
    return output.astype(jnp.bfloat16)


def reconstruct(padded, kernels, height, breadth):
    accumulated = jnp.zeros((padded.shape[0], height, breadth, kernels.shape[-1]), jnp.float32)
    for kernel_spot in range(9):
        spot_row, spot_col = (kernel_spot // 3, kernel_spot % 3)
        window = padded[:, spot_row : spot_row + height, spot_col : spot_col + breadth]
        accumulated = accumulated + jnp.einsum(
            "vrcd,vde->vrce", window, kernels[:, kernel_spot], preferred_element_type=jnp.float32
        )
    return accumulated


def refine(average, region, w_qkv, w_proj, bias_grid):
    normed = normalize(average).astype(jnp.bfloat16)[None]
    return average + attend(normed, region, w_qkv, w_proj, bias_grid)[0]


def local(
    features,
    labels,
    qkv_weight,
    proj_weight,
    up_weight,
    down_weight,
    swin_bias,
    recon_weight,
    refine_qkv,
    refine_proj,
    refine_bias,
):
    height, breadth, channels = features.shape
    variant_codes = lax.axis_index("var") * VAR_DEV + jnp.arange(VAR_DEV, dtype=jnp.int32)
    first_bias = bias_table(swin_bias[0], variant_codes)
    second_bias = bias_table(swin_bias[1], variant_codes)
    region = extended(labels, (("ty", 0), ("tx", 1)), SHIFT)
    block_one = block_on_grid(
        features[None], labels, qkv_weight[0], proj_weight[0], up_weight[0], down_weight[0], first_bias
    )
    shifted = extended(block_one, (("ty", 1), ("tx", 2)), SHIFT)
    block_two = block_on_grid(
        shifted, region, qkv_weight[1], proj_weight[1], up_weight[1], down_weight[1], second_bias
    )
    padded = block_two[:, SHIFT - 1 : SHIFT + height + 1, SHIFT - 1 : SHIFT + breadth + 1]
    row = lax.axis_index("ty") * height - 1 + jnp.arange(height + 2)
    col = lax.axis_index("tx") * breadth - 1 + jnp.arange(breadth + 2)
    inside = ((row >= 0) & (row < lax.axis_size("ty") * height))[:, None] & (
        (col >= 0) & (col < lax.axis_size("tx") * breadth)
    )[None, :]
    padded = jnp.where(inside[None, :, :, None], padded, jnp.zeros_like(padded))
    kernels = variant_kernels(recon_weight, variant_codes)
    summed = jnp.sum(reconstruct(padded, kernels, height, breadth), axis=0)
    region_windows = to_windows(labels[None, :, :, None])[0, :, :, 0]
    refine_grid = bias_table(refine_bias, jnp.zeros((1,), jnp.int32))
    rows, cols, depth = summed.shape
    combined = var_sum(summed.astype(jnp.bfloat16).reshape(rows, cols * depth)).reshape(rows, cols, depth)
    refined = refine(
        to_windows(combined[None])[0] / 8.0, region_windows, refine_qkv, refine_proj, refine_grid
    )
    refined = lax.optimization_barrier(refined)
    colours = refined.shape[-1] // (SCALE * SCALE)
    picture = refined.reshape(
        height // WIN, breadth // WIN, WIN, WIN, colours * SCALE, SCALE
    ).transpose(4, 0, 2, 1, 3, 5)
    picture = picture.reshape(colours, SCALE, height, breadth * SCALE).transpose(0, 2, 1, 3)
    return picture.reshape(colours, SCALE * height, SCALE * breadth)


def solution(mesh):
    placed = (P("ty", "tx", None), P("ty", "tx"), P(), P(), P(), P(), P(), P(), P(), P(), P())
    return jax.shard_map(
        local, mesh=mesh, in_specs=placed, out_specs=P(None, "ty", "tx"), check_vma=False
    )
```

profile of v0, /device:TPU:99, one launch (start us, length us, event | category | flops | bytes accessed | tf_op | source)
XLA Modules:
  0.0 142.4 jit_solution(8332742226850135243)
XLA Ops:
  0.0 0.8 reshape_broadcast_in_dim.11
  1.2 0.8 fusion.91
  2.0 0.7 add_add_fusion
  2.8 0.6 copy-done.13
  3.4 1.8 %fusion.8 = f32[2,18,64,64]{3,1,2,0:T(8,128)S(1)} fusion(s32[2,64,64]{2,1,0:T(8,128)S(1)} %fusion.35, bf16[6,225]{1,0:T(8,128)(2,1)S(1)} %get-tuple-element.42, bf16[6,225]{1,0:T(8,128)(2,1)S(1)} %get-tuple-element.41, bf16[6,225]{1,0:T(8,128)(2,1)S(1)} %get-tuple-element.43), kind=kOutput, calls=%fused_computation.11 | convolution fusion | flops 68222704 | bytes 630692 | tf_op jit(solution)/shard_map/vqkt,ht->vhqk/dot_general | solution.py:251
  5.7 0.9 tile.9.bias_ref
  6.6 1.5 %fusion.87 = (bf16[1,180,360]{2,0,1:T(2,128)(2,1)S(1)}, bf16[1,180,360]{2,0,1:T(2,128)(2,1)S(1)}) fusion(bf16[2,180,360]{2,0,1:T(2,128)(2,1)} %param.15), kind=kLoop, calls=%fused_computation.206 | loop fusion | bytes 518400 | tf_op jit(solution)/shard_map/slice | solution.py:372
  8.1 2.0 %fusion.88 = (bf16[1,180,180]{2,0,1:T(2,128)(2,1)S(1)}, bf16[1,180,180]{2,0,1:T(2,128)(2,1)}) fusion(bf16[2,180,180]{2,0,1:T(2,128)(2,1)} %param.14), kind=kLoop, calls=%fused_computation.207 | loop fusion | bytes 259200 | tf_op jit(solution)/shard_map/slice | solution.py:372
  10.1 1.4 fusion.85
  11.5 0.7 copy.70
  12.3 1.6 %copy_bitcast_fusion.2 = (bf16[180,180]{1,0:T(8,128)(2,1)}, bf16[180,180]{1,0:T(8,128)(2,1)S(1)}) fusion(bf16[1,180,180]{2,0,1:T(2,128)(2,1)S(1)} %get-tuple-element.15, bf16[1,180,180]{2,0,1:T(2,128)(2,1)} %get-tuple-element.16), kind=kLoop, calls=%fused_computation.70 | loop fusion | bytes 259200 | tf_op jit(solution)/shard_map/squeeze | solution.py:372
  14.2 1.1 fusion.86
  15.5 1.1 copy.66
  16.7 13.7 %shard_map.109 = bf16[2,4,256,180]{3,2,1,0:T(8,128)(2,1)S(1)} custom-call(bf16[1,4,256,180]{3,2,1,0:T(8,128)(2,1)S(1)} %bitcast.222, s32[4,256,1]{2,1,0:T(8,128)S(1)} %reshape.823.labq_ref, s32[4,1,256]{2,1,0:T(1,128)S(1)} %reshape.786.labk_ref, f32[2,6,64,256]{3,2,1,0:T(8,128)S(1)} %tile.9.bias_ref, bf16[180,768]{1,0:T(8,128)(2,1)S(1)} %copy.118.wqkv_ref, ...), custom_call_target="tpu_custom_call" | custom-call | tf_op jit(solution)/shard_map/pallas_call | solution.py:181
  30.5 0.7 fusion.84
  31.2 3.2 %collective-permute-start = (bf16[2,4,32,180]{3,2,1,0:T(8,128)(2,1)}, bf16[2,4,32,180]{3,2,1,0:T(8,128)(2,1)S(1)}, u32[]{:S(2)}, u32[]{:S(2)}) collective-permute-start(bf16[2,4,32,180]{3,2,1,0:T(8,128)(2,1)} %get-tuple-element.7), channel_id=1, source_target_pairs={{0,8},{8,16},{16,24},{24,32},{32,40},{40,48},{48,56},{1,9},{9,17},... | collective-permute-start | bytes 276488 | tf_op jit(solution)/shard_map/ppermute | solution.py:30
  34.4 4.2 %collective-permute-start.1 = (bf16[2,4,32,180]{3,2,1,0:T(8,128)(2,1)}, bf16[2,4,32,180]{3,2,1,0:T(8,128)(2,1)}, u32[]{:S(2)}, u32[]{:S(2)}) collective-permute-start(bf16[2,4,32,180]{3,2,1,0:T(8,128)(2,1)} %get-tuple-element.8), channel_id=1, source_target_pairs={{8,0},{16,8},{24,16},{32,24},{40,32},{48,40},{56,48},{9,1},{17,9},... | collective-permute-start | bytes 276488 | tf_op jit(solution)/shard_map/ppermute | solution.py:32
  38.6 1.9 %collective-permute-start.4 = (s32[4,32]{1,0:T(4,128)S(1)}, s32[4,32]{1,0:T(4,128)S(1)}, u32[]{:S(2)}, u32[]{:S(2)}) collective-permute-start(s32[4,32]{1,0:T(4,128)S(1)} %get-tuple-element.19), channel_id=1, source_target_pairs={{0,8},{8,16},{16,24},{24,32},{32,40},{40,48},{48,56},{1,9},{9,17},... | collective-permute-start | bytes 1544 | tf_op jit(solution)/shard_map/ppermute | solution.py:30
  40.6 5.7 %collective-permute-start.5 = (s32[4,32]{1,0:T(4,128)S(1)}, s32[4,32]{1,0:T(4,128)S(1)}, u32[]{:S(2)}, u32[]{:S(2)}) collective-permute-start(s32[4,32]{1,0:T(4,128)S(1)} %get-tuple-element.20), channel_id=1, source_target_pairs={{8,0},{16,8},{24,16},{32,24},{40,32},{48,40},{56,48},{9,1},{17,9},... | collective-permute-start | bytes 1544 | tf_op jit(solution)/shard_map/ppermute | solution.py:32
  46.2 0.6 fusion.70
  46.8 0.6 fusion.77
  47.4 0.6 and_select_fusion
  48.0 0.5 fusion.67
  48.5 0.5 broadcast_subtract_fusion.3
  49.0 1.8 %fusion.9 = f32[2,18,64,64]{3,1,2,0:T(8,128)S(1)} fusion(s32[2,64,64]{2,1,0:T(8,128)S(1)} %copy-done.14, bf16[6,225]{1,0:T(8,128)(2,1)S(1)} %get-tuple-element.24, bf16[6,225]{1,0:T(8,128)(2,1)S(1)} %get-tuple-element.25, bf16[6,225]{1,0:T(8,128)(2,1)S(1)} %get-tuple-element.23), kind=kOutput, calls=%fused_computation.12 | convolution fusion | flops 68222704 | bytes 630692 | tf_op jit(solution)/shard_map/vqkt,ht->vhqk/dot_general | solution.py:251
  51.1 0.5 copy-done.18
  51.6 1.0 fusion.14
  52.7 0.9 broadcast_compare_fusion
  53.6 0.7 fusion.63
  54.8 1.1 convolution_convert_fusion.2
  56.2 1.7 %pad_maximum_fusion.3 = (bf16[2,40,4,180]{3,2,1,0:T(4,128)(2,1)}, bf16[2,40,4,180]{3,2,1,0:T(4,128)(2,1)}) fusion(bf16[2,4,32,180]{3,2,1,0:T(8,128)(2,1)} %collective-permute-done.1, bf16[2,32,32,180]{3,2,1,0:T(8,128)(2,1)S(1)} %bitcast.227, bf16[2,4,32,180]{3,2,1,0:T(8,128)(2,1)S(1)} %collective-permute-done), kind=kLoop, calls=%fused_computation.64 | loop fusion | flops 691200 | bytes 1152000 | tf_op jit(solution)/shard_map/slice | solution.py:27
  57.9 4.8 %collective-permute-start.2 = (bf16[2,40,4,180]{3,2,1,0:T(4,128)(2,1)}, bf16[2,40,4,180]{3,2,1,0:T(4,128)(2,1)}, u32[]{:S(2)}, u32[]{:S(2)}) collective-permute-start(bf16[2,40,4,180]{3,2,1,0:T(4,128)(2,1)} %get-tuple-element.5), channel_id=1, source_target_pairs={{0,1},{1,2},{2,3},{3,4},{4,5},{5,6},{6,7},{8,9},{9,10},{10,11},{11... | collective-permute-start | bytes 345608 | tf_op jit(solution)/shard_map/ppermute | solution.py:30
  62.6 1.9 %collective-permute-start.3 = (bf16[2,40,4,180]{3,2,1,0:T(4,128)(2,1)}, bf16[2,40,4,180]{3,2,1,0:T(4,128)(2,1)}, u32[]{:S(2)}, u32[]{:S(2)}) collective-permute-start(bf16[2,40,4,180]{3,2,1,0:T(4,128)(2,1)} %get-tuple-element.6), channel_id=1, source_target_pairs={{1,0},{2,1},{3,2},{4,3},{5,4},{6,5},{7,6},{9,8},{10,9},{11,10},{12... | collective-permute-start | bytes 345608 | tf_op jit(solution)/shard_map/ppermute | solution.py:32
  64.6 0.7 fusion.89
  65.2 4.6 %collective-permute-start.6 = (s32[40,4]{1,0:T(8,128)}, s32[40,4]{1,0:T(8,128)S(1)}, u32[]{:S(2)}, u32[]{:S(2)}) collective-permute-start(s32[40,4]{1,0:T(8,128)} %get-tuple-element.17), channel_id=1, source_target_pairs={{0,1},{1,2},{2,3},{3,4},{4,5},{5,6},{6,7},{8,9},{9,10},{10,11},{11... | collective-permute-start | bytes 1928 | tf_op jit(solution)/shard_map/ppermute | solution.py:30
  69.8 1.9 %collective-permute-start.7 = (s32[40,4]{1,0:T(8,128)S(1)}, s32[40,4]{1,0:T(8,128)S(1)}, u32[]{:S(2)}, u32[]{:S(2)}) collective-permute-start(s32[40,4]{1,0:T(8,128)S(1)} %get-tuple-element.18), channel_id=1, source_target_pairs={{1,0},{2,1},{3,2},{4,3},{5,4},{6,5},{7,6},{9,8},{10,9},{11,10},{12... | collective-permute-start | bytes 1928 | tf_op jit(solution)/shard_map/ppermute | solution.py:32
  71.7 1.5 %tile.20 = f32[2,6,64,4,64]{4,3,2,1,0:T(4,128)} broadcast(f32[2,6,64,64]{3,2,1,0:T(8,128)S(1)} %copy.80), dimensions={0,1,2,4} | broadcast | bytes 983040 | tf_op jit(solution)/shard_map/tile | solution.py:177
  73.2 2.3 %tile.21.bias_ref = f32[2,6,64,256]{3,2,1,0:T(8,128)S(1)} reshape(f32[2,6,64,4,64]{4,3,2,1,0:T(4,128)} %tile.20) | data formatting | bytes 1572864 | tf_op jit(solution)/shard_map/tile | solution.py:177
  75.6 0.8 copy.81
  76.9 0.7 copy.96
  77.9 0.9 reshape.824.labq_ref
  78.9 2.1 %pad_maximum_fusion = bf16[2,40,40,180]{3,2,1,0:T(8,128)(2,1)S(1)} fusion(bf16[2,40,4,180]{3,2,1,0:T(4,128)(2,1)} %collective-permute-done.3, bf16[2,4,32,180]{3,2,1,0:T(8,128)(2,1)} %collective-permute-done.1, bf16[2,32,32,180]{3,2,1,0:T(8,128)(2,1)S(1)} %bitcast.228, bf16[2,4,32,180]{3,2,1,0:T(8,128)(2,1)} %copy-done.9, ...), kind=kLoop, calls=%fused_computation.9 | loop fusion | flops 5760000 | bytes 2304000 | tf_op jit(solution)/shard_map/concatenate | solution.py:28
  81.2 0.4 pad.24
  81.7 27.8 %shard_map.110 = bf16[2,7,256,180]{3,2,1,0:T(8,128)(2,1)S(1)} custom-call(bf16[2,7,256,180]{3,2,1,0:T(8,128)(2,1)S(1)} %bitcast.219, s32[7,256,1]{2,1,0:T(8,128)S(1)} %reshape.824.labq_ref, s32[7,1,256]{2,1,0:T(1,128)S(1)} %reshape.793.labk_ref, f32[2,6,64,256]{3,2,1,0:T(8,128)S(1)} %tile.21.bias_ref, bf16[180,768]{1,0:T(8,128)(2,1)S(1)} %copy.119.wqkv_ref, ...), custom_call_target="tpu_custom_call" | custom-call | tf_op jit(solution)/shard_map/pallas_call | solution.py:181
  109.7 0.4 slice_select_fusion
  110.1 0.6 copy-done.3
  111.1 0.4 convolution_add_fusion.7
  111.5 0.4 convolution_add_fusion.6
  112.0 0.4 convolution_add_fusion.5
  112.4 0.4 convolution_add_fusion.4
  112.8 0.4 convolution_add_fusion.3
  113.3 0.4 convolution_add_fusion.2
  113.7 0.4 convolution_add_fusion.1
  114.1 0.4 fusion.13
  114.6 1.0 convert_element_type.54.part_ref
  115.6 12.4 %shard_map.111 = f32[32,1536]{1,0:T(8,128)} custom-call(bf16[32,1536]{1,0:T(8,128)(2,1)} %convert_element_type.54.part_ref), custom_call_target="tpu_custom_call" | custom-call | tf_op jit(solution)/shard_map/pallas_call | solution.py:82
  128.0 0.9 broadcast_multiply_fusion
  130.1 0.5 convolution_convert_fusion.1
  131.3 0.7 fusion.92
  132.9 1.0 convolution_add_fusion.8
  133.9 1.9 %reshape.803 = f32[4,4,8,8,12,4]{3,2,5,4,1,0:T(8,128)S(1)} reshape(f32[16,64,48]{1,2,0:T(8,128)} %convolution_add_fusion.8) | data formatting | bytes 393216 | tf_op jit(solution)/shard_map/reshape | solution.py:392
  135.8 2.8 %copy.100 = f32[12,4,8,4,8,4]{2,1,5,4,3,0:T(4,128)} copy(f32[12,4,8,4,8,4]{4,2,5,0,3,1:T(8,128)S(1)} %bitcast.225) | data formatting | bytes 393216 | tf_op jit(solution)/shard_map/transpose | solution.py:394
  138.6 2.8 %reshape.804 = f32[3,4,32,128]{2,3,1,0:T(8,128)S(1)} reshape(f32[12,4,8,4,8,4]{2,1,5,4,3,0:T(4,128)} %copy.100) | data formatting | bytes 393216 | tf_op jit(solution)/shard_map/reshape | solution.py:395
  141.5 0.9 copy.101
  (115 shorter events, 7.1 us)
Async XLA Ops:
  0.0 130.1 %copy-start = (bf16[48,144]{1,0:T(8,128)(2,1)S(1)}, bf16[48,144]{1,0:T(8,128)(2,1)}, u32[]{:S(2)}) copy-start(bf16[48,144]{1,0:T(8,128)(2,1)} %param.19) | copy-start | bytes 41476
  0.9 4.3 %copy-start.6 = (s32[1,4,8,4,8,1]{4,2,3,1,5,0:T(8,128)}, s32[1,4,8,4,8,1]{4,2,3,1,5,0:T(8,128)S(1)}, u32[]{:S(2)}) copy-start(s32[1,4,8,4,8,1]{4,2,3,1,5,0:T(8,128)S(1)} %copy.163) | copy-start | bytes 12292
  2.8 0.6 copy-start.13
  5.7 4.4 %copy-start.1 = (bf16[2,180,540]{2,0,1:T(2,128)(2,1)S(1)}, bf16[2,180,540]{2,0,1:T(2,128)(2,1)}, u32[]{:S(2)}) copy-start(bf16[2,180,540]{2,0,1:T(2,128)(2,1)} %param.13) | copy-start | bytes 1166404
  11.5 2.6 %copy-start.5 = (bf16[2,360,180]{1,0,2:T(2,128)(2,1)S(1)}, bf16[2,360,180]{1,0,2:T(2,128)(2,1)}, u32[]{:S(2)}) copy-start(bf16[2,360,180]{1,0,2:T(2,128)(2,1)} %param.16) | copy-start | bytes 777604
  30.3 8.3 %copy-start.11 = (s32[32,32]{1,0:T(8,128)S(1)}, s32[32,32]{1,0:T(8,128)}, u32[]{:S(2)}) copy-start(s32[32,32]{1,0:T(8,128)} %param.12) | copy-start | bytes 12292
  30.3 18.6 %copy-start.7 = (s32[1,4,8,4,8,1]{4,2,3,1,5,0:T(8,128)S(1)}, s32[1,4,8,4,8,1]{4,2,3,1,5,0:T(8,128)}, u32[]{:S(2)}) copy-start(s32[1,4,8,4,8,1]{4,2,3,1,5,0:T(8,128)} %copy-done.6) | copy-start | bytes 12292
  30.4 18.7 %copy-start.14 = (s32[2,64,64]{2,1,0:T(8,128)S(1)}, s32[2,64,64]{2,1,0:T(8,128)}, u32[]{:S(2)}) copy-start(s32[2,64,64]{2,1,0:T(8,128)} %copy-done.13) | copy-start | bytes 98308
  31.2 24.9 %collective-permute-start = (bf16[2,4,32,180]{3,2,1,0:T(8,128)(2,1)}, bf16[2,4,32,180]{3,2,1,0:T(8,128)(2,1)S(1)}, u32[]{:S(2)}, u32[]{:S(2)}) collective-permute-start(bf16[2,4,32,180]{3,2,1,0:T(8,128)(2,1)} %get-tuple-element.7), channel_id=1, source_target_pairs={{0,8},{8,16},{16,24},{24,32},{32,40},{40,48},{48,56},{1,9},{9,17},... | collective-permute-start | bytes 276488 | tf_op jit(solution)/shard_map/ppermute | solution.py:30
  34.4 21.7 %collective-permute-start.1 = (bf16[2,4,32,180]{3,2,1,0:T(8,128)(2,1)}, bf16[2,4,32,180]{3,2,1,0:T(8,128)(2,1)}, u32[]{:S(2)}, u32[]{:S(2)}) collective-permute-start(bf16[2,4,32,180]{3,2,1,0:T(8,128)(2,1)} %get-tuple-element.8), channel_id=1, source_target_pairs={{8,0},{16,8},{24,16},{32,24},{40,32},{48,40},{56,48},{9,1},{17,9},... | collective-permute-start | bytes 276488 | tf_op jit(solution)/shard_map/ppermute | solution.py:32
  38.6 17.5 %collective-permute-start.4 = (s32[4,32]{1,0:T(4,128)S(1)}, s32[4,32]{1,0:T(4,128)S(1)}, u32[]{:S(2)}, u32[]{:S(2)}) collective-permute-start(s32[4,32]{1,0:T(4,128)S(1)} %get-tuple-element.19), channel_id=1, source_target_pairs={{0,8},{8,16},{16,24},{24,32},{32,40},{40,48},{48,56},{1,9},{9,17},... | collective-permute-start | bytes 1544 | tf_op jit(solution)/shard_map/ppermute | solution.py:30
  40.6 15.5 %collective-permute-start.5 = (s32[4,32]{1,0:T(4,128)S(1)}, s32[4,32]{1,0:T(4,128)S(1)}, u32[]{:S(2)}, u32[]{:S(2)}) collective-permute-start(s32[4,32]{1,0:T(4,128)S(1)} %get-tuple-element.20), channel_id=1, source_target_pairs={{8,0},{16,8},{24,16},{32,24},{40,32},{48,40},{56,48},{9,1},{17,9},... | collective-permute-start | bytes 1544 | tf_op jit(solution)/shard_map/ppermute | solution.py:32
  50.9 0.7 copy-start.18
  50.9 0.8 copy-start.16
  50.9 2.7 %copy-start.24 = (s32[9]{0:T(128)S(1)}, s32[9]{0:T(128)}, u32[]{:S(2)}) copy-start(s32[9]{0:T(128)} %get-tuple-element.50) | copy-start | bytes 112
  50.9 2.7 %copy-start.25 = (s32[9]{0:T(128)S(1)}, s32[9]{0:T(128)}, u32[]{:S(2)}) copy-start(s32[9]{0:T(128)} %get-tuple-element.51) | copy-start | bytes 112
  50.9 2.7 %copy-start.26 = (s32[9]{0:T(128)S(1)}, s32[9]{0:T(128)}, u32[]{:S(2)}) copy-start(s32[9]{0:T(128)} %get-tuple-element.52) | copy-start | bytes 112
  51.0 3.3 %copy-start.8 = (bf16[9,180,48]{1,2,0:T(8,128)(2,1)S(1)}, bf16[9,180,48]{1,2,0:T(8,128)(2,1)}, u32[]{:S(2)}) copy-start(bf16[9,180,48]{1,2,0:T(8,128)(2,1)} %param.18) | copy-start | bytes 466564
  51.0 3.7 %copy-start.19 = (s32[48]{0:T(128)S(1)}, s32[48]{0:T(128)}, u32[]{:S(2)}) copy-start(s32[48]{0:T(128)} %get-tuple-element.54) | copy-start | bytes 580
  51.0 3.7 %copy-start.20 = (s32[48]{0:T(128)S(1)}, s32[48]{0:T(128)}, u32[]{:S(2)}) copy-start(s32[48]{0:T(128)} %get-tuple-element.55) | copy-start | bytes 580
  51.0 3.7 %copy-start.21 = (s32[48]{0:T(128)S(1)}, s32[48]{0:T(128)}, u32[]{:S(2)}) copy-start(s32[48]{0:T(128)} %get-tuple-element.56) | copy-start | bytes 580
  51.1 3.7 %copy-start.22 = (s32[48]{0:T(128)S(1)}, s32[48]{0:T(128)}, u32[]{:S(2)}) copy-start(s32[48]{0:T(128)} %get-tuple-element.57) | copy-start | bytes 580
  51.1 3.7 %copy-start.23 = (s32[48]{0:T(128)S(1)}, s32[48]{0:T(128)}, u32[]{:S(2)}) copy-start(s32[48]{0:T(128)} %broadcast_subtract_fusion.3) | copy-start | bytes 580
  56.1 17.1 %copy-start.9 = (bf16[2,4,32,180]{3,2,1,0:T(8,128)(2,1)}, bf16[2,4,32,180]{3,2,1,0:T(8,128)(2,1)S(1)}, u32[]{:S(2)}) copy-start(bf16[2,4,32,180]{3,2,1,0:T(8,128)(2,1)S(1)} %collective-permute-done) | copy-start | bytes 276484
  57.9 21.0 %collective-permute-start.2 = (bf16[2,40,4,180]{3,2,1,0:T(4,128)(2,1)}, bf16[2,40,4,180]{3,2,1,0:T(4,128)(2,1)}, u32[]{:S(2)}, u32[]{:S(2)}) collective-permute-start(bf16[2,40,4,180]{3,2,1,0:T(4,128)(2,1)} %get-tuple-element.5), channel_id=1, source_target_pairs={{0,1},{1,2},{2,3},{3,4},{4,5},{5,6},{6,7},{8,9},{9,10},{10,11},{11... | collective-permute-start | bytes 345608 | tf_op jit(solution)/shard_map/ppermute | solution.py:30
  62.6 16.3 %collective-permute-start.3 = (bf16[2,40,4,180]{3,2,1,0:T(4,128)(2,1)}, bf16[2,40,4,180]{3,2,1,0:T(4,128)(2,1)}, u32[]{:S(2)}, u32[]{:S(2)}) collective-permute-start(bf16[2,40,4,180]{3,2,1,0:T(4,128)(2,1)} %get-tuple-element.6), channel_id=1, source_target_pairs={{1,0},{2,1},{3,2},{4,3},{5,4},{6,5},{7,6},{9,8},{10,9},{11,10},{12... | collective-permute-start | bytes 345608 | tf_op jit(solution)/shard_map/ppermute | solution.py:32
  65.2 12.4 %collective-permute-start.6 = (s32[40,4]{1,0:T(8,128)}, s32[40,4]{1,0:T(8,128)S(1)}, u32[]{:S(2)}, u32[]{:S(2)}) collective-permute-start(s32[40,4]{1,0:T(8,128)} %get-tuple-element.17), channel_id=1, source_target_pairs={{0,1},{1,2},{2,3},{3,4},{4,5},{5,6},{6,7},{8,9},{9,10},{10,11},{11... | collective-permute-start | bytes 1928 | tf_op jit(solution)/shard_map/ppermute | solution.py:30
  69.8 7.8 %collective-permute-start.7 = (s32[40,4]{1,0:T(8,128)S(1)}, s32[40,4]{1,0:T(8,128)S(1)}, u32[]{:S(2)}, u32[]{:S(2)}) collective-permute-start(s32[40,4]{1,0:T(8,128)S(1)} %get-tuple-element.18), channel_id=1, source_target_pairs={{1,0},{2,1},{3,2},{4,3},{5,4},{6,5},{7,6},{9,8},{10,9},{11,10},{12... | collective-permute-start | bytes 1928 | tf_op jit(solution)/shard_map/ppermute | solution.py:32
  73.2 2.3 %copy-start.10 = (bf16[180,180]{1,0:T(8,128)(2,1)S(1)}, bf16[180,180]{1,0:T(8,128)(2,1)}, u32[]{:S(2)}) copy-start(bf16[180,180]{1,0:T(8,128)(2,1)} %get-tuple-element.44) | copy-start | bytes 194404
  73.2 2.4 %copy-start.2 = (bf16[1,180,540]{2,0,1:T(2,128)(2,1)S(1)}, bf16[1,180,540]{2,0,1:T(2,128)(2,1)}, u32[]{:S(2)}) copy-start(bf16[1,180,540]{2,0,1:T(2,128)(2,1)} %get-tuple-element.9) | copy-start | bytes 583204
  75.5 1.1 copy-start.4
  109.7 1.0 copy-start.3
  129.5 1.5 %copy-start.12 = (pred[16,64,64]{1,2,0:T(8,128)(4,1)S(1)}, pred[16,64,64]{1,2,0:T(8,128)(4,1)}, u32[]{:S(2)}) copy-start(pred[16,64,64]{1,2,0:T(8,128)(4,1)} %broadcast_compare_fusion) | copy-start | bytes 196612
  129.5 1.5 %copy-start.15 = (f32[2,64,64]{1,2,0:T(8,128)S(1)}, f32[2,64,64]{1,2,0:T(8,128)}, u32[]{:S(2)}) copy-start(f32[2,64,64]{1,2,0:T(8,128)} %copy.96) | copy-start | bytes 98308
  132.1 0.7 copy-start.17
where the time goes:
time: 143 us; the launch traced here: 142 us
  Pallas kernels  53.9 us (38%)
  local copies, waits for them, and re-layouts  35.2 us (25%)
  starting transfers between devices  28.1 us (20%)
  matrix products  12.9 us (9%)
  other arithmetic  11.5 us (8%)
    pallas_call x2, Pallas kernels, swin_block(): pl.pallas_call(functools.partial(block_kernel, variants, heads, scale), o...  41.4 us
    ppermute x4, starting transfers between devices, extended(): lax.ppermute(tail, axis, [(i, (i + 1) % count) for i in range(ends)])  14.4 us
    ppermute x4, starting transfers between devices, extended(): lax.ppermute(head, axis, [((i + 1) % count, i) for i in range(ends)])  13.7 us
    pallas_call x1, Pallas kernels, var_sum(): pl.pallas_call(functools.partial(var_sum_kernel, count), out_shape=jax.Sh...  12.4 us
    another operation x4, local copies, waits for them, and re-layouts, swin_block(): bias = jnp.tile(bias_grid, (1, 1, 1, GROUP))  4.92 us
    dot_general x3, matrix products, bias_table(): jnp.einsum('vqkt,ht->vhqk', one_hot, parts, preferred_element_type=jnp.fl...  4.62 us
    dot_general x9, matrix products, reconstruct(): jnp.einsum('vrcd,vde->vrce', window, kernels[:, kernel_spot], preferred_e...  3.83 us
  transfers between devices with their start and end apart: 8, of which 0 were waited for; matrix products, arithmetic and copies ran while one was open for 12% of the time, Pallas kernels for 0%

commit v1 on v0

--- a/solution.py
+++ b/solution.py
@@ -363,11 +363,13 @@
     variant_codes = lax.axis_index("var") * VAR_DEV + jnp.arange(VAR_DEV, dtype=jnp.int32)
     first_bias = bias_table(swin_bias[0], variant_codes)
     second_bias = bias_table(swin_bias[1], variant_codes)
-    region = extended(labels, (("ty", 0), ("tx", 1)), SHIFT)
     block_one = block_on_grid(
         features[None], labels, qkv_weight[0], proj_weight[0], up_weight[0], down_weight[0], first_bias
     )
-    shifted = extended(block_one, (("ty", 1), ("tx", 2)), SHIFT)
+    tagged = jnp.broadcast_to(labels.astype(jnp.bfloat16)[None, :, :, None], block_one.shape[:3] + (1,))
+    carried = extended(jnp.concatenate([block_one, tagged], axis=-1), (("ty", 1), ("tx", 2)), SHIFT)
+    shifted = carried[..., :channels]
+    region = carried[0, :, :, channels].astype(jnp.int32)
     block_two = block_on_grid(
         shifted, region, qkv_weight[1], proj_weight[1], up_weight[1], down_weight[1], second_bias
     )

time: 143 us -> 140 us (0.979)
  starting transfers between devices: 28.1 us -> 14.2 us
  waiting for transfers between devices: 0.02 us -> 5.27 us
  other arithmetic: 11.5 us -> 14.2 us
  matrix products: 12.9 us -> 14.6 us
    ppermute x4 -> x2, starting transfers between devices: 13.7 us -> 6.29 us  [extended(): lax.ppermute(head, axis, [((i + 1) % count, i) for i in range(ends)])]
    ppermute x4 -> x2, starting transfers between devices: 14.4 us -> 7.96 us  [extended(): lax.ppermute(tail, axis, [(i, (i + 1) % count) for i in range(ends)])]
    ppermute x4 -> x2, waiting for transfers between devices: 0.01 us -> 5.03 us  [extended(): lax.ppermute(head, axis, [((i + 1) % count, i) for i in range(ends)])]
    unnamed x56 -> x58, local copies, waits for them, and re-layouts: 2.54 us -> 3.57 us
  transfers between devices with their start and end apart: 8 -> 4, of which waited for: 0 -> 2; matrix products, arithmetic and copies ran while one was open for 12% -> 12% of each run, Pallas kernels for 0% -> 0%
where the time goes in v1:
time: 140 us; the launch traced here: 139 us
  Pallas kernels  53.8 us (38%)
  local copies, waits for them, and re-layouts  36.2 us (26%)
  matrix products  14.6 us (10%)
  other arithmetic  14.2 us (10%)
  starting transfers between devices  14.2 us (10%)
  waiting for transfers between devices  5.27 us (4%)
    pallas_call x2, Pallas kernels, swin_block(): pl.pallas_call(functools.partial(block_kernel, variants, heads, scale), o...  41.3 us
    pallas_call x1, Pallas kernels, var_sum(): pl.pallas_call(functools.partial(var_sum_kernel, count), out_shape=jax.Sh...  12.5 us
    ppermute x2, starting transfers between devices, extended(): lax.ppermute(tail, axis, [(i, (i + 1) % count) for i in range(ends)])  7.96 us
    ppermute x2, starting transfers between devices, extended(): lax.ppermute(head, axis, [((i + 1) % count, i) for i in range(ends)])  6.29 us
    dot_general x3, matrix products, bias_table(): jnp.einsum('vqkt,ht->vhqk', one_hot, parts, preferred_element_type=jnp.fl...  5.37 us
    ppermute x2, waiting for transfers between devices, extended(): lax.ppermute(head, axis, [((i + 1) % count, i) for i in range(ends)])  5.03 us
    another operation x4, local copies, waits for them, and re-layouts, swin_block(): bias = jnp.tile(bias_grid, (1, 1, 1, GROUP))  4.9 us
    dot_general x9, matrix products, reconstruct(): jnp.einsum('vrcd,vde->vrce', window, kernels[:, kernel_spot], preferred_e...  3.85 us
  transfers between devices with their start and end apart: 4, of which 2 were waited for; matrix products, arithmetic and copies ran while one was open for 12% of the time, Pallas kernels for 0%

profile of v1, /device:TPU:99, one launch (start us, length us, event | category | flops | bytes accessed | tf_op | source)
XLA Modules:
  0.0 139.0 jit_solution(8429610510737646085)
XLA Ops:
  0.1 0.8 reshape_broadcast_in_dim.9
  1.2 0.7 convert_element_type.65
  1.9 0.8 fusion.88
  2.7 0.7 add_add_fusion
  3.4 0.6 reduce-precision_convert_fusion.1
  4.1 0.6 copy-done.12
  4.7 1.8 %fusion.8 = f32[2,18,64,64]{3,1,2,0:T(8,128)S(1)} fusion(s32[2,64,64]{2,1,0:T(8,128)S(1)} %fusion.35, bf16[6,225]{1,0:T(8,128)(2,1)S(1)} %get-tuple-element.38, bf16[6,225]{1,0:T(8,128)(2,1)S(1)} %get-tuple-element.37, bf16[6,225]{1,0:T(8,128)(2,1)S(1)} %get-tuple-element.39), kind=kOutput, calls=%fused_computation.11 | convolution fusion | flops 68222704 | bytes 630692 | tf_op jit(solution)/shard_map/vqkt,ht->vhqk/dot_general | solution.py:251
  7.1 0.9 tile.9.bias_ref
  8.0 2.4 %fusion.86 = (bf16[1,180,360]{2,0,1:T(2,128)(2,1)}, bf16[1,180,360]{2,0,1:T(2,128)(2,1)}) fusion(bf16[2,180,360]{2,0,1:T(2,128)(2,1)} %param.15), kind=kLoop, calls=%fused_computation.208 | loop fusion | bytes 518400 | tf_op jit(solution)/shard_map/slice | solution.py:374
  10.4 2.0 %fusion.87 = (bf16[1,180,180]{2,0,1:T(2,128)(2,1)S(1)}, bf16[1,180,180]{2,0,1:T(2,128)(2,1)}) fusion(bf16[2,180,180]{2,0,1:T(2,128)(2,1)} %param.14), kind=kLoop, calls=%fused_computation.209 | loop fusion | bytes 259200 | tf_op jit(solution)/shard_map/slice | solution.py:374
  12.4 0.6 fusion.84
  13.0 0.8 copy.69
  13.9 1.6 %copy_bitcast_fusion.2 = (bf16[180,180]{1,0:T(8,128)(2,1)}, bf16[180,180]{1,0:T(8,128)(2,1)S(1)}) fusion(bf16[1,180,180]{2,0,1:T(2,128)(2,1)S(1)} %get-tuple-element.15, bf16[1,180,180]{2,0,1:T(2,128)(2,1)} %get-tuple-element.16), kind=kLoop, calls=%fused_computation.74 | loop fusion | bytes 259200 | tf_op jit(solution)/shard_map/squeeze | solution.py:374
  15.7 2.2 %fusion.85 = (bf16[1,360,180]{1,0,2:T(2,128)(2,1)}, bf16[1,360,180]{1,0,2:T(2,128)(2,1)S(1)}) fusion(bf16[2,360,180]{1,0,2:T(2,128)(2,1)} %param.16), kind=kLoop, calls=%fused_computation.207 | loop fusion | bytes 518400 | tf_op jit(solution)/shard_map/slice | solution.py:374
  18.2 1.1 copy.65
  19.3 13.7 %shard_map.109 = bf16[2,4,256,180]{3,2,1,0:T(8,128)(2,1)S(1)} custom-call(bf16[1,4,256,180]{3,2,1,0:T(8,128)(2,1)S(1)} %bitcast.223, s32[4,256,1]{2,1,0:T(8,128)S(1)} %reshape.838.labq_ref, s32[4,1,256]{2,1,0:T(1,128)S(1)} %reshape.801.labk_ref, f32[2,6,64,256]{3,2,1,0:T(8,128)S(1)} %tile.9.bias_ref, bf16[180,768]{1,0:T(8,128)(2,1)S(1)} %copy.117.wqkv_ref, ...), custom_call_target="tpu_custom_call" | custom-call | tf_op jit(solution)/shard_map/pallas_call | solution.py:181
  33.4 0.9 pad_maximum_fusion.6
  34.3 3.2 %collective-permute-start = (bf16[2,4,32,181]{3,2,1,0:T(8,128)(2,1)}, bf16[2,4,32,181]{3,2,1,0:T(8,128)(2,1)}, u32[]{:S(2)}, u32[]{:S(2)}) collective-permute-start(bf16[2,4,32,181]{3,2,1,0:T(8,128)(2,1)} %get-tuple-element.7), channel_id=1, source_target_pairs={{0,8},{8,16},{16,24},{24,32},{32,40},{40,48},{48,56},{1,9},{9,17},... | collective-permute-start | bytes 278024 | tf_op jit(solution)/shard_map/ppermute | solution.py:30
  37.5 4.4 %collective-permute-start.1 = (bf16[2,4,32,181]{3,2,1,0:T(8,128)(2,1)}, bf16[2,4,32,181]{3,2,1,0:T(8,128)(2,1)}, u32[]{:S(2)}, u32[]{:S(2)}) collective-permute-start(bf16[2,4,32,181]{3,2,1,0:T(8,128)(2,1)} %get-tuple-element.8), channel_id=1, source_target_pairs={{8,0},{16,8},{24,16},{32,24},{40,32},{48,40},{56,48},{9,1},{17,9},... | collective-permute-start | bytes 278024 | tf_op jit(solution)/shard_map/ppermute | solution.py:32
  41.8 0.6 fusion.70
  42.4 0.6 fusion.77
  43.0 0.5 fusion.67
  43.6 0.5 broadcast_subtract_fusion.3
  44.2 1.8 %fusion.9 = f32[2,18,64,64]{3,1,2,0:T(8,128)S(1)} fusion(s32[2,64,64]{2,1,0:T(8,128)S(1)} %copy-done.13, bf16[6,225]{1,0:T(8,128)(2,1)S(1)} %copy-done.23, bf16[6,225]{1,0:T(8,128)(2,1)S(1)} %copy-done.24, bf16[6,225]{1,0:T(8,128)(2,1)S(1)} %copy-done.22), kind=kOutput, calls=%fused_computation.12 | convolution fusion | flops 68222704 | bytes 630692 | tf_op jit(solution)/shard_map/vqkt,ht->vhqk/dot_general | solution.py:251
  46.2 1.5 %tile.20 = f32[2,6,64,4,64]{4,3,2,1,0:T(4,128)} broadcast(f32[2,6,64,64]{3,2,1,0:T(8,128)S(1)} %copy.79), dimensions={0,1,2,4} | broadcast | bytes 983040 | tf_op jit(solution)/shard_map/tile | solution.py:177
  47.7 2.3 %tile.21.bias_ref = f32[2,6,64,256]{3,2,1,0:T(8,128)S(1)} reshape(f32[2,6,64,4,64]{4,3,2,1,0:T(4,128)} %tile.20) | data formatting | bytes 1572864 | tf_op jit(solution)/shard_map/tile | solution.py:177
  50.0 0.8 copy.80
  51.1 1.1 copy.127
  52.3 1.8 %fusion.14 = f32[1,6,64,64]{3,1,2,0:T(8,128)S(1)} fusion(s32[64,64]{1,0:T(8,128)} %get-tuple-element.28, bf16[2,225]{1,0:T(2,128)(2,1)S(1)} %get-tuple-element.26, bf16[2,225]{1,0:T(2,128)(2,1)S(1)} %get-tuple-element.27, bf16[2,225]{1,0:T(2,128)(2,1)S(1)} %get-tuple-element.25), kind=kOutput, calls=%fused_computation.32 | convolution fusion | flops 11988900 | bytes 117388 | tf_op jit(solution)/shard_map/vqkt,ht->vhqk/dot_general | solution.py:251
  54.1 0.7 copy.95
  54.8 0.8 broadcast_compare_fusion
  55.7 0.8 fusion.63
  56.4 1.3 convolution_convert_fusion
  57.9 1.1 convolution_convert_fusion.2
  59.0 1.1 pad_maximum_fusion.4
  60.1 4.8 %collective-permute-start.2 = (bf16[2,40,4,181]{3,2,1,0:T(4,128)(2,1)S(1)}, bf16[2,40,4,181]{3,2,1,0:T(4,128)(2,1)S(1)}, u32[]{:S(2)}, u32[]{:S(2)}) collective-permute-start(bf16[2,40,4,181]{3,2,1,0:T(4,128)(2,1)S(1)} %get-tuple-element.5), channel_id=1, source_target_pairs={{0,1},{1,2},{2,3},{3,4},{4,5},{5,6},{6,7},{8,9},{9,10},{10,11},{11... | collective-permute-start | bytes 347528 | tf_op jit(solution)/shard_map/ppermute | solution.py:30
  64.9 1.9 %collective-permute-start.3 = (bf16[2,40,4,181]{3,2,1,0:T(4,128)(2,1)S(1)}, bf16[2,40,4,181]{3,2,1,0:T(4,128)(2,1)S(1)}, u32[]{:S(2)}, u32[]{:S(2)}) collective-permute-start(bf16[2,40,4,181]{3,2,1,0:T(4,128)(2,1)S(1)} %get-tuple-element.6), channel_id=1, source_target_pairs={{1,0},{2,1},{3,2},{4,3},{5,4},{6,5},{7,6},{9,8},{10,9},{11,10},{12... | collective-permute-start | bytes 347528 | tf_op jit(solution)/shard_map/ppermute | solution.py:32
  67.1 5.0 %collective-permute-done.3 = bf16[2,40,4,181]{3,2,1,0:T(4,128)(2,1)S(1)} collective-permute-done((bf16[2,40,4,181]{3,2,1,0:T(4,128)(2,1)S(1)}, bf16[2,40,4,181]{3,2,1,0:T(4,128)(2,1)S(1)}, u32[]{:S(2)}, u32[]{:S(2)}) %collective-permute-start.3) | collective-permute-done | bytes 115872 | tf_op jit(solution)/shard_map/ppermute | solution.py:32
  72.2 0.7 copy-done.9
  72.8 1.3 maximum_reduce_fusion
  74.4 0.9 reshape.839.labq_ref
  75.3 2.4 %pad_maximum_fusion = bf16[2,40,40,181]{3,2,1,0:T(8,128)(2,1)S(1)} fusion(bf16[2,40,4,181]{3,2,1,0:T(4,128)(2,1)} %copy-done.9, bf16[2,4,32,181]{3,2,1,0:T(8,128)(2,1)} %collective-permute-done.1, bf16[2,32,32,1]{3,2,1,0:T(8,128)(2,1)} %copy-done.1, bf16[2,32,32,180]{3,2,1,0:T(8,128)(2,1)S(1)} %bitcast.229, bf16[2,4,32,181]{3,2,1,0:T(8,128)(2,1)} %collective-permute-done, ...), kind=kLoop, calls=%fused_computation.9 | loop fusion | flops 6950400 | bytes 2316800 | tf_op jit(solution)/shard_map/concatenate | solution.py:28
  78.0 0.4 pad.27
  78.4 27.6 %shard_map.110 = bf16[2,7,256,180]{3,2,1,0:T(8,128)(2,1)S(1)} custom-call(bf16[2,7,256,180]{3,2,1,0:T(8,128)(2,1)S(1)} %bitcast.220, s32[7,256,1]{2,1,0:T(8,128)S(1)} %reshape.839.labq_ref, s32[7,1,256]{2,1,0:T(1,128)S(1)} %reshape.808.labk_ref, f32[2,6,64,256]{3,2,1,0:T(8,128)S(1)} %tile.21.bias_ref, bf16[180,768]{1,0:T(8,128)(2,1)S(1)} %copy.118.wqkv_ref, ...), custom_call_target="tpu_custom_call" | custom-call | tf_op jit(solution)/shard_map/pallas_call | solution.py:181
  106.3 0.4 slice_select_fusion
  106.7 0.6 copy-done.3
  107.7 0.4 convolution_add_fusion.7
  108.1 0.4 convolution_add_fusion.6
  109.0 0.4 convolution_add_fusion.4
  109.4 0.4 convolution_add_fusion.3
  109.8 0.4 convolution_add_fusion.2
  110.3 0.4 convolution_add_fusion.1
  110.7 0.5 fusion.13
  111.2 1.0 convert_element_type.70.part_ref
  112.1 12.5 %shard_map.111 = f32[32,1536]{1,0:T(8,128)} custom-call(bf16[32,1536]{1,0:T(8,128)(2,1)} %convert_element_type.70.part_ref), custom_call_target="tpu_custom_call" | custom-call | tf_op jit(solution)/shard_map/pallas_call | solution.py:82
  124.6 0.9 broadcast_multiply_fusion
  126.7 0.5 convolution_convert_fusion.1
  127.9 0.7 fusion.89
  128.8 0.4 convolution_convert_fusion.3
  129.5 1.0 convolution_add_fusion.8
  130.5 1.9 %reshape.818 = f32[4,4,8,8,12,4]{3,2,5,4,1,0:T(8,128)S(1)} reshape(f32[16,64,48]{1,2,0:T(8,128)} %convolution_add_fusion.8) | data formatting | bytes 393216 | tf_op jit(solution)/shard_map/reshape | solution.py:394
  132.4 2.9 %copy.99 = f32[12,4,8,4,8,4]{2,1,5,4,3,0:T(4,128)} copy(f32[12,4,8,4,8,4]{4,2,5,0,3,1:T(8,128)S(1)} %bitcast.230) | data formatting | bytes 393216 | tf_op jit(solution)/shard_map/transpose | solution.py:396
  135.3 2.8 %reshape.819 = f32[3,4,32,128]{2,3,1,0:T(8,128)S(1)} reshape(f32[12,4,8,4,8,4]{2,1,5,4,3,0:T(4,128)} %copy.99) | data formatting | bytes 393216 | tf_op jit(solution)/shard_map/reshape | solution.py:397
  138.1 0.9 copy.100
  (108 shorter events, 6.7 us)
Async XLA Ops:
  0.0 126.7 %copy-start = (bf16[48,144]{1,0:T(8,128)(2,1)S(1)}, bf16[48,144]{1,0:T(8,128)(2,1)}, u32[]{:S(2)}) copy-start(bf16[48,144]{1,0:T(8,128)(2,1)} %param.19) | copy-start | bytes 41476
  0.0 6.5 %copy-start.16 = (pred[2]{0:T(512)(128)(4,1)}, pred[2]{0:T(512)(128)(4,1)S(1)}, u32[]{:S(2)}) copy-start(pred[2]{0:T(512)(128)(4,1)S(1)} %get-tuple-element.35) | copy-start | bytes 10
  0.0 6.5 %copy-start.18 = (pred[2]{0:T(512)(128)(4,1)}, pred[2]{0:T(512)(128)(4,1)S(1)}, u32[]{:S(2)}) copy-start(pred[2]{0:T(512)(128)(4,1)S(1)} %get-tuple-element.36) | copy-start | bytes 10
  0.1 6.5 %copy-start.20 = (pred[2]{0:T(512)(128)(4,1)}, pred[2]{0:T(512)(128)(4,1)S(1)}, u32[]{:S(2)}) copy-start(pred[2]{0:T(512)(128)(4,1)S(1)} %fusion.76) | copy-start | bytes 10
  0.9 5.7 %copy-start.6 = (s32[1,4,8,4,8,1]{4,2,3,1,5,0:T(8,128)}, s32[1,4,8,4,8,1]{4,2,3,1,5,0:T(8,128)S(1)}, u32[]{:S(2)}) copy-start(s32[1,4,8,4,8,1]{4,2,3,1,5,0:T(8,128)S(1)} %copy.162) | copy-start | bytes 12292
  4.1 0.6 copy-start.12
  7.1 5.3 %copy-start.2 = (bf16[2,180,540]{2,0,1:T(2,128)(2,1)S(1)}, bf16[2,180,540]{2,0,1:T(2,128)(2,1)}, u32[]{:S(2)}) copy-start(bf16[2,180,540]{2,0,1:T(2,128)(2,1)} %param.13) | copy-start | bytes 1166404
  15.5 3.7 %copy-start.4 = (bf16[1,180,360]{2,0,1:T(2,128)(2,1)S(1)}, bf16[1,180,360]{2,0,1:T(2,128)(2,1)}, u32[]{:S(2)}) copy-start(bf16[1,180,360]{2,0,1:T(2,128)(2,1)} %get-tuple-element.13) | copy-start | bytes 388804
  15.5 3.7 %copy-start.5 = (bf16[1,180,360]{2,0,1:T(2,128)(2,1)S(1)}, bf16[1,180,360]{2,0,1:T(2,128)(2,1)}, u32[]{:S(2)}) copy-start(bf16[1,180,360]{2,0,1:T(2,128)(2,1)} %get-tuple-element.14) | copy-start | bytes 388804
  33.1 10.9 %copy-start.7 = (s32[1,4,8,4,8,1]{4,2,3,1,5,0:T(8,128)S(1)}, s32[1,4,8,4,8,1]{4,2,3,1,5,0:T(8,128)}, u32[]{:S(2)}) copy-start(s32[1,4,8,4,8,1]{4,2,3,1,5,0:T(8,128)} %copy-done.6) | copy-start | bytes 12292
  33.1 11.0 %copy-start.13 = (s32[2,64,64]{2,1,0:T(8,128)S(1)}, s32[2,64,64]{2,1,0:T(8,128)}, u32[]{:S(2)}) copy-start(s32[2,64,64]{2,1,0:T(8,128)} %copy-done.12) | copy-start | bytes 98308
  33.2 11.0 %copy-start.22 = (bf16[6,225]{1,0:T(8,128)(2,1)S(1)}, bf16[6,225]{1,0:T(8,128)(2,1)}, u32[]{:S(2)}) copy-start(bf16[6,225]{1,0:T(8,128)(2,1)} %get-tuple-element.19) | copy-start | bytes 8104
  33.2 11.0 %copy-start.23 = (bf16[6,225]{1,0:T(8,128)(2,1)S(1)}, bf16[6,225]{1,0:T(8,128)(2,1)}, u32[]{:S(2)}) copy-start(bf16[6,225]{1,0:T(8,128)(2,1)} %get-tuple-element.20) | copy-start | bytes 8104
  33.2 11.0 %copy-start.24 = (bf16[6,225]{1,0:T(8,128)(2,1)S(1)}, bf16[6,225]{1,0:T(8,128)(2,1)}, u32[]{:S(2)}) copy-start(bf16[6,225]{1,0:T(8,128)(2,1)} %get-tuple-element.21) | copy-start | bytes 8104
  33.4 38.8 %copy-start.1 = (bf16[2,32,32,1]{3,2,1,0:T(8,128)(2,1)}, bf16[2,32,32,1]{3,2,1,0:T(8,128)(2,1)S(1)}, u32[]{:S(2)}) copy-start(bf16[2,32,32,1]{3,2,1,0:T(8,128)(2,1)S(1)} %broadcast_in_dim.264) | copy-start | bytes 12292
  34.3 24.7 %collective-permute-start = (bf16[2,4,32,181]{3,2,1,0:T(8,128)(2,1)}, bf16[2,4,32,181]{3,2,1,0:T(8,128)(2,1)}, u32[]{:S(2)}, u32[]{:S(2)}) collective-permute-start(bf16[2,4,32,181]{3,2,1,0:T(8,128)(2,1)} %get-tuple-element.7), channel_id=1, source_target_pairs={{0,8},{8,16},{16,24},{24,32},{32,40},{40,48},{48,56},{1,9},{9,17},... | collective-permute-start | bytes 278024 | tf_op jit(solution)/shard_map/ppermute | solution.py:30
  37.5 21.5 %collective-permute-start.1 = (bf16[2,4,32,181]{3,2,1,0:T(8,128)(2,1)}, bf16[2,4,32,181]{3,2,1,0:T(8,128)(2,1)}, u32[]{:S(2)}, u32[]{:S(2)}) collective-permute-start(bf16[2,4,32,181]{3,2,1,0:T(8,128)(2,1)} %get-tuple-element.8), channel_id=1, source_target_pairs={{8,0},{16,8},{24,16},{32,24},{40,32},{48,40},{56,48},{9,1},{17,9},... | collective-permute-start | bytes 278024 | tf_op jit(solution)/shard_map/ppermute | solution.py:32
  47.7 2.3 %copy-start.10 = (bf16[180,180]{1,0:T(8,128)(2,1)S(1)}, bf16[180,180]{1,0:T(8,128)(2,1)}, u32[]{:S(2)}) copy-start(bf16[180,180]{1,0:T(8,128)(2,1)} %get-tuple-element.40) | copy-start | bytes 194404
  50.0 2.3 %copy-start.25 = (f32[2,225]{1,0:T(2,128)S(1)}, f32[2,225]{1,0:T(2,128)}, u32[]{:S(2)}) copy-start(f32[2,225]{1,0:T(2,128)} %param.21) | copy-start | bytes 5404
  50.9 4.8 %copy-start.17 = (pred[2]{0:T(512)(128)(4,1)S(1)}, pred[2]{0:T(512)(128)(4,1)}, u32[]{:S(2)}) copy-start(pred[2]{0:T(512)(128)(4,1)} %copy-done.16) | copy-start | bytes 10
  50.9 4.8 %copy-start.19 = (pred[2]{0:T(512)(128)(4,1)S(1)}, pred[2]{0:T(512)(128)(4,1)}, u32[]{:S(2)}) copy-start(pred[2]{0:T(512)(128)(4,1)} %copy-done.18) | copy-start | bytes 10
  50.9 4.8 %copy-start.21 = (pred[2]{0:T(512)(128)(4,1)S(1)}, pred[2]{0:T(512)(128)(4,1)}, u32[]{:S(2)}) copy-start(pred[2]{0:T(512)(128)(4,1)} %copy-done.20) | copy-start | bytes 10
  51.1 6.7 %copy-start.26 = (s32[48]{0:T(128)S(1)}, s32[48]{0:T(128)}, u32[]{:S(2)}) copy-start(s32[48]{0:T(128)} %get-tuple-element.53) | copy-start | bytes 580
  51.1 6.7 %copy-start.27 = (s32[48]{0:T(128)S(1)}, s32[48]{0:T(128)}, u32[]{:S(2)}) copy-start(s32[48]{0:T(128)} %broadcast_subtract_fusion.3) | copy-start | bytes 580
  60.1 7.0 %collective-permute-start.2 = (bf16[2,40,4,181]{3,2,1,0:T(4,128)(2,1)S(1)}, bf16[2,40,4,181]{3,2,1,0:T(4,128)(2,1)S(1)}, u32[]{:S(2)}, u32[]{:S(2)}) collective-permute-start(bf16[2,40,4,181]{3,2,1,0:T(4,128)(2,1)S(1)} %get-tuple-element.5), channel_id=1, source_target_pairs={{0,1},{1,2},{2,3},{3,4},{4,5},{5,6},{6,7},{8,9},{9,10},{10,11},{11... | collective-permute-start | bytes 347528 | tf_op jit(solution)/shard_map/ppermute | solution.py:30
  64.9 7.3 %collective-permute-start.3 = (bf16[2,40,4,181]{3,2,1,0:T(4,128)(2,1)S(1)}, bf16[2,40,4,181]{3,2,1,0:T(4,128)(2,1)S(1)}, u32[]{:S(2)}, u32[]{:S(2)}) collective-permute-start(bf16[2,40,4,181]{3,2,1,0:T(4,128)(2,1)S(1)} %get-tuple-element.6), channel_id=1, source_target_pairs={{1,0},{2,1},{3,2},{4,3},{5,4},{6,5},{7,6},{9,8},{10,9},{11,10},{12... | collective-permute-start | bytes 347528 | tf_op jit(solution)/shard_map/ppermute | solution.py:32
  67.1 5.0 %copy-start.8 = (bf16[2,40,4,181]{3,2,1,0:T(4,128)(2,1)}, bf16[2,40,4,181]{3,2,1,0:T(4,128)(2,1)S(1)}, u32[]{:S(2)}) copy-start(bf16[2,40,4,181]{3,2,1,0:T(4,128)(2,1)S(1)} %collective-permute-done.2) | copy-start | bytes 347524
  72.2 0.7 copy-start.9
  106.3 1.0 copy-start.3
  126.1 1.5 %copy-start.11 = (pred[16,64,64]{1,2,0:T(8,128)(4,1)S(1)}, pred[16,64,64]{1,2,0:T(8,128)(4,1)}, u32[]{:S(2)}) copy-start(pred[16,64,64]{1,2,0:T(8,128)(4,1)} %broadcast_compare_fusion) | copy-start | bytes 196612
  126.1 1.5 %copy-start.14 = (f32[2,64,64]{1,2,0:T(8,128)S(1)}, f32[2,64,64]{1,2,0:T(8,128)}, u32[]{:S(2)}) copy-start(f32[2,64,64]{1,2,0:T(8,128)} %copy.95) | copy-start | bytes 98308
  128.8 0.7 copy-start.15

commit v2 on v1

--- a/solution.py
+++ b/solution.py
@@ -163,7 +163,7 @@
     return columns.reshape(channels, 3 * span), rows
 
 
-def swin_block(windows, region, w_qkv, w_proj, w_up, w_down, bias_grid):
+def swin_block(windows, region, layer, w_qkv, w_proj, w_up, w_down, bias_grid):
     inputs, count, cells, channels = windows.shape
     variants, heads = bias_grid.shape[:2]
     groups = -(-count // GROUP)
@@ -175,7 +175,6 @@
     labq = region.reshape(groups, tokens, 1)
     labk = region.reshape(groups, 1, tokens)
     bias = jnp.tile(bias_grid, (1, 1, 1, GROUP))
-    wqkv, wp = padded_weights(w_qkv, w_proj, heads)
     scale = (channels // heads) ** (-0.5)
     whole = lambda shape: pl.BlockSpec(shape, lambda g: (0,) * len(shape))
     out = pl.pallas_call(
@@ -187,23 +186,23 @@
             pl.BlockSpec((1, tokens, 1), lambda g: (g, 0, 0)),
             pl.BlockSpec((1, 1, tokens), lambda g: (g, 0, 0)),
             whole(bias.shape),
-            whole(wqkv.shape),
-            whole(wp.shape),
-            whole(w_up.shape),
-            whole(w_down.shape),
+            pl.BlockSpec((None,) + w_qkv.shape[1:], lambda g: (layer, 0, 0)),
+            pl.BlockSpec((None,) + w_proj.shape[1:], lambda g: (layer, 0, 0)),
+            pl.BlockSpec((None,) + w_up.shape[1:], lambda g: (layer, 0, 0)),
+            pl.BlockSpec((None,) + w_down.shape[1:], lambda g: (layer, 0, 0)),
         ],
         out_specs=pl.BlockSpec((variants, 1, tokens, channels), lambda g: (0, g, 0, 0)),
         compiler_params=pltpu.CompilerParams(vmem_limit_bytes=48 * 1024 * 1024),
-    )(x, labq, labk, bias, wqkv, wp, w_up, w_down)
+    )(x, labq, labk, bias, w_qkv, w_proj, w_up, w_down)
     out = out.reshape(variants, groups * GROUP, cells, channels)
     return out[:, :count]
 
 
-def block_on_grid(tokens, region, w_qkv, w_proj, w_up, w_down, bias_grid):
+def block_on_grid(tokens, region, layer, w_qkv, w_proj, w_up, w_down, bias_grid):
     height, breadth = tokens.shape[1], tokens.shape[2]
     windows = to_windows(tokens)
     region_windows = to_windows(region[None, :, :, None])[0, :, :, 0]
-    out = swin_block(windows, region_windows, w_qkv, w_proj, w_up, w_down, bias_grid)
+    out = swin_block(windows, region_windows, layer, w_qkv, w_proj, w_up, w_down, bias_grid)
     return from_windows(out, height, breadth)
 
 
@@ -364,14 +363,14 @@
     first_bias = bias_table(swin_bias[0], variant_codes)
     second_bias = bias_table(swin_bias[1], variant_codes)
     block_one = block_on_grid(
-        features[None], labels, qkv_weight[0], proj_weight[0], up_weight[0], down_weight[0], first_bias
+        features[None], labels, 0, qkv_weight, proj_weight, up_weight, down_weight, first_bias
     )
     tagged = jnp.broadcast_to(labels.astype(jnp.bfloat16)[None, :, :, None], block_one.shape[:3] + (1,))
     carried = extended(jnp.concatenate([block_one, tagged], axis=-1), (("ty", 1), ("tx", 2)), SHIFT)
     shifted = carried[..., :channels]
     region = carried[0, :, :, channels].astype(jnp.int32)
     block_two = block_on_grid(
-        shifted, region, qkv_weight[1], proj_weight[1], up_weight[1], down_weight[1], second_bias
+        shifted, region, 1, qkv_weight, proj_weight, up_weight, down_weight, second_bias
     )
     padded = block_two[:, SHIFT - 1 : SHIFT + height + 1, SHIFT - 1 : SHIFT + breadth + 1]
     row = lax.axis_index("ty") * height - 1 + jnp.arange(height + 2)

time: 140 us -> 130 us (0.929)
  local copies, waits for them, and re-layouts: 36.2 us -> 28.2 us
  other arithmetic: 14.2 us -> 12.1 us
    slice x6 -> x0, local copies, waits for them, and re-layouts: 8.8 us -> none  [the longest x1 2.41 us: local(): up_weight[1]]
    another operation x4, local copies, waits for them, and re-layouts: 4.9 us -> 7.48 us  [swin_block(): bias = jnp.tile(bias_grid, (1, 1, 1, GROUP))]
    squeeze x2 -> x0, local copies, waits for them, and re-layouts: 1.64 us -> none  [the longest x1 1.59 us: local(): proj_weight[1]]
    unnamed x58 -> x46, local copies, waits for them, and re-layouts: 3.57 us -> 3.8 us
  transfers between devices with their start and end apart: 4 -> 4, of which waited for: 2 -> 2; matrix products, arithmetic and copies ran while one was open for 12% -> 11% of each run, Pallas kernels for 0% -> 0%
where the time goes in v2:
time: 130 us; the launch traced here: 129 us
  Pallas kernels  54.8 us (42%)
  local copies, waits for them, and re-layouts  28.2 us (22%)
  starting transfers between devices  14.2 us (11%)
  matrix products  13.8 us (11%)
  other arithmetic  12.1 us (9%)
  waiting for transfers between devices  5.27 us (4%)
    pallas_call x2, Pallas kernels, swin_block(): pl.pallas_call(functools.partial(block_kernel, variants, heads, scale), o...  42.3 us
    pallas_call x1, Pallas kernels, var_sum(): pl.pallas_call(functools.partial(var_sum_kernel, count), out_shape=jax.Sh...  12.5 us
    ppermute x2, starting transfers between devices, extended(): lax.ppermute(tail, axis, [(i, (i + 1) % count) for i in range(ends)])  7.94 us
    another operation x4, local copies, waits for them, and re-layouts, swin_block(): bias = jnp.tile(bias_grid, (1, 1, 1, GROUP))  7.48 us
    ppermute x2, starting transfers between devices, extended(): lax.ppermute(head, axis, [((i + 1) % count, i) for i in range(ends)])  6.3 us
    ppermute x2, waiting for transfers between devices, extended(): lax.ppermute(head, axis, [((i + 1) % count, i) for i in range(ends)])  5.03 us
    dot_general x3, matrix products, bias_table(): jnp.einsum('vqkt,ht->vhqk', one_hot, parts, preferred_element_type=jnp.fl...  4.62 us
    dot_general x9, matrix products, reconstruct(): jnp.einsum('vrcd,vde->vrce', window, kernels[:, kernel_spot], preferred_e...  3.85 us
  transfers between devices with their start and end apart: 4, of which 2 were waited for; matrix products, arithmetic and copies ran while one was open for 11% of the time, Pallas kernels for 0%

profile of v2, /device:TPU:99, one launch (start us, length us, event | category | flops | bytes accessed | tf_op | source)
XLA Modules:
  0.0 129.0 jit_solution(14258967101349483566)
XLA Ops:
  0.0 0.8 reshape_broadcast_in_dim.9
  1.2 0.7 convert_element_type.59
  1.9 0.8 fusion.84
  2.7 0.7 add_add_fusion
  3.5 1.8 %fusion.8 = f32[2,18,64,64]{3,1,2,0:T(8,128)S(1)} fusion(s32[2,64,64]{2,1,0:T(8,128)S(1)} %fusion.35, bf16[6,225]{1,0:T(8,128)(2,1)S(1)} %get-tuple-element.30, bf16[6,225]{1,0:T(8,128)(2,1)S(1)} %get-tuple-element.29, bf16[6,225]{1,0:T(8,128)(2,1)S(1)} %get-tuple-element.31), kind=kOutput, calls=%fused_computation.11 | convolution fusion | flops 68222704 | bytes 630692 | tf_op jit(solution)/shard_map/vqkt,ht->vhqk/dot_general | solution.py:250
  5.5 1.4 %tile.8 = f32[2,6,64,4,64]{4,3,2,1,0:T(4,128)} broadcast(f32[2,6,64,64]{3,2,1,0:T(8,128)S(1)} %copy.68), dimensions={0,1,2,4} | broadcast | bytes 983040 | tf_op jit(solution)/shard_map/tile | solution.py:177
  7.0 2.3 %tile.9.bias_ref = f32[2,6,64,256]{3,2,1,0:T(8,128)S(1)} reshape(f32[2,6,64,4,64]{4,3,2,1,0:T(4,128)} %tile.8) | data formatting | bytes 1572864 | tf_op jit(solution)/shard_map/tile | solution.py:177
  9.4 0.3 copy.73.wdown_ref
  9.7 0.9 copy.71.wp_ref
  10.7 14.0 %shard_map.109 = bf16[2,4,256,180]{3,2,1,0:T(8,128)(2,1)S(1)} custom-call(bf16[1,4,256,180]{3,2,1,0:T(8,128)(2,1)S(1)} %bitcast.206, s32[4,256,1]{2,1,0:T(8,128)S(1)} %reshape.830.labq_ref, s32[4,1,256]{2,1,0:T(1,128)S(1)} %reshape.795.labk_ref, f32[2,6,64,256]{3,2,1,0:T(8,128)S(1)} %tile.9.bias_ref, bf16[2,180,540]{2,1,0:T(8,128)(2,1)S(1)} %copy.70.wqkv_ref, ...), custom_call_target="tpu_custom_call" | custom-call | tf_op jit(solution)/shard_map/pallas_call | solution.py:180
  25.2 0.9 copy-done.2
  26.1 0.8 pad_maximum_fusion.6
  26.9 3.2 %collective-permute-start = (bf16[2,4,32,181]{3,2,1,0:T(8,128)(2,1)}, bf16[2,4,32,181]{3,2,1,0:T(8,128)(2,1)S(1)}, u32[]{:S(2)}, u32[]{:S(2)}) collective-permute-start(bf16[2,4,32,181]{3,2,1,0:T(8,128)(2,1)} %get-tuple-element.7), channel_id=1, source_target_pairs={{0,8},{8,16},{16,24},{24,32},{32,40},{40,48},{48,56},{1,9},{9,17},... | collective-permute-start | bytes 278024 | tf_op jit(solution)/shard_map/ppermute | solution.py:30
  30.1 4.4 %collective-permute-start.1 = (bf16[2,4,32,181]{3,2,1,0:T(8,128)(2,1)}, bf16[2,4,32,181]{3,2,1,0:T(8,128)(2,1)S(1)}, u32[]{:S(2)}, u32[]{:S(2)}) collective-permute-start(bf16[2,4,32,181]{3,2,1,0:T(8,128)(2,1)} %get-tuple-element.8), channel_id=1, source_target_pairs={{8,0},{16,8},{24,16},{32,24},{40,32},{48,40},{56,48},{9,1},{17,9},... | collective-permute-start | bytes 278024 | tf_op jit(solution)/shard_map/ppermute | solution.py:32
  34.5 0.5 fusion.70
  35.0 0.5 fusion.77
  35.5 0.6 fusion.67
  36.1 0.5 broadcast_subtract_fusion.3
  36.7 1.8 %fusion.9 = f32[2,18,64,64]{3,1,2,0:T(8,128)S(1)} fusion(s32[2,64,64]{2,1,0:T(8,128)S(1)} %copy-done.13, bf16[6,225]{1,0:T(8,128)(2,1)S(1)} %get-tuple-element.12, bf16[6,225]{1,0:T(8,128)(2,1)S(1)} %get-tuple-element.13, bf16[6,225]{1,0:T(8,128)(2,1)S(1)} %get-tuple-element.11), kind=kOutput, calls=%fused_computation.12 | convolution fusion | flops 68222704 | bytes 630692 | tf_op jit(solution)/shard_map/vqkt,ht->vhqk/dot_general | solution.py:250
  38.7 1.4 %tile.20 = f32[2,6,64,4,64]{4,3,2,1,0:T(4,128)} broadcast(f32[2,6,64,64]{3,2,1,0:T(8,128)S(1)} %copy.78), dimensions={0,1,2,4} | broadcast | bytes 983040 | tf_op jit(solution)/shard_map/tile | solution.py:177
  40.2 2.3 %tile.21.bias_ref = f32[2,6,64,256]{3,2,1,0:T(8,128)S(1)} reshape(f32[2,6,64,4,64]{4,3,2,1,0:T(4,128)} %tile.20) | data formatting | bytes 1572864 | tf_op jit(solution)/shard_map/tile | solution.py:177
  42.5 1.0 fusion.14
  43.6 0.7 copy.93
  44.3 0.9 broadcast_compare_fusion
  45.2 0.7 fusion.63
  45.9 1.3 %convolution_convert_fusion = bf16[2,9,180,48]{2,1,3,0:T(8,128)(2,1)S(1)} fusion(bf16[9,180,48]{1,2,0:T(8,128)(2,1)} %param.18, s32[2,9]{1,0:T(2,128)S(1)} %fusion.63), kind=kOutput, calls=%fused_computation.13 | convolution fusion | flops 2955042 | bytes 466632 | tf_op jit(solution)/shard_map/vpq,qcs->vpcs/dot_general | solution.py:278
  47.3 1.1 convolution_convert_fusion.2
  48.5 0.3 pad_maximum_fusion.4
  48.8 4.8 %collective-permute-start.2 = (bf16[2,40,4,181]{3,2,1,0:T(4,128)(2,1)S(1)}, bf16[2,40,4,181]{3,2,1,0:T(4,128)(2,1)S(1)}, u32[]{:S(2)}, u32[]{:S(2)}) collective-permute-start(bf16[2,40,4,181]{3,2,1,0:T(4,128)(2,1)S(1)} %get-tuple-element.5), channel_id=1, source_target_pairs={{0,1},{1,2},{2,3},{3,4},{4,5},{5,6},{6,7},{8,9},{9,10},{10,11},{11... | collective-permute-start | bytes 347528 | tf_op jit(solution)/shard_map/ppermute | solution.py:30
  53.5 1.9 %collective-permute-start.3 = (bf16[2,40,4,181]{3,2,1,0:T(4,128)(2,1)S(1)}, bf16[2,40,4,181]{3,2,1,0:T(4,128)(2,1)S(1)}, u32[]{:S(2)}, u32[]{:S(2)}) collective-permute-start(bf16[2,40,4,181]{3,2,1,0:T(4,128)(2,1)S(1)} %get-tuple-element.6), channel_id=1, source_target_pairs={{1,0},{2,1},{3,2},{4,3},{5,4},{6,5},{7,6},{9,8},{10,9},{11,10},{12... | collective-permute-start | bytes 347528 | tf_op jit(solution)/shard_map/ppermute | solution.py:32
  55.5 0.2 collective-permute-done.2
  55.8 5.0 %collective-permute-done.3 = bf16[2,40,4,181]{3,2,1,0:T(4,128)(2,1)S(1)} collective-permute-done((bf16[2,40,4,181]{3,2,1,0:T(4,128)(2,1)S(1)}, bf16[2,40,4,181]{3,2,1,0:T(4,128)(2,1)S(1)}, u32[]{:S(2)}, u32[]{:S(2)}) %collective-permute-start.3) | collective-permute-done | bytes 115872 | tf_op jit(solution)/shard_map/ppermute | solution.py:32
  60.8 0.7 copy-done.6
  61.5 0.6 maximum_reduce_fusion
  62.3 0.9 reshape.831.labq_ref
  63.3 2.6 %pad_maximum_fusion = bf16[2,40,40,181]{3,2,1,0:T(8,128)(2,1)S(1)} fusion(bf16[2,40,4,181]{3,2,1,0:T(4,128)(2,1)} %copy-done.6, bf16[2,4,32,181]{3,2,1,0:T(8,128)(2,1)S(1)} %collective-permute-done.1, bf16[2,32,32,1]{3,2,1,0:T(8,128)(2,1)} %copy-done.2, bf16[2,32,32,180]{3,2,1,0:T(8,128)(2,1)} %bitcast.210, ...), kind=kLoop, calls=%fused_computation.9 | loop fusion | flops 6950400 | bytes 2316800 | tf_op jit(solution)/shard_map/concatenate | solution.py:28
  66.1 1.7 %pad.11 = bf16[2,28,64,180]{3,2,1,0:T(8,128)(2,1)} pad(bf16[2,25,64,180]{3,2,1,0:T(8,128)(2,1)S(1)} %bitcast.214, bf16[]{:T(256)} %constant.302.clone.1), padding=0_0x0_3x0_0x0_0 | pad | bytes 2442242 | tf_op jit(solution)/shard_map/jit(_pad)/pad | solution.py:171
  67.8 28.2 %shard_map.110 = bf16[2,7,256,180]{3,2,1,0:T(8,128)(2,1)S(1)} custom-call(bf16[2,7,256,180]{3,2,1,0:T(8,128)(2,1)} %bitcast.212, s32[7,256,1]{2,1,0:T(8,128)S(1)} %reshape.831.labq_ref, s32[7,1,256]{2,1,0:T(1,128)S(1)} %reshape.801.labk_ref, f32[2,6,64,256]{3,2,1,0:T(8,128)S(1)} %tile.21.bias_ref, bf16[2,180,540]{2,1,0:T(8,128)(2,1)S(1)} %copy.70.wqkv_ref, ...), custom_call_target="tpu_custom_call" | custom-call | tf_op jit(solution)/shard_map/pallas_call | solution.py:180
  96.3 0.4 slice_select_fusion
  96.7 0.6 copy-done.4
  97.3 0.4 fusion.23
  97.7 0.4 convolution_add_fusion.7
  98.1 0.4 convolution_add_fusion.6
  98.6 0.4 convolution_add_fusion.5
  99.0 0.4 convolution_add_fusion.4
  99.4 0.4 convolution_add_fusion.3
  99.9 0.4 convolution_add_fusion.2
  100.3 0.4 convolution_add_fusion.1
  100.7 0.5 fusion.13
  101.2 1.0 convert_element_type.64.part_ref
  102.2 12.5 %shard_map.111 = f32[32,1536]{1,0:T(8,128)} custom-call(bf16[32,1536]{1,0:T(8,128)(2,1)} %convert_element_type.64.part_ref), custom_call_target="tpu_custom_call" | custom-call | tf_op jit(solution)/shard_map/pallas_call | solution.py:82
  114.6 0.9 broadcast_multiply_fusion
  116.1 0.4 fusion.26
  116.7 0.5 convolution_convert_fusion.1
  117.2 0.4 copy.89
  117.6 0.3 fusion.12
  117.9 0.7 fusion.85
  118.8 0.4 convolution_convert_fusion.3
  119.2 0.3 copy-done.16
  119.5 1.0 convolution_add_fusion.8
  120.5 1.9 %reshape.810 = f32[4,4,8,8,12,4]{3,2,5,4,1,0:T(8,128)S(1)} reshape(f32[16,64,48]{1,2,0:T(8,128)} %convolution_add_fusion.8) | data formatting | bytes 393216 | tf_op jit(solution)/shard_map/reshape | solution.py:393
  122.4 2.8 %copy.97 = f32[12,4,8,4,8,4]{2,1,5,4,3,0:T(4,128)} copy(f32[12,4,8,4,8,4]{4,2,5,0,3,1:T(8,128)S(1)} %bitcast.211) | data formatting | bytes 393216 | tf_op jit(solution)/shard_map/transpose | solution.py:395
  125.3 2.8 %reshape.811 = f32[3,4,32,128]{2,3,1,0:T(8,128)S(1)} reshape(f32[12,4,8,4,8,4]{2,1,5,4,3,0:T(4,128)} %copy.97) | data formatting | bytes 393216 | tf_op jit(solution)/shard_map/reshape | solution.py:396
  128.1 0.9 copy.98
  (80 shorter events, 3.3 us)
Async XLA Ops:
  0.0 116.7 %copy-start = (bf16[48,144]{1,0:T(8,128)(2,1)S(1)}, bf16[48,144]{1,0:T(8,128)(2,1)}, u32[]{:S(2)}) copy-start(bf16[48,144]{1,0:T(8,128)(2,1)} %param.19) | copy-start | bytes 41476
  3.5 1.9 %copy-start.12 = (s32[2,64,64]{2,1,0:T(8,128)}, s32[2,64,64]{2,1,0:T(8,128)S(1)}, u32[]{:S(2)}) copy-start(s32[2,64,64]{2,1,0:T(8,128)S(1)} %fusion.35) | copy-start | bytes 98308
  7.0 2.3 %copy-start.8 = (bf16[2,180,540]{2,0,1:T(2,128)(2,1)S(1)}, bf16[2,180,540]{2,0,1:T(2,128)(2,1)}, u32[]{:S(2)}) copy-start(bf16[2,180,540]{2,0,1:T(2,128)(2,1)} %param.13) | copy-start | bytes 1166404
  7.0 2.4 %copy-start.9 = (bf16[2,360,180]{1,0,2:T(2,128)(2,1)S(1)}, bf16[2,360,180]{1,0,2:T(2,128)(2,1)}, u32[]{:S(2)}) copy-start(bf16[2,360,180]{1,0,2:T(2,128)(2,1)} %param.16) | copy-start | bytes 777604
  7.0 2.7 %copy-start.10 = (bf16[2,180,360]{2,0,1:T(2,128)(2,1)S(1)}, bf16[2,180,360]{2,0,1:T(2,128)(2,1)}, u32[]{:S(2)}) copy-start(bf16[2,180,360]{2,0,1:T(2,128)(2,1)} %param.15) | copy-start | bytes 777604
  9.3 1.4 %copy-start.7 = (bf16[32,32,180]{2,1,0:T(8,128)(2,1)S(1)}, bf16[32,32,180]{2,1,0:T(8,128)(2,1)}, u32[]{:S(2)}) copy-start(bf16[32,32,180]{2,1,0:T(8,128)(2,1)} %param.11) | copy-start | bytes 1105924
  24.9 35.9 %copy-start.1 = (bf16[2,4,4,8,8,180]{5,4,2,3,1,0:T(8,128)(2,1)}, bf16[2,4,4,8,8,180]{5,4,2,3,1,0:T(8,128)(2,1)S(1)}, u32[]{:S(2)}) copy-start(bf16[2,4,4,8,8,180]{5,4,2,3,1,0:T(8,128)(2,1)S(1)} %copy.74) | copy-start | bytes 2211844
  24.9 11.8 %copy-start.13 = (s32[2,64,64]{2,1,0:T(8,128)S(1)}, s32[2,64,64]{2,1,0:T(8,128)}, u32[]{:S(2)}) copy-start(s32[2,64,64]{2,1,0:T(8,128)} %copy-done.12) | copy-start | bytes 98308
  25.2 0.9 copy-start.2
  26.9 21.6 %collective-permute-start = (bf16[2,4,32,181]{3,2,1,0:T(8,128)(2,1)}, bf16[2,4,32,181]{3,2,1,0:T(8,128)(2,1)S(1)}, u32[]{:S(2)}, u32[]{:S(2)}) collective-permute-start(bf16[2,4,32,181]{3,2,1,0:T(8,128)(2,1)} %get-tuple-element.7), channel_id=1, source_target_pairs={{0,8},{8,16},{16,24},{24,32},{32,40},{40,48},{48,56},{1,9},{9,17},... | collective-permute-start | bytes 278024 | tf_op jit(solution)/shard_map/ppermute | solution.py:30
  30.1 18.4 %collective-permute-start.1 = (bf16[2,4,32,181]{3,2,1,0:T(8,128)(2,1)}, bf16[2,4,32,181]{3,2,1,0:T(8,128)(2,1)S(1)}, u32[]{:S(2)}, u32[]{:S(2)}) collective-permute-start(bf16[2,4,32,181]{3,2,1,0:T(8,128)(2,1)} %get-tuple-element.8), channel_id=1, source_target_pairs={{8,0},{16,8},{24,16},{32,24},{40,32},{48,40},{56,48},{9,1},{17,9},... | collective-permute-start | bytes 278024 | tf_op jit(solution)/shard_map/ppermute | solution.py:32
  40.2 2.3 %copy-start.17 = (f32[2,225]{1,0:T(2,128)S(1)}, f32[2,225]{1,0:T(2,128)}, u32[]{:S(2)}) copy-start(f32[2,225]{1,0:T(2,128)} %param.21) | copy-start | bytes 5404
  40.2 2.3 %copy-start.15 = (s32[64,64]{1,0:T(8,128)S(1)}, s32[64,64]{1,0:T(8,128)}, u32[]{:S(2)}) copy-start(s32[64,64]{1,0:T(8,128)} %get-tuple-element.20) | copy-start | bytes 49156
  42.5 4.8 %copy-start.18 = (s32[48]{0:T(128)S(1)}, s32[48]{0:T(128)}, u32[]{:S(2)}) copy-start(s32[48]{0:T(128)} %get-tuple-element.40) | copy-start | bytes 580
  42.5 4.8 %copy-start.19 = (s32[48]{0:T(128)S(1)}, s32[48]{0:T(128)}, u32[]{:S(2)}) copy-start(s32[48]{0:T(128)} %get-tuple-element.41) | copy-start | bytes 580
  42.5 4.8 %copy-start.20 = (s32[48]{0:T(128)S(1)}, s32[48]{0:T(128)}, u32[]{:S(2)}) copy-start(s32[48]{0:T(128)} %broadcast_subtract_fusion.3) | copy-start | bytes 580
  44.3 4.2 %copy-start.3 = (bf16[2,32,32,1]{3,2,1,0:T(8,128)(2,1)S(1)}, bf16[2,32,32,1]{3,2,1,0:T(8,128)(2,1)}, u32[]{:S(2)}) copy-start(bf16[2,32,32,1]{3,2,1,0:T(8,128)(2,1)} %copy-done.2) | copy-start | bytes 12292
  48.8 7.0 %collective-permute-start.2 = (bf16[2,40,4,181]{3,2,1,0:T(4,128)(2,1)S(1)}, bf16[2,40,4,181]{3,2,1,0:T(4,128)(2,1)S(1)}, u32[]{:S(2)}, u32[]{:S(2)}) collective-permute-start(bf16[2,40,4,181]{3,2,1,0:T(4,128)(2,1)S(1)} %get-tuple-element.5), channel_id=1, source_target_pairs={{0,1},{1,2},{2,3},{3,4},{4,5},{5,6},{6,7},{8,9},{9,10},{10,11},{11... | collective-permute-start | bytes 347528 | tf_op jit(solution)/shard_map/ppermute | solution.py:30
  53.5 7.3 %collective-permute-start.3 = (bf16[2,40,4,181]{3,2,1,0:T(4,128)(2,1)S(1)}, bf16[2,40,4,181]{3,2,1,0:T(4,128)(2,1)S(1)}, u32[]{:S(2)}, u32[]{:S(2)}) collective-permute-start(bf16[2,40,4,181]{3,2,1,0:T(4,128)(2,1)S(1)} %get-tuple-element.6), channel_id=1, source_target_pairs={{1,0},{2,1},{3,2},{4,3},{5,4},{6,5},{7,6},{9,8},{10,9},{11,10},{12... | collective-permute-start | bytes 347528 | tf_op jit(solution)/shard_map/ppermute | solution.py:32
  55.8 5.0 %copy-start.5 = (bf16[2,40,4,181]{3,2,1,0:T(4,128)(2,1)}, bf16[2,40,4,181]{3,2,1,0:T(4,128)(2,1)S(1)}, u32[]{:S(2)}) copy-start(bf16[2,40,4,181]{3,2,1,0:T(4,128)(2,1)S(1)} %collective-permute-done.2) | copy-start | bytes 347524
  60.8 0.7 copy-start.6
  96.3 1.0 copy-start.4
  116.1 1.5 %copy-start.11 = (pred[16,64,64]{1,2,0:T(8,128)(4,1)S(1)}, pred[16,64,64]{1,2,0:T(8,128)(4,1)}, u32[]{:S(2)}) copy-start(pred[16,64,64]{1,2,0:T(8,128)(4,1)} %broadcast_compare_fusion) | copy-start | bytes 196612
  116.1 1.5 %copy-start.14 = (f32[2,64,64]{1,2,0:T(8,128)S(1)}, f32[2,64,64]{1,2,0:T(8,128)}, u32[]{:S(2)}) copy-start(f32[2,64,64]{1,2,0:T(8,128)} %copy.93) | copy-start | bytes 98308
  118.8 0.7 copy-start.16

commit v3 on v2

--- a/solution.py
+++ b/solution.py
@@ -133,9 +133,9 @@
                 preferred_element_type=jnp.float32,
             )
             scores = scores * scale
-            scores = (scores.reshape(GROUP, WIN * WIN, tokens) + bias_ref[variant, head][None]).reshape(
-                tokens, tokens
-            )
+            table = bias_ref[variant, head]
+            table = jnp.concatenate([table] * GROUP, axis=1)
+            scores = (scores.reshape(GROUP, WIN * WIN, tokens) + table[None]).reshape(tokens, tokens)
             scores = jnp.where(match, scores, MASKED)
             largest = jnp.max(scores, axis=-1, keepdims=True)
             weights = jnp.exp(scores - largest)
@@ -174,7 +174,7 @@
     x = windows.reshape(inputs, groups, tokens, channels)
     labq = region.reshape(groups, tokens, 1)
     labk = region.reshape(groups, 1, tokens)
-    bias = jnp.tile(bias_grid, (1, 1, 1, GROUP))
+    bias = bias_grid
     scale = (channels // heads) ** (-0.5)
     whole = lambda shape: pl.BlockSpec(shape, lambda g: (0,) * len(shape))
     out = pl.pallas_call(

time: 130 us -> 133 us (1.023)
  Pallas kernels: 54.8 us -> 65.2 us
  local copies, waits for them, and re-layouts: 28.2 us -> 22.3 us
  other arithmetic: 12.1 us -> 10.6 us
    pallas_call x2, Pallas kernels: 42.3 us -> 52.7 us  [swin_block(): pl.pallas_call(functools.partial(block_kernel, variants, heads, scale), o...]
    another operation x4 -> x0, local copies, waits for them, and re-layouts: 7.48 us -> none  [swin_block(): bias = jnp.tile(bias_grid, (1, 1, 1, GROUP))]
    unnamed x46 -> x30, local copies, waits for them, and re-layouts: 3.8 us -> 4.04 us
  transfers between devices with their start and end apart: 4 -> 4, of which waited for: 2 -> 2; matrix products, arithmetic and copies ran while one was open for 11% -> 6% of each run, Pallas kernels for 0% -> 0%
where the time goes in v3:
time: 133 us; the launch traced here: 132 us
  Pallas kernels  65.2 us (49%)
  local copies, waits for them, and re-layouts  22.3 us (17%)
  starting transfers between devices  14.2 us (11%)
  matrix products  13.8 us (10%)
  other arithmetic  10.6 us (8%)
  waiting for transfers between devices  5.09 us (4%)
    pallas_call x2, Pallas kernels, swin_block(): pl.pallas_call(functools.partial(block_kernel, variants, heads, scale), o...  52.7 us
    pallas_call x1, Pallas kernels, var_sum(): pl.pallas_call(functools.partial(var_sum_kernel, count), out_shape=jax.Sh...  12.5 us
    ppermute x2, starting transfers between devices, extended(): lax.ppermute(tail, axis, [(i, (i + 1) % count) for i in range(ends)])  7.95 us
    ppermute x2, starting transfers between devices, extended(): lax.ppermute(head, axis, [((i + 1) % count, i) for i in range(ends)])  6.29 us
    ppermute x2, waiting for transfers between devices, extended(): lax.ppermute(head, axis, [((i + 1) % count, i) for i in range(ends)])  5.03 us
    dot_general x3, matrix products, bias_table(): jnp.einsum('vqkt,ht->vhqk', one_hot, parts, preferred_element_type=jnp.fl...  4.62 us
    unnamed x30, local copies, waits for them, and re-layouts  4.04 us
    dot_general x9, matrix products, reconstruct(): jnp.einsum('vrcd,vde->vrce', window, kernels[:, kernel_spot], preferred_e...  3.85 us
  transfers between devices with their start and end apart: 4, of which 2 were waited for; matrix products, arithmetic and copies ran while one was open for 6% of the time, Pallas kernels for 0%

profile of v3, /device:TPU:99, one launch (start us, length us, event | category | flops | bytes accessed | tf_op | source)
XLA Modules:
  0.0 131.8 jit_solution(18100921200964189253)
XLA Ops:
  0.0 0.8 reshape_broadcast_in_dim.9
  0.9 0.2 reshape.822.labq_ref
  1.2 0.7 convert_element_type.59
  1.9 0.8 fusion.82
  2.9 1.8 %fusion.2 = f32[18,2,64,64]{3,0,2,1:T(8,128)S(1)} fusion(s32[2,64,64]{2,1,0:T(8,128)S(1)} %fusion.33, bf16[6,225]{1,0:T(8,128)(2,1)S(1)} %get-tuple-element.30, bf16[6,225]{1,0:T(8,128)(2,1)S(1)} %get-tuple-element.29, bf16[6,225]{1,0:T(8,128)(2,1)S(1)} %get-tuple-element.31), kind=kOutput, calls=%fused_computation.3 | convolution fusion | flops 68222704 | bytes 630692 | tf_op jit(solution)/shard_map/vqkt,ht->vhqk/dot_general | solution.py:250
  4.7 0.2 copy.151
  5.0 0.7 copy-done.5
  5.9 0.3 copy.73.wdown_ref
  6.3 0.9 copy.71.wp_ref
  7.2 1.1 copy.65
  8.3 17.1 %shard_map.109 = bf16[2,4,256,180]{3,2,1,0:T(8,128)(2,1)S(1)} custom-call(bf16[1,4,256,180]{3,2,1,0:T(8,128)(2,1)S(1)} %bitcast.208, s32[4,256,1]{2,1,0:T(8,128)S(1)} %reshape.822.labq_ref, s32[4,1,256]{2,1,0:T(1,128)S(1)} %reshape.787.labk_ref, f32[2,6,64,64]{3,2,1,0:T(8,128)S(1)} %slice_add_fusion.2.bias_ref, bf16[2,180,540]{2,1,0:T(8,128)(2,1)S(1)} %copy.70.wqkv_ref, ...), custom_call_target="tpu_custom_call" | custom-call | tf_op jit(solution)/shard_map/pallas_call | solution.py:180
  25.5 0.2 broadcast_in_dim.264
  25.7 0.8 pad_maximum_fusion.6
  26.6 3.2 %collective-permute-start = (bf16[2,4,32,181]{3,2,1,0:T(8,128)(2,1)}, bf16[2,4,32,181]{3,2,1,0:T(8,128)(2,1)S(1)}, u32[]{:S(2)}, u32[]{:S(2)}) collective-permute-start(bf16[2,4,32,181]{3,2,1,0:T(8,128)(2,1)} %get-tuple-element.7), channel_id=1, source_target_pairs={{0,8},{8,16},{16,24},{24,32},{32,40},{40,48},{48,56},{1,9},{9,17},... | collective-permute-start | bytes 278024 | tf_op jit(solution)/shard_map/ppermute | solution.py:30
  29.8 4.2 %collective-permute-start.1 = (bf16[2,4,32,181]{3,2,1,0:T(8,128)(2,1)}, bf16[2,4,32,181]{3,2,1,0:T(8,128)(2,1)}, u32[]{:S(2)}, u32[]{:S(2)}) collective-permute-start(bf16[2,4,32,181]{3,2,1,0:T(8,128)(2,1)} %get-tuple-element.8), channel_id=1, source_target_pairs={{8,0},{16,8},{24,16},{32,24},{40,32},{48,40},{56,48},{9,1},{17,9},... | collective-permute-start | bytes 278024 | tf_op jit(solution)/shard_map/ppermute | solution.py:32
  34.0 0.6 fusion.75
  34.7 1.8 %fusion.1 = f32[18,2,64,64]{3,0,2,1:T(8,128)S(1)} fusion(s32[2,64,64]{2,1,0:T(8,128)S(1)} %fusion.33, bf16[6,225]{1,0:T(8,128)(2,1)S(1)} %get-tuple-element.12, bf16[6,225]{1,0:T(8,128)(2,1)S(1)} %get-tuple-element.13, bf16[6,225]{1,0:T(8,128)(2,1)S(1)} %get-tuple-element.11), kind=kOutput, calls=%fused_computation.2 | convolution fusion | flops 68222704 | bytes 630692 | tf_op jit(solution)/shard_map/vqkt,ht->vhqk/dot_general | solution.py:250
  36.5 0.2 copy.150
  36.8 0.4 copy-done.11
  37.2 1.0 fusion.12
  38.3 0.7 copy.93
  39.0 0.9 broadcast_compare_fusion
  39.9 1.3 %convolution_convert_fusion = bf16[2,9,180,48]{2,1,3,0:T(8,128)(2,1)S(1)} fusion(bf16[9,180,48]{1,2,0:T(8,128)(2,1)} %param.18, s32[2,9]{1,0:T(2,128)S(1)} %fusion.61), kind=kOutput, calls=%fused_computation.11 | convolution fusion | flops 2955042 | bytes 466632 | tf_op jit(solution)/shard_map/vpq,qcs->vpcs/dot_general | solution.py:278
  41.3 1.1 convolution_convert_fusion.2
  42.5 1.0 pad_maximum_fusion.4
  43.5 4.8 %collective-permute-start.2 = (bf16[2,40,4,181]{3,2,1,0:T(4,128)(2,1)S(1)}, bf16[2,40,4,181]{3,2,1,0:T(4,128)(2,1)S(1)}, u32[]{:S(2)}, u32[]{:S(2)}) collective-permute-start(bf16[2,40,4,181]{3,2,1,0:T(4,128)(2,1)S(1)} %get-tuple-element.5), channel_id=1, source_target_pairs={{0,1},{1,2},{2,3},{3,4},{4,5},{5,6},{6,7},{8,9},{9,10},{10,11},{11... | collective-permute-start | bytes 347528 | tf_op jit(solution)/shard_map/ppermute | solution.py:30
  48.3 2.1 %collective-permute-start.3 = (bf16[2,40,4,181]{3,2,1,0:T(4,128)(2,1)S(1)}, bf16[2,40,4,181]{3,2,1,0:T(4,128)(2,1)S(1)}, u32[]{:S(2)}, u32[]{:S(2)}) collective-permute-start(bf16[2,40,4,181]{3,2,1,0:T(4,128)(2,1)S(1)} %get-tuple-element.6), channel_id=1, source_target_pairs={{1,0},{2,1},{3,2},{4,3},{5,4},{6,5},{7,6},{9,8},{10,9},{11,10},{12... | collective-permute-start | bytes 347528 | tf_op jit(solution)/shard_map/ppermute | solution.py:32
  50.6 5.0 %collective-permute-done.3 = bf16[2,40,4,181]{3,2,1,0:T(4,128)(2,1)S(1)} collective-permute-done((bf16[2,40,4,181]{3,2,1,0:T(4,128)(2,1)S(1)}, bf16[2,40,4,181]{3,2,1,0:T(4,128)(2,1)S(1)}, u32[]{:S(2)}, u32[]{:S(2)}) %collective-permute-start.3) | collective-permute-done | bytes 115872 | tf_op jit(solution)/shard_map/ppermute | solution.py:32
  55.6 0.7 copy-done.4
  56.3 1.3 maximum_reduce_fusion
  57.8 0.9 reshape.823.labq_ref
  58.8 2.5 %pad_maximum_fusion = bf16[2,40,40,181]{3,2,1,0:T(8,128)(2,1)S(1)} fusion(bf16[2,40,4,181]{3,2,1,0:T(4,128)(2,1)} %copy-done.4, bf16[2,4,32,181]{3,2,1,0:T(8,128)(2,1)} %collective-permute-done.1, bf16[2,32,32,1]{3,2,1,0:T(8,128)(2,1)S(1)} %broadcast_in_dim.264, bf16[2,32,32,180]{3,2,1,0:T(8,128)(2,1)} %bitcast.212, ...), kind=kLoop, calls=%fused_computation.9 | loop fusion | flops 6950400 | bytes 2316800 | tf_op jit(solution)/shard_map/concatenate | solution.py:28
  61.3 0.2 copy.75
  61.5 1.7 %pad.11 = bf16[2,28,64,180]{3,2,1,0:T(8,128)(2,1)} pad(bf16[2,25,64,180]{3,2,1,0:T(8,128)(2,1)S(1)} %bitcast.216, bf16[]{:T(256)} %constant.302.clone.1), padding=0_0x0_3x0_0x0_0 | pad | bytes 2442242 | tf_op jit(solution)/shard_map/jit(_pad)/pad | solution.py:171
  63.1 35.7 %shard_map.110 = bf16[2,7,256,180]{3,2,1,0:T(8,128)(2,1)S(1)} custom-call(bf16[2,7,256,180]{3,2,1,0:T(8,128)(2,1)} %bitcast.214, s32[7,256,1]{2,1,0:T(8,128)S(1)} %reshape.823.labq_ref, s32[7,1,256]{2,1,0:T(1,128)S(1)} %reshape.793.labk_ref, f32[2,6,64,64]{3,2,1,0:T(8,128)S(1)} %slice_add_fusion.bias_ref, bf16[2,180,540]{2,1,0:T(8,128)(2,1)S(1)} %copy.70.wqkv_ref, ...), custom_call_target="tpu_custom_call" | custom-call | tf_op jit(solution)/shard_map/pallas_call | solution.py:180
  99.1 0.4 slice_select_fusion
  99.5 0.6 copy-done.2
  100.1 0.4 fusion.21
  100.5 0.4 convolution_add_fusion.7
  100.9 0.4 convolution_add_fusion.6
  101.4 0.4 convolution_add_fusion.5
  101.8 0.4 convolution_add_fusion.4
  102.2 0.4 convolution_add_fusion.3
  102.7 0.4 convolution_add_fusion.2
  103.1 0.4 convolution_add_fusion.1
  103.5 0.5 fusion.11
  104.0 1.0 convert_element_type.64.part_ref
  104.9 12.5 %shard_map.111 = f32[32,1536]{1,0:T(8,128)} custom-call(bf16[32,1536]{1,0:T(8,128)(2,1)} %convert_element_type.64.part_ref), custom_call_target="tpu_custom_call" | custom-call | tf_op jit(solution)/shard_map/pallas_call | solution.py:82
  117.4 0.9 broadcast_multiply_fusion
  118.4 0.2 div.142
  118.6 0.2 bitcast_reduce_fusion
  118.9 0.4 fusion.24
  119.5 0.5 convolution_convert_fusion.1
  120.0 0.4 copy.89
  120.4 0.3 fusion.10
  120.7 0.7 fusion.83
  121.4 0.2 copy.96
  121.6 0.4 convolution_convert_fusion.3
  122.0 0.3 copy-done.10
  122.3 1.0 convolution_add_fusion.8
  123.3 1.9 %reshape.802 = f32[4,4,8,8,12,4]{3,2,5,4,1,0:T(8,128)S(1)} reshape(f32[16,64,48]{1,2,0:T(8,128)} %convolution_add_fusion.8) | data formatting | bytes 393216 | tf_op jit(solution)/shard_map/reshape | solution.py:393
  125.2 2.8 %copy.97 = f32[12,4,8,4,8,4]{2,1,5,4,3,0:T(4,128)} copy(f32[12,4,8,4,8,4]{4,2,5,0,3,1:T(8,128)S(1)} %bitcast.213) | data formatting | bytes 393216 | tf_op jit(solution)/shard_map/transpose | solution.py:395
  128.0 2.8 %reshape.803 = f32[3,4,32,128]{2,3,1,0:T(8,128)S(1)} reshape(f32[12,4,8,4,8,4]{2,1,5,4,3,0:T(4,128)} %copy.97) | data formatting | bytes 393216 | tf_op jit(solution)/shard_map/reshape | solution.py:396
  130.9 0.9 copy.98
  (60 shorter events, 2.1 us)
Async XLA Ops:
  0.0 119.5 %copy-start = (bf16[48,144]{1,0:T(8,128)(2,1)S(1)}, bf16[48,144]{1,0:T(8,128)(2,1)}, u32[]{:S(2)}) copy-start(bf16[48,144]{1,0:T(8,128)(2,1)} %param.19) | copy-start | bytes 41476
  4.7 1.0 copy-start.5
  4.9 1.0 copy-start.6
  5.0 1.2 copy-start.7
  25.5 30.1 %copy-start.1 = (bf16[2,4,4,8,8,180]{5,4,2,3,1,0:T(8,128)(2,1)}, bf16[2,4,4,8,8,180]{5,4,2,3,1,0:T(8,128)(2,1)S(1)}, u32[]{:S(2)}) copy-start(bf16[2,4,4,8,8,180]{5,4,2,3,1,0:T(8,128)(2,1)S(1)} %copy.74) | copy-start | bytes 2211844
  26.6 15.9 %collective-permute-start = (bf16[2,4,32,181]{3,2,1,0:T(8,128)(2,1)}, bf16[2,4,32,181]{3,2,1,0:T(8,128)(2,1)S(1)}, u32[]{:S(2)}, u32[]{:S(2)}) collective-permute-start(bf16[2,4,32,181]{3,2,1,0:T(8,128)(2,1)} %get-tuple-element.7), channel_id=1, source_target_pairs={{0,8},{8,16},{16,24},{24,32},{32,40},{40,48},{48,56},{1,9},{9,17},... | collective-permute-start | bytes 278024 | tf_op jit(solution)/shard_map/ppermute | solution.py:30
  29.8 12.7 %collective-permute-start.1 = (bf16[2,4,32,181]{3,2,1,0:T(8,128)(2,1)}, bf16[2,4,32,181]{3,2,1,0:T(8,128)(2,1)}, u32[]{:S(2)}, u32[]{:S(2)}) collective-permute-start(bf16[2,4,32,181]{3,2,1,0:T(8,128)(2,1)} %get-tuple-element.8), channel_id=1, source_target_pairs={{8,0},{16,8},{24,16},{32,24},{40,32},{48,40},{56,48},{9,1},{17,9},... | collective-permute-start | bytes 278024 | tf_op jit(solution)/shard_map/ppermute | solution.py:32
  36.5 0.7 copy-start.11
  36.7 3.1 %copy-start.12 = (s32[9]{0:T(128)S(1)}, s32[9]{0:T(128)}, u32[]{:S(2)}) copy-start(s32[9]{0:T(128)} %get-tuple-element.37) | copy-start | bytes 112
  43.5 7.0 %collective-permute-start.2 = (bf16[2,40,4,181]{3,2,1,0:T(4,128)(2,1)S(1)}, bf16[2,40,4,181]{3,2,1,0:T(4,128)(2,1)S(1)}, u32[]{:S(2)}, u32[]{:S(2)}) collective-permute-start(bf16[2,40,4,181]{3,2,1,0:T(4,128)(2,1)S(1)} %get-tuple-element.5), channel_id=1, source_target_pairs={{0,1},{1,2},{2,3},{3,4},{4,5},{5,6},{6,7},{8,9},{9,10},{10,11},{11... | collective-permute-start | bytes 347528 | tf_op jit(solution)/shard_map/ppermute | solution.py:30
  48.3 7.3 %collective-permute-start.3 = (bf16[2,40,4,181]{3,2,1,0:T(4,128)(2,1)S(1)}, bf16[2,40,4,181]{3,2,1,0:T(4,128)(2,1)S(1)}, u32[]{:S(2)}, u32[]{:S(2)}) collective-permute-start(bf16[2,40,4,181]{3,2,1,0:T(4,128)(2,1)S(1)} %get-tuple-element.6), channel_id=1, source_target_pairs={{1,0},{2,1},{3,2},{4,3},{5,4},{6,5},{7,6},{9,8},{10,9},{11,10},{12... | collective-permute-start | bytes 347528 | tf_op jit(solution)/shard_map/ppermute | solution.py:32
  50.6 5.0 %copy-start.3 = (bf16[2,40,4,181]{3,2,1,0:T(4,128)(2,1)}, bf16[2,40,4,181]{3,2,1,0:T(4,128)(2,1)S(1)}, u32[]{:S(2)}) copy-start(bf16[2,40,4,181]{3,2,1,0:T(4,128)(2,1)S(1)} %collective-permute-done.2) | copy-start | bytes 347524
  55.6 0.7 copy-start.4
  99.1 1.0 copy-start.2
  118.9 1.5 %copy-start.8 = (pred[16,64,64]{1,2,0:T(8,128)(4,1)S(1)}, pred[16,64,64]{1,2,0:T(8,128)(4,1)}, u32[]{:S(2)}) copy-start(pred[16,64,64]{1,2,0:T(8,128)(4,1)} %broadcast_compare_fusion) | copy-start | bytes 196612
  118.9 1.5 %copy-start.9 = (f32[2,64,64]{1,2,0:T(8,128)S(1)}, f32[2,64,64]{1,2,0:T(8,128)}, u32[]{:S(2)}) copy-start(f32[2,64,64]{1,2,0:T(8,128)} %copy.93) | copy-start | bytes 98308
  121.6 0.7 copy-start.10

commit v4 on v2

--- a/solution.py
+++ b/solution.py
@@ -99,8 +99,14 @@
 
 
 def block_kernel(
-    variants, heads, scale, x_ref, labq_ref, labk_ref, bias_ref, wqkv_ref, wp_ref, wup_ref, wdown_ref, out_ref
+    variants, heads, scale, x_ref, labq_ref, labk_ref, bias_ref, wqkv_ref, wp_ref, wup_ref, wdown_ref, out_ref, wide_ref
 ):
+    @pl.when(pl.program_id(0) == 0)
+    def _():
+        for variant in range(variants):
+            for head in range(heads):
+                wide_ref[variant, head] = jnp.concatenate([bias_ref[variant, head]] * GROUP, axis=1)
+
     inputs = x_ref.shape[0]
     tokens = x_ref.shape[2]
     labq = labq_ref[0]
@@ -133,7 +139,7 @@
                 preferred_element_type=jnp.float32,
             )
             scores = scores * scale
-            scores = (scores.reshape(GROUP, WIN * WIN, tokens) + bias_ref[variant, head][None]).reshape(
+            scores = (scores.reshape(GROUP, WIN * WIN, tokens) + wide_ref[variant, head][None]).reshape(
                 tokens, tokens
             )
             scores = jnp.where(match, scores, MASKED)
@@ -174,7 +180,7 @@
     x = windows.reshape(inputs, groups, tokens, channels)
     labq = region.reshape(groups, tokens, 1)
     labk = region.reshape(groups, 1, tokens)
-    bias = jnp.tile(bias_grid, (1, 1, 1, GROUP))
+    bias = bias_grid
     scale = (channels // heads) ** (-0.5)
     whole = lambda shape: pl.BlockSpec(shape, lambda g: (0,) * len(shape))
     out = pl.pallas_call(
@@ -192,6 +198,7 @@
             pl.BlockSpec((None,) + w_down.shape[1:], lambda g: (layer, 0, 0)),
         ],
         out_specs=pl.BlockSpec((variants, 1, tokens, channels), lambda g: (0, g, 0, 0)),
+        scratch_shapes=[pltpu.VMEM((variants, heads, cells, tokens), jnp.float32)],
         compiler_params=pltpu.CompilerParams(vmem_limit_bytes=48 * 1024 * 1024),
     )(x, labq, labk, bias, w_qkv, w_proj, w_up, w_down)
     out = out.reshape(variants, groups * GROUP, cells, channels)

time: 130 us -> 122 us (0.938)
  local copies, waits for them, and re-layouts: 28.2 us -> 22.3 us
  other arithmetic: 12.1 us -> 10.6 us
    another operation x4 -> x0, local copies, waits for them, and re-layouts: 7.48 us -> none  [swin_block(): bias = jnp.tile(bias_grid, (1, 1, 1, GROUP))]
    unnamed x46 -> x30, local copies, waits for them, and re-layouts: 3.8 us -> 4.04 us
  transfers between devices with their start and end apart: 4 -> 4, of which waited for: 2 -> 2; matrix products, arithmetic and copies ran while one was open for 11% -> 7% of each run, Pallas kernels for 0% -> 0%
where the time goes in v4:
time: 122 us
  Pallas kernels  54.9 us (45%)
  local copies, waits for them, and re-layouts  22.3 us (18%)
  starting transfers between devices  14.2 us (12%)
  matrix products  13.8 us (11%)
  other arithmetic  10.6 us (9%)
  waiting for transfers between devices  5.09 us (4%)
    pallas_call x2, Pallas kernels, swin_block(): pl.pallas_call(functools.partial(block_kernel, variants, heads, scale), o...  42.4 us
    pallas_call x1, Pallas kernels, var_sum(): pl.pallas_call(functools.partial(var_sum_kernel, count), out_shape=jax.Sh...  12.5 us
    ppermute x2, starting transfers between devices, extended(): lax.ppermute(tail, axis, [(i, (i + 1) % count) for i in range(ends)])  7.96 us
    ppermute x2, starting transfers between devices, extended(): lax.ppermute(head, axis, [((i + 1) % count, i) for i in range(ends)])  6.29 us
    ppermute x2, waiting for transfers between devices, extended(): lax.ppermute(head, axis, [((i + 1) % count, i) for i in range(ends)])  5.03 us
    dot_general x3, matrix products, bias_table(): jnp.einsum('vqkt,ht->vhqk', one_hot, parts, preferred_element_type=jnp.fl...  4.62 us
    unnamed x30, local copies, waits for them, and re-layouts  4.04 us
    dot_general x9, matrix products, reconstruct(): jnp.einsum('vrcd,vde->vrce', window, kernels[:, kernel_spot], preferred_e...  3.85 us
  transfers between devices with their start and end apart: 4, of which 2 were waited for; matrix products, arithmetic and copies ran while one was open for 7% of the time, Pallas kernels for 0%

profile of v4, /device:TPU:99, one launch (start us, length us, event | category | flops | bytes accessed | tf_op | source)
XLA Modules:
  0.0 121.5 jit_solution(5549427363384996762)
XLA Ops:
  0.0 0.8 reshape_broadcast_in_dim.9
  0.9 0.2 reshape.822.labq_ref
  1.2 0.7 convert_element_type.59
  1.9 0.8 fusion.82
  2.9 1.8 %fusion.2 = f32[18,2,64,64]{3,0,2,1:T(8,128)S(1)} fusion(s32[2,64,64]{2,1,0:T(8,128)S(1)} %fusion.33, bf16[6,225]{1,0:T(8,128)(2,1)S(1)} %get-tuple-element.30, bf16[6,225]{1,0:T(8,128)(2,1)S(1)} %get-tuple-element.29, bf16[6,225]{1,0:T(8,128)(2,1)S(1)} %get-tuple-element.31), kind=kOutput, calls=%fused_computation.3 | convolution fusion | flops 68222704 | bytes 630692 | tf_op jit(solution)/shard_map/vqkt,ht->vhqk/dot_general | solution.py:257
  4.7 0.2 copy.151
  5.0 0.7 copy-done.5
  5.9 0.3 copy.73.wdown_ref
  6.3 0.9 copy.71.wp_ref
  7.2 1.1 copy.65
  8.3 14.1 %shard_map.109 = bf16[2,4,256,180]{3,2,1,0:T(8,128)(2,1)S(1)} custom-call(bf16[1,4,256,180]{3,2,1,0:T(8,128)(2,1)S(1)} %bitcast.208, s32[4,256,1]{2,1,0:T(8,128)S(1)} %reshape.822.labq_ref, s32[4,1,256]{2,1,0:T(1,128)S(1)} %reshape.787.labk_ref, f32[2,6,64,64]{3,2,1,0:T(8,128)S(1)} %slice_add_fusion.2.bias_ref, bf16[2,180,540]{2,1,0:T(8,128)(2,1)S(1)} %copy.70.wqkv_ref, ...), custom_call_target="tpu_custom_call" | custom-call | tf_op jit(solution)/shard_map/pallas_call | solution.py:186
  22.5 0.2 broadcast_in_dim.264
  22.8 0.8 pad_maximum_fusion.6
  23.6 3.2 %collective-permute-start = (bf16[2,4,32,181]{3,2,1,0:T(8,128)(2,1)}, bf16[2,4,32,181]{3,2,1,0:T(8,128)(2,1)S(1)}, u32[]{:S(2)}, u32[]{:S(2)}) collective-permute-start(bf16[2,4,32,181]{3,2,1,0:T(8,128)(2,1)} %get-tuple-element.7), channel_id=1, source_target_pairs={{0,8},{8,16},{16,24},{24,32},{32,40},{40,48},{48,56},{1,9},{9,17},... | collective-permute-start | bytes 278024 | tf_op jit(solution)/shard_map/ppermute | solution.py:30
  26.8 4.2 %collective-permute-start.1 = (bf16[2,4,32,181]{3,2,1,0:T(8,128)(2,1)}, bf16[2,4,32,181]{3,2,1,0:T(8,128)(2,1)}, u32[]{:S(2)}, u32[]{:S(2)}) collective-permute-start(bf16[2,4,32,181]{3,2,1,0:T(8,128)(2,1)} %get-tuple-element.8), channel_id=1, source_target_pairs={{8,0},{16,8},{24,16},{32,24},{40,32},{48,40},{56,48},{9,1},{17,9},... | collective-permute-start | bytes 278024 | tf_op jit(solution)/shard_map/ppermute | solution.py:32
  31.0 0.6 fusion.75
  31.7 1.8 %fusion.1 = f32[18,2,64,64]{3,0,2,1:T(8,128)S(1)} fusion(s32[2,64,64]{2,1,0:T(8,128)S(1)} %fusion.33, bf16[6,225]{1,0:T(8,128)(2,1)S(1)} %get-tuple-element.12, bf16[6,225]{1,0:T(8,128)(2,1)S(1)} %get-tuple-element.13, bf16[6,225]{1,0:T(8,128)(2,1)S(1)} %get-tuple-element.11), kind=kOutput, calls=%fused_computation.2 | convolution fusion | flops 68222704 | bytes 630692 | tf_op jit(solution)/shard_map/vqkt,ht->vhqk/dot_general | solution.py:257
  33.5 0.2 copy.150
  33.8 0.4 copy-done.11
  34.2 1.0 fusion.12
  35.3 0.7 copy.93
  36.0 0.9 broadcast_compare_fusion
  36.9 1.3 %convolution_convert_fusion = bf16[2,9,180,48]{2,1,3,0:T(8,128)(2,1)S(1)} fusion(bf16[9,180,48]{1,2,0:T(8,128)(2,1)} %param.18, s32[2,9]{1,0:T(2,128)S(1)} %fusion.61), kind=kOutput, calls=%fused_computation.11 | convolution fusion | flops 2955042 | bytes 466632 | tf_op jit(solution)/shard_map/vpq,qcs->vpcs/dot_general | solution.py:285
  38.4 1.1 convolution_convert_fusion.2
  39.5 1.0 pad_maximum_fusion.4
  40.6 4.8 %collective-permute-start.2 = (bf16[2,40,4,181]{3,2,1,0:T(4,128)(2,1)S(1)}, bf16[2,40,4,181]{3,2,1,0:T(4,128)(2,1)S(1)}, u32[]{:S(2)}, u32[]{:S(2)}) collective-permute-start(bf16[2,40,4,181]{3,2,1,0:T(4,128)(2,1)S(1)} %get-tuple-element.5), channel_id=1, source_target_pairs={{0,1},{1,2},{2,3},{3,4},{4,5},{5,6},{6,7},{8,9},{9,10},{10,11},{11... | collective-permute-start | bytes 347528 | tf_op jit(solution)/shard_map/ppermute | solution.py:30
  45.3 2.1 %collective-permute-start.3 = (bf16[2,40,4,181]{3,2,1,0:T(4,128)(2,1)S(1)}, bf16[2,40,4,181]{3,2,1,0:T(4,128)(2,1)S(1)}, u32[]{:S(2)}, u32[]{:S(2)}) collective-permute-start(bf16[2,40,4,181]{3,2,1,0:T(4,128)(2,1)S(1)} %get-tuple-element.6), channel_id=1, source_target_pairs={{1,0},{2,1},{3,2},{4,3},{5,4},{6,5},{7,6},{9,8},{10,9},{11,10},{12... | collective-permute-start | bytes 347528 | tf_op jit(solution)/shard_map/ppermute | solution.py:32
  47.6 5.0 %collective-permute-done.3 = bf16[2,40,4,181]{3,2,1,0:T(4,128)(2,1)S(1)} collective-permute-done((bf16[2,40,4,181]{3,2,1,0:T(4,128)(2,1)S(1)}, bf16[2,40,4,181]{3,2,1,0:T(4,128)(2,1)S(1)}, u32[]{:S(2)}, u32[]{:S(2)}) %collective-permute-start.3) | collective-permute-done | bytes 115872 | tf_op jit(solution)/shard_map/ppermute | solution.py:32
  52.6 0.7 copy-done.4
  53.3 1.3 %maximum_reduce_fusion = bf16[40,40]{1,0:T(8,128)(2,1)S(1)} fusion(bf16[2,40,4,181]{3,2,1,0:T(4,128)(2,1)S(1)} %collective-permute-done.3, bf16[2,40,4,181]{3,2,1,0:T(4,128)(2,1)S(1)} %collective-permute-done.2, bf16[2,4,32,181]{3,2,1,0:T(8,128)(2,1)} %collective-permute-done.1, bf16[2,4,32,181]{3,2,1,0:T(8,128)(2,1)S(1)} %collective-permute-done, ...), kind=kLoop, calls=%fused_computation.50 | loop fusion | flops 19200 | bytes 1161600 | tf_op jit(solution)/shard_map/slice | solution.py:378
  54.8 0.9 reshape.823.labq_ref
  55.8 2.5 %pad_maximum_fusion = bf16[2,40,40,181]{3,2,1,0:T(8,128)(2,1)S(1)} fusion(bf16[2,40,4,181]{3,2,1,0:T(4,128)(2,1)} %copy-done.4, bf16[2,4,32,181]{3,2,1,0:T(8,128)(2,1)} %collective-permute-done.1, bf16[2,32,32,1]{3,2,1,0:T(8,128)(2,1)S(1)} %broadcast_in_dim.264, bf16[2,32,32,180]{3,2,1,0:T(8,128)(2,1)} %bitcast.212, ...), kind=kLoop, calls=%fused_computation.9 | loop fusion | flops 6950400 | bytes 2316800 | tf_op jit(solution)/shard_map/concatenate | solution.py:28
  58.3 0.2 copy.75
  58.5 1.7 %pad.11 = bf16[2,28,64,180]{3,2,1,0:T(8,128)(2,1)} pad(bf16[2,25,64,180]{3,2,1,0:T(8,128)(2,1)S(1)} %bitcast.216, bf16[]{:T(256)} %constant.302.clone.1), padding=0_0x0_3x0_0x0_0 | pad | bytes 2442242 | tf_op jit(solution)/shard_map/jit(_pad)/pad | solution.py:177
  60.2 28.3 %shard_map.110 = bf16[2,7,256,180]{3,2,1,0:T(8,128)(2,1)S(1)} custom-call(bf16[2,7,256,180]{3,2,1,0:T(8,128)(2,1)} %bitcast.214, s32[7,256,1]{2,1,0:T(8,128)S(1)} %reshape.823.labq_ref, s32[7,1,256]{2,1,0:T(1,128)S(1)} %reshape.793.labk_ref, f32[2,6,64,64]{3,2,1,0:T(8,128)S(1)} %slice_add_fusion.bias_ref, bf16[2,180,540]{2,1,0:T(8,128)(2,1)S(1)} %copy.70.wqkv_ref, ...), custom_call_target="tpu_custom_call" | custom-call | tf_op jit(solution)/shard_map/pallas_call | solution.py:186
  88.8 0.4 slice_select_fusion
  89.2 0.6 copy-done.2
  89.8 0.4 fusion.21
  90.2 0.4 convolution_add_fusion.7
  90.6 0.4 convolution_add_fusion.6
  91.1 0.4 convolution_add_fusion.5
  91.5 0.4 convolution_add_fusion.4
  91.9 0.4 convolution_add_fusion.3
  92.4 0.4 convolution_add_fusion.2
  92.8 0.4 convolution_add_fusion.1
  93.2 0.5 fusion.11
  93.7 1.0 convert_element_type.64.part_ref
  94.7 12.5 %shard_map.111 = f32[32,1536]{1,0:T(8,128)} custom-call(bf16[32,1536]{1,0:T(8,128)(2,1)} %convert_element_type.64.part_ref), custom_call_target="tpu_custom_call" | custom-call | tf_op jit(solution)/shard_map/pallas_call | solution.py:82
  107.1 0.9 broadcast_multiply_fusion
  108.1 0.2 div.142
  108.3 0.2 bitcast_reduce_fusion
  108.6 0.4 fusion.24
  109.2 0.5 convolution_convert_fusion.1
  109.7 0.4 copy.89
  110.1 0.3 fusion.10
  110.4 0.7 fusion.83
  111.1 0.2 copy.96
  111.3 0.4 convolution_convert_fusion.3
  111.7 0.3 copy-done.10
  112.0 1.0 convolution_add_fusion.8
  113.0 1.9 %reshape.802 = f32[4,4,8,8,12,4]{3,2,5,4,1,0:T(8,128)S(1)} reshape(f32[16,64,48]{1,2,0:T(8,128)} %convolution_add_fusion.8) | data formatting | bytes 393216 | tf_op jit(solution)/shard_map/reshape | solution.py:400
  114.9 2.8 %copy.97 = f32[12,4,8,4,8,4]{2,1,5,4,3,0:T(4,128)} copy(f32[12,4,8,4,8,4]{4,2,5,0,3,1:T(8,128)S(1)} %bitcast.213) | data formatting | bytes 393216 | tf_op jit(solution)/shard_map/transpose | solution.py:402
  117.7 2.8 %reshape.803 = f32[3,4,32,128]{2,3,1,0:T(8,128)S(1)} reshape(f32[12,4,8,4,8,4]{2,1,5,4,3,0:T(4,128)} %copy.97) | data formatting | bytes 393216 | tf_op jit(solution)/shard_map/reshape | solution.py:403
  120.6 0.9 copy.98
  (60 shorter events, 2.1 us)
Async XLA Ops:
  0.0 109.2 %copy-start = (bf16[48,144]{1,0:T(8,128)(2,1)S(1)}, bf16[48,144]{1,0:T(8,128)(2,1)}, u32[]{:S(2)}) copy-start(bf16[48,144]{1,0:T(8,128)(2,1)} %param.19) | copy-start | bytes 41476
  4.7 1.0 copy-start.5
  4.9 1.0 copy-start.6
  5.0 1.2 %copy-start.7 = (bf16[2,180,360]{2,0,1:T(2,128)(2,1)S(1)}, bf16[2,180,360]{2,0,1:T(2,128)(2,1)}, u32[]{:S(2)}) copy-start(bf16[2,180,360]{2,0,1:T(2,128)(2,1)} %param.15) | copy-start | bytes 777604
  22.5 30.1 %copy-start.1 = (bf16[2,4,4,8,8,180]{5,4,2,3,1,0:T(8,128)(2,1)}, bf16[2,4,4,8,8,180]{5,4,2,3,1,0:T(8,128)(2,1)S(1)}, u32[]{:S(2)}) copy-start(bf16[2,4,4,8,8,180]{5,4,2,3,1,0:T(8,128)(2,1)S(1)} %copy.74) | copy-start | bytes 2211844
  23.6 15.9 %collective-permute-start = (bf16[2,4,32,181]{3,2,1,0:T(8,128)(2,1)}, bf16[2,4,32,181]{3,2,1,0:T(8,128)(2,1)S(1)}, u32[]{:S(2)}, u32[]{:S(2)}) collective-permute-start(bf16[2,4,32,181]{3,2,1,0:T(8,128)(2,1)} %get-tuple-element.7), channel_id=1, source_target_pairs={{0,8},{8,16},{16,24},{24,32},{32,40},{40,48},{48,56},{1,9},{9,17},... | collective-permute-start | bytes 278024 | tf_op jit(solution)/shard_map/ppermute | solution.py:30
  26.8 12.7 %collective-permute-start.1 = (bf16[2,4,32,181]{3,2,1,0:T(8,128)(2,1)}, bf16[2,4,32,181]{3,2,1,0:T(8,128)(2,1)}, u32[]{:S(2)}, u32[]{:S(2)}) collective-permute-start(bf16[2,4,32,181]{3,2,1,0:T(8,128)(2,1)} %get-tuple-element.8), channel_id=1, source_target_pairs={{8,0},{16,8},{24,16},{32,24},{40,32},{48,40},{56,48},{9,1},{17,9},... | collective-permute-start | bytes 278024 | tf_op jit(solution)/shard_map/ppermute | solution.py:32
  33.5 0.7 copy-start.11
  33.8 3.1 %copy-start.12 = (s32[9]{0:T(128)S(1)}, s32[9]{0:T(128)}, u32[]{:S(2)}) copy-start(s32[9]{0:T(128)} %get-tuple-element.37) | copy-start | bytes 112
  40.6 7.0 %collective-permute-start.2 = (bf16[2,40,4,181]{3,2,1,0:T(4,128)(2,1)S(1)}, bf16[2,40,4,181]{3,2,1,0:T(4,128)(2,1)S(1)}, u32[]{:S(2)}, u32[]{:S(2)}) collective-permute-start(bf16[2,40,4,181]{3,2,1,0:T(4,128)(2,1)S(1)} %get-tuple-element.5), channel_id=1, source_target_pairs={{0,1},{1,2},{2,3},{3,4},{4,5},{5,6},{6,7},{8,9},{9,10},{10,11},{11... | collective-permute-start | bytes 347528 | tf_op jit(solution)/shard_map/ppermute | solution.py:30
  45.3 7.3 %collective-permute-start.3 = (bf16[2,40,4,181]{3,2,1,0:T(4,128)(2,1)S(1)}, bf16[2,40,4,181]{3,2,1,0:T(4,128)(2,1)S(1)}, u32[]{:S(2)}, u32[]{:S(2)}) collective-permute-start(bf16[2,40,4,181]{3,2,1,0:T(4,128)(2,1)S(1)} %get-tuple-element.6), channel_id=1, source_target_pairs={{1,0},{2,1},{3,2},{4,3},{5,4},{6,5},{7,6},{9,8},{10,9},{11,10},{12... | collective-permute-start | bytes 347528 | tf_op jit(solution)/shard_map/ppermute | solution.py:32
  47.6 5.0 %copy-start.3 = (bf16[2,40,4,181]{3,2,1,0:T(4,128)(2,1)}, bf16[2,40,4,181]{3,2,1,0:T(4,128)(2,1)S(1)}, u32[]{:S(2)}) copy-start(bf16[2,40,4,181]{3,2,1,0:T(4,128)(2,1)S(1)} %collective-permute-done.2) | copy-start | bytes 347524
  52.6 0.7 copy-start.4
  88.8 1.0 copy-start.2
  108.6 1.5 %copy-start.8 = (pred[16,64,64]{1,2,0:T(8,128)(4,1)S(1)}, pred[16,64,64]{1,2,0:T(8,128)(4,1)}, u32[]{:S(2)}) copy-start(pred[16,64,64]{1,2,0:T(8,128)(4,1)} %broadcast_compare_fusion) | copy-start | bytes 196612
  108.6 1.5 %copy-start.9 = (f32[2,64,64]{1,2,0:T(8,128)S(1)}, f32[2,64,64]{1,2,0:T(8,128)}, u32[]{:S(2)}) copy-start(f32[2,64,64]{1,2,0:T(8,128)} %copy.93) | copy-start | bytes 98308
  111.3 0.7 copy-start.10

commit v5 on v4

--- a/solution.py
+++ b/solution.py
@@ -373,7 +373,7 @@
         features[None], labels, 0, qkv_weight, proj_weight, up_weight, down_weight, first_bias
     )
     tagged = jnp.broadcast_to(labels.astype(jnp.bfloat16)[None, :, :, None], block_one.shape[:3] + (1,))
-    carried = extended(jnp.concatenate([block_one, tagged], axis=-1), (("ty", 1), ("tx", 2)), SHIFT)
+    carried = extended(jnp.concatenate([block_one, tagged], axis=-1), (("tx", 2), ("ty", 1)), SHIFT)
     shifted = carried[..., :channels]
     region = carried[0, :, :, channels].astype(jnp.int32)
     block_two = block_on_grid(

time: 122 us -> 120 us (0.984)
  the two profiles are of different devices: /device:TPU:99 before, /device:TPU:153 now
where the time goes in v5:
time: 120 us; the launch traced here: 119 us
  Pallas kernels  54.9 us (46%)
  local copies, waits for them, and re-layouts  22.3 us (19%)
  matrix products  13.8 us (12%)
  starting transfers between devices  11.9 us (10%)
  other arithmetic  10.5 us (9%)
  waiting for transfers between devices  5.4 us (4%)
    pallas_call x2, Pallas kernels, swin_block(): pl.pallas_call(functools.partial(block_kernel, variants, heads, scale), o...  42.5 us
    pallas_call x1, Pallas kernels, var_sum(): pl.pallas_call(functools.partial(var_sum_kernel, count), out_shape=jax.Sh...  12.5 us
    ppermute x2, starting transfers between devices, extended(): lax.ppermute(head, axis, [((i + 1) % count, i) for i in range(ends)])  6.54 us
    ppermute x2, starting transfers between devices, extended(): lax.ppermute(tail, axis, [(i, (i + 1) % count) for i in range(ends)])  5.4 us
    ppermute x2, waiting for transfers between devices, extended(): lax.ppermute(head, axis, [((i + 1) % count, i) for i in range(ends)])  4.89 us
    dot_general x3, matrix products, bias_table(): jnp.einsum('vqkt,ht->vhqk', one_hot, parts, preferred_element_type=jnp.fl...  4.62 us
    unnamed x30, local copies, waits for them, and re-layouts  4.04 us
    dot_general x9, matrix products, reconstruct(): jnp.einsum('vrcd,vde->vrce', window, kernels[:, kernel_spot], preferred_e...  3.85 us
  transfers between devices with their start and end apart: 4, of which 2 were waited for; matrix products, arithmetic and copies ran while one was open for 7% of the time, Pallas kernels for 0%

profile of v5, /device:TPU:153, one launch (start us, length us, event | category | flops | bytes accessed | tf_op | source)
XLA Modules:
  0.0 119.4 jit_solution(1294178915706906153)
XLA Ops:
  0.0 0.8 reshape_broadcast_in_dim.9
  1.2 0.7 convert_element_type.59
  1.9 0.8 fusion.82
  2.9 1.8 %fusion.2 = f32[18,2,64,64]{3,0,2,1:T(8,128)S(1)} fusion(s32[2,64,64]{2,1,0:T(8,128)S(1)} %fusion.33, bf16[6,225]{1,0:T(8,128)(2,1)S(1)} %get-tuple-element.30, bf16[6,225]{1,0:T(8,128)(2,1)S(1)} %get-tuple-element.29, bf16[6,225]{1,0:T(8,128)(2,1)S(1)} %get-tuple-element.31), kind=kOutput, calls=%fused_computation.3 | convolution fusion | flops 68222704 | bytes 630692 | tf_op jit(solution)/shard_map/vqkt,ht->vhqk/dot_general | solution.py:257
  4.7 0.2 copy.151
  5.0 0.7 copy-done.5
  5.9 0.3 copy.73.wdown_ref
  6.3 0.9 copy.71.wp_ref
  7.2 1.1 copy.65
  8.3 14.1 %shard_map.109 = bf16[2,4,256,180]{3,2,1,0:T(8,128)(2,1)S(1)} custom-call(bf16[1,4,256,180]{3,2,1,0:T(8,128)(2,1)S(1)} %bitcast.208, s32[4,256,1]{2,1,0:T(8,128)S(1)} %reshape.822.labq_ref, s32[4,1,256]{2,1,0:T(1,128)S(1)} %reshape.787.labk_ref, f32[2,6,64,64]{3,2,1,0:T(8,128)S(1)} %slice_add_fusion.2.bias_ref, bf16[2,180,540]{2,1,0:T(8,128)(2,1)S(1)} %copy.70.wqkv_ref, ...), custom_call_target="tpu_custom_call" | custom-call | tf_op jit(solution)/shard_map/pallas_call | solution.py:186
  22.6 0.2 broadcast_in_dim.264
  22.8 1.0 pad_maximum_fusion.6
  23.7 2.6 %collective-permute-start = (bf16[2,32,4,181]{3,2,1,0:T(4,128)(2,1)}, bf16[2,32,4,181]{3,2,1,0:T(4,128)(2,1)S(1)}, u32[]{:S(2)}, u32[]{:S(2)}) collective-permute-start(bf16[2,32,4,181]{3,2,1,0:T(4,128)(2,1)} %get-tuple-element.7), channel_id=1, source_target_pairs={{0,1},{1,2},{2,3},{3,4},{4,5},{5,6},{6,7},{8,9},{9,10},{10,11},{11... | collective-permute-start | bytes 278024 | tf_op jit(solution)/shard_map/ppermute | solution.py:30
  26.4 3.9 %collective-permute-start.1 = (bf16[2,32,4,181]{3,2,1,0:T(4,128)(2,1)}, bf16[2,32,4,181]{3,2,1,0:T(4,128)(2,1)}, u32[]{:S(2)}, u32[]{:S(2)}) collective-permute-start(bf16[2,32,4,181]{3,2,1,0:T(4,128)(2,1)} %get-tuple-element.8), channel_id=1, source_target_pairs={{1,0},{2,1},{3,2},{4,3},{5,4},{6,5},{7,6},{9,8},{10,9},{11,10},{12... | collective-permute-start | bytes 278024 | tf_op jit(solution)/shard_map/ppermute | solution.py:32
  30.2 0.6 fusion.75
  30.9 1.8 %fusion.1 = f32[18,2,64,64]{3,0,2,1:T(8,128)S(1)} fusion(s32[2,64,64]{2,1,0:T(8,128)S(1)} %fusion.33, bf16[6,225]{1,0:T(8,128)(2,1)S(1)} %get-tuple-element.12, bf16[6,225]{1,0:T(8,128)(2,1)S(1)} %get-tuple-element.13, bf16[6,225]{1,0:T(8,128)(2,1)S(1)} %get-tuple-element.11), kind=kOutput, calls=%fused_computation.2 | convolution fusion | flops 68222704 | bytes 630692 | tf_op jit(solution)/shard_map/vqkt,ht->vhqk/dot_general | solution.py:257
  32.7 0.2 copy.150
  33.1 0.4 copy-done.11
  33.4 1.0 fusion.12
  34.5 0.7 copy.93
  35.2 0.9 broadcast_compare_fusion
  36.2 1.3 %convolution_convert_fusion = bf16[2,9,180,48]{2,1,3,0:T(8,128)(2,1)S(1)} fusion(bf16[9,180,48]{1,2,0:T(8,128)(2,1)} %param.18, s32[2,9]{1,0:T(2,128)S(1)} %fusion.61), kind=kOutput, calls=%fused_computation.11 | convolution fusion | flops 2955042 | bytes 466632 | tf_op jit(solution)/shard_map/vpq,qcs->vpcs/dot_general | solution.py:285
  37.6 1.1 convolution_convert_fusion.2
  38.7 0.9 pad_maximum_fusion.4
  39.7 2.8 %collective-permute-start.2 = (bf16[2,4,40,181]{3,2,1,0:T(8,128)(2,1)S(1)}, bf16[2,4,40,181]{3,2,1,0:T(8,128)(2,1)S(1)}, u32[]{:S(2)}, u32[]{:S(2)}) collective-permute-start(bf16[2,4,40,181]{3,2,1,0:T(8,128)(2,1)S(1)} %get-tuple-element.5), channel_id=1, source_target_pairs={{0,8},{8,16},{16,24},{24,32},{32,40},{40,48},{48,56},{1,9},{9,17},... | collective-permute-start | bytes 347528 | tf_op jit(solution)/shard_map/ppermute | solution.py:30
  42.5 2.7 %collective-permute-start.3 = (bf16[2,4,40,181]{3,2,1,0:T(8,128)(2,1)S(1)}, bf16[2,4,40,181]{3,2,1,0:T(8,128)(2,1)S(1)}, u32[]{:S(2)}, u32[]{:S(2)}) collective-permute-start(bf16[2,4,40,181]{3,2,1,0:T(8,128)(2,1)S(1)} %get-tuple-element.6), channel_id=1, source_target_pairs={{8,0},{16,8},{24,16},{32,24},{40,32},{48,40},{56,48},{9,1},{17,9},... | collective-permute-start | bytes 347528 | tf_op jit(solution)/shard_map/ppermute | solution.py:32
  45.3 0.5 collective-permute-done.2
  45.8 4.9 %collective-permute-done.3 = bf16[2,4,40,181]{3,2,1,0:T(8,128)(2,1)S(1)} collective-permute-done((bf16[2,4,40,181]{3,2,1,0:T(8,128)(2,1)S(1)}, bf16[2,4,40,181]{3,2,1,0:T(8,128)(2,1)S(1)}, u32[]{:S(2)}, u32[]{:S(2)}) %collective-permute-start.3) | collective-permute-done | bytes 115872 | tf_op jit(solution)/shard_map/ppermute | solution.py:32
  50.7 0.7 copy-done.4
  51.3 1.3 %maximum_reduce_fusion = bf16[40,40]{1,0:T(8,128)(2,1)S(1)} fusion(bf16[2,4,40,181]{3,2,1,0:T(8,128)(2,1)S(1)} %collective-permute-done.3, bf16[2,4,40,181]{3,2,1,0:T(8,128)(2,1)S(1)} %collective-permute-done.2, bf16[2,32,4,181]{3,2,1,0:T(4,128)(2,1)} %collective-permute-done.1, bf16[2,32,4,181]{3,2,1,0:T(4,128)(2,1)S(1)} %collective-permute-done, ...), kind=kLoop, calls=%fused_computation.50 | loop fusion | flops 19200 | bytes 1161600 | tf_op jit(solution)/shard_map/slice | solution.py:378
  52.8 0.9 reshape.823.labq_ref
  53.8 2.5 %pad_maximum_fusion = bf16[2,40,40,181]{3,2,1,0:T(8,128)(2,1)S(1)} fusion(bf16[2,4,40,181]{3,2,1,0:T(8,128)(2,1)} %copy-done.4, bf16[2,32,4,181]{3,2,1,0:T(4,128)(2,1)} %collective-permute-done.1, bf16[2,32,32,1]{3,2,1,0:T(8,128)(2,1)S(1)} %broadcast_in_dim.264, bf16[2,32,32,180]{3,2,1,0:T(8,128)(2,1)} %bitcast.212, ...), kind=kLoop, calls=%fused_computation.9 | loop fusion | flops 6950400 | bytes 2316800 | tf_op jit(solution)/shard_map/concatenate | solution.py:28
  56.3 0.2 copy.75
  56.5 1.7 %pad.11 = bf16[2,28,64,180]{3,2,1,0:T(8,128)(2,1)} pad(bf16[2,25,64,180]{3,2,1,0:T(8,128)(2,1)S(1)} %bitcast.216, bf16[]{:T(256)} %constant.302.clone.1), padding=0_0x0_3x0_0x0_0 | pad | bytes 2442242 | tf_op jit(solution)/shard_map/jit(_pad)/pad | solution.py:177
  58.1 28.3 %shard_map.110 = bf16[2,7,256,180]{3,2,1,0:T(8,128)(2,1)S(1)} custom-call(bf16[2,7,256,180]{3,2,1,0:T(8,128)(2,1)} %bitcast.214, s32[7,256,1]{2,1,0:T(8,128)S(1)} %reshape.823.labq_ref, s32[7,1,256]{2,1,0:T(1,128)S(1)} %reshape.793.labk_ref, f32[2,6,64,64]{3,2,1,0:T(8,128)S(1)} %slice_add_fusion.bias_ref, bf16[2,180,540]{2,1,0:T(8,128)(2,1)S(1)} %copy.70.wqkv_ref, ...), custom_call_target="tpu_custom_call" | custom-call | tf_op jit(solution)/shard_map/pallas_call | solution.py:186
  86.7 0.4 slice_select_fusion
  87.2 0.6 copy-done.2
  87.7 0.4 fusion.21
  88.1 0.4 convolution_add_fusion.7
  88.6 0.4 convolution_add_fusion.6
  89.0 0.4 convolution_add_fusion.5
  89.4 0.4 convolution_add_fusion.4
  89.9 0.4 convolution_add_fusion.3
  90.3 0.4 convolution_add_fusion.2
  90.7 0.4 convolution_add_fusion.1
  91.2 0.5 fusion.11
  91.6 1.0 convert_element_type.64.part_ref
  92.6 12.5 %shard_map.111 = f32[32,1536]{1,0:T(8,128)} custom-call(bf16[32,1536]{1,0:T(8,128)(2,1)} %convert_element_type.64.part_ref), custom_call_target="tpu_custom_call" | custom-call | tf_op jit(solution)/shard_map/pallas_call | solution.py:82
  105.1 0.9 broadcast_multiply_fusion
  106.0 0.2 div.142
  106.3 0.2 bitcast_reduce_fusion
  106.6 0.4 fusion.24
  107.2 0.5 convolution_convert_fusion.1
  107.6 0.4 copy.89
  108.0 0.3 fusion.10
  108.4 0.7 fusion.83
  109.0 0.2 copy.96
  109.2 0.4 convolution_convert_fusion.3
  109.7 0.3 copy-done.10
  110.0 1.0 convolution_add_fusion.8
  110.9 1.9 %reshape.802 = f32[4,4,8,8,12,4]{3,2,5,4,1,0:T(8,128)S(1)} reshape(f32[16,64,48]{1,2,0:T(8,128)} %convolution_add_fusion.8) | data formatting | bytes 393216 | tf_op jit(solution)/shard_map/reshape | solution.py:400
  112.8 2.8 %copy.97 = f32[12,4,8,4,8,4]{2,1,5,4,3,0:T(4,128)} copy(f32[12,4,8,4,8,4]{4,2,5,0,3,1:T(8,128)S(1)} %bitcast.213) | data formatting | bytes 393216 | tf_op jit(solution)/shard_map/transpose | solution.py:402
  115.7 2.8 %reshape.803 = f32[3,4,32,128]{2,3,1,0:T(8,128)S(1)} reshape(f32[12,4,8,4,8,4]{2,1,5,4,3,0:T(4,128)} %copy.97) | data formatting | bytes 393216 | tf_op jit(solution)/shard_map/reshape | solution.py:403
  118.5 0.9 copy.98
  (60 shorter events, 2.2 us)
Async XLA Ops:
  0.0 107.2 %copy-start = (bf16[48,144]{1,0:T(8,128)(2,1)S(1)}, bf16[48,144]{1,0:T(8,128)(2,1)}, u32[]{:S(2)}) copy-start(bf16[48,144]{1,0:T(8,128)(2,1)} %param.19) | copy-start | bytes 41476
  4.7 1.0 copy-start.5
  4.9 1.0 copy-start.6
  5.0 1.2 %copy-start.7 = (bf16[2,180,360]{2,0,1:T(2,128)(2,1)S(1)}, bf16[2,180,360]{2,0,1:T(2,128)(2,1)}, u32[]{:S(2)}) copy-start(bf16[2,180,360]{2,0,1:T(2,128)(2,1)} %param.15) | copy-start | bytes 777604
  22.5 28.1 %copy-start.1 = (bf16[2,4,4,8,8,180]{5,4,2,3,1,0:T(8,128)(2,1)}, bf16[2,4,4,8,8,180]{5,4,2,3,1,0:T(8,128)(2,1)S(1)}, u32[]{:S(2)}) copy-start(bf16[2,4,4,8,8,180]{5,4,2,3,1,0:T(8,128)(2,1)S(1)} %copy.74) | copy-start | bytes 2211844
  23.7 15.0 %collective-permute-start = (bf16[2,32,4,181]{3,2,1,0:T(4,128)(2,1)}, bf16[2,32,4,181]{3,2,1,0:T(4,128)(2,1)S(1)}, u32[]{:S(2)}, u32[]{:S(2)}) collective-permute-start(bf16[2,32,4,181]{3,2,1,0:T(4,128)(2,1)} %get-tuple-element.7), channel_id=1, source_target_pairs={{0,1},{1,2},{2,3},{3,4},{4,5},{5,6},{6,7},{8,9},{9,10},{10,11},{11... | collective-permute-start | bytes 278024 | tf_op jit(solution)/shard_map/ppermute | solution.py:30
  26.4 12.4 %collective-permute-start.1 = (bf16[2,32,4,181]{3,2,1,0:T(4,128)(2,1)}, bf16[2,32,4,181]{3,2,1,0:T(4,128)(2,1)}, u32[]{:S(2)}, u32[]{:S(2)}) collective-permute-start(bf16[2,32,4,181]{3,2,1,0:T(4,128)(2,1)} %get-tuple-element.8), channel_id=1, source_target_pairs={{1,0},{2,1},{3,2},{4,3},{5,4},{6,5},{7,6},{9,8},{10,9},{11,10},{12... | collective-permute-start | bytes 278024 | tf_op jit(solution)/shard_map/ppermute | solution.py:32
  32.7 0.7 copy-start.11
  33.0 3.1 %copy-start.12 = (s32[9]{0:T(128)S(1)}, s32[9]{0:T(128)}, u32[]{:S(2)}) copy-start(s32[9]{0:T(128)} %get-tuple-element.37) | copy-start | bytes 112
  39.7 6.1 %collective-permute-start.2 = (bf16[2,4,40,181]{3,2,1,0:T(8,128)(2,1)S(1)}, bf16[2,4,40,181]{3,2,1,0:T(8,128)(2,1)S(1)}, u32[]{:S(2)}, u32[]{:S(2)}) collective-permute-start(bf16[2,4,40,181]{3,2,1,0:T(8,128)(2,1)S(1)} %get-tuple-element.5), channel_id=1, source_target_pairs={{0,8},{8,16},{16,24},{24,32},{32,40},{40,48},{48,56},{1,9},{9,17},... | collective-permute-start | bytes 347528 | tf_op jit(solution)/shard_map/ppermute | solution.py:30
  42.5 8.2 %collective-permute-start.3 = (bf16[2,4,40,181]{3,2,1,0:T(8,128)(2,1)S(1)}, bf16[2,4,40,181]{3,2,1,0:T(8,128)(2,1)S(1)}, u32[]{:S(2)}, u32[]{:S(2)}) collective-permute-start(bf16[2,4,40,181]{3,2,1,0:T(8,128)(2,1)S(1)} %get-tuple-element.6), channel_id=1, source_target_pairs={{8,0},{16,8},{24,16},{32,24},{40,32},{48,40},{56,48},{9,1},{17,9},... | collective-permute-start | bytes 347528 | tf_op jit(solution)/shard_map/ppermute | solution.py:32
  45.8 4.9 %copy-start.3 = (bf16[2,4,40,181]{3,2,1,0:T(8,128)(2,1)}, bf16[2,4,40,181]{3,2,1,0:T(8,128)(2,1)S(1)}, u32[]{:S(2)}) copy-start(bf16[2,4,40,181]{3,2,1,0:T(8,128)(2,1)S(1)} %collective-permute-done.2) | copy-start | bytes 347524
  50.7 0.7 copy-start.4
  86.7 1.0 copy-start.2
  106.5 1.5 %copy-start.8 = (pred[16,64,64]{1,2,0:T(8,128)(4,1)S(1)}, pred[16,64,64]{1,2,0:T(8,128)(4,1)}, u32[]{:S(2)}) copy-start(pred[16,64,64]{1,2,0:T(8,128)(4,1)} %broadcast_compare_fusion) | copy-start | bytes 196612
  106.6 1.5 %copy-start.9 = (f32[2,64,64]{1,2,0:T(8,128)S(1)}, f32[2,64,64]{1,2,0:T(8,128)}, u32[]{:S(2)}) copy-start(f32[2,64,64]{1,2,0:T(8,128)} %copy.93) | copy-start | bytes 98308
  109.2 0.7 copy-start.10

commit v6 on v5

--- a/solution.py
+++ b/solution.py
@@ -105,7 +105,7 @@
     def _():
         for variant in range(variants):
             for head in range(heads):
-                wide_ref[variant, head] = jnp.concatenate([bias_ref[variant, head]] * GROUP, axis=1)
+                wide_ref[variant, head] = jnp.concatenate([bias_ref[variant, head]] * (wide_ref.shape[-1] // (WIN * WIN)), axis=1)
 
     inputs = x_ref.shape[0]
     tokens = x_ref.shape[2]
@@ -139,7 +139,7 @@
                 preferred_element_type=jnp.float32,
             )
             scores = scores * scale
-            scores = (scores.reshape(GROUP, WIN * WIN, tokens) + wide_ref[variant, head][None]).reshape(
+            scores = (scores.reshape(tokens // (WIN * WIN), WIN * WIN, tokens) + wide_ref[variant, head][None]).reshape(
                 tokens, tokens
             )
             scores = jnp.where(match, scores, MASKED)
@@ -172,11 +172,12 @@
 def swin_block(windows, region, layer, w_qkv, w_proj, w_up, w_down, bias_grid):
     inputs, count, cells, channels = windows.shape
     variants, heads = bias_grid.shape[:2]
-    groups = -(-count // GROUP)
-    extra = groups * GROUP - count
+    size = 5 if count % GROUP and count % 5 == 0 else GROUP
+    groups = -(-count // size)
+    extra = groups * size - count
     windows = jnp.pad(windows, ((0, 0), (0, extra), (0, 0), (0, 0)))
     region = jnp.pad(region, ((0, extra), (0, 0)))
-    tokens = GROUP * cells
+    tokens = size * cells
     x = windows.reshape(inputs, groups, tokens, channels)
     labq = region.reshape(groups, tokens, 1)
     labk = region.reshape(groups, 1, tokens)
@@ -201,7 +202,7 @@
         scratch_shapes=[pltpu.VMEM((variants, heads, cells, tokens), jnp.float32)],
         compiler_params=pltpu.CompilerParams(vmem_limit_bytes=48 * 1024 * 1024),
     )(x, labq, labk, bias, w_qkv, w_proj, w_up, w_down)
-    out = out.reshape(variants, groups * GROUP, cells, channels)
+    out = out.reshape(variants, groups * size, cells, channels)
     return out[:, :count]
 
 

time: 120 us -> 120 us (level)
    transpose x0 -> x1, other arithmetic: none -> 1.78 us  [to_windows(): grid = grid.transpose(0, 1, 3, 2, 4, 5)]
    pad x1 -> x0, local copies, waits for them, and re-layouts: 1.65 us -> none  [swin_block(): windows = jnp.pad(windows, ((0, 0), (0, extra), (0, 0), (0, 0)))]
    slice x1 -> x0, other arithmetic: 1.28 us -> none  [local(): region = carried[0, :, :, channels].astype(jnp.int32)]
    unnamed x30 -> x32, local copies, waits for them, and re-layouts: 4.04 us -> 4.04 us
where the time goes in v6:
time: 120 us; the launch traced here: 119 us
  Pallas kernels  54.7 us (46%)
  local copies, waits for them, and re-layouts  21.4 us (18%)
  matrix products  13.8 us (12%)
  starting transfers between devices  11.9 us (10%)
  other arithmetic  11 us (9%)
  waiting for transfers between devices  5.4 us (4%)
    pallas_call x2, Pallas kernels, swin_block(): pl.pallas_call(functools.partial(block_kernel, variants, heads, scale), o...  42 us
    pallas_call x1, Pallas kernels, var_sum(): pl.pallas_call(functools.partial(var_sum_kernel, count), out_shape=jax.Sh...  12.7 us
    ppermute x2, starting transfers between devices, extended(): lax.ppermute(head, axis, [((i + 1) % count, i) for i in range(ends)])  6.54 us
    ppermute x2, starting transfers between devices, extended(): lax.ppermute(tail, axis, [(i, (i + 1) % count) for i in range(ends)])  5.41 us
    ppermute x2, waiting for transfers between devices, extended(): lax.ppermute(head, axis, [((i + 1) % count, i) for i in range(ends)])  4.89 us
    dot_general x3, matrix products, bias_table(): jnp.einsum('vqkt,ht->vhqk', one_hot, parts, preferred_element_type=jnp.fl...  4.62 us
    unnamed x32, local copies, waits for them, and re-layouts  4.04 us
    dot_general x9, matrix products, reconstruct(): jnp.einsum('vrcd,vde->vrce', window, kernels[:, kernel_spot], preferred_e...  3.84 us
  transfers between devices with their start and end apart: 4, of which 2 were waited for; matrix products, arithmetic and copies ran while one was open for 7% of the time, Pallas kernels for 0%

profile of v6, /device:TPU:153, one launch (start us, length us, event | category | flops | bytes accessed | tf_op | source)
XLA Modules:
  0.0 118.8 jit_solution(16598924505819360755)
XLA Ops:
  0.0 0.8 reshape_broadcast_in_dim.9
  1.2 0.7 convert_element_type.57
  1.9 0.8 fusion.82
  2.9 1.8 %fusion.2 = f32[18,2,64,64]{3,0,2,1:T(8,128)S(1)} fusion(s32[2,64,64]{2,1,0:T(8,128)S(1)} %fusion.33, bf16[6,225]{1,0:T(8,128)(2,1)S(1)} %get-tuple-element.30, bf16[6,225]{1,0:T(8,128)(2,1)S(1)} %get-tuple-element.29, bf16[6,225]{1,0:T(8,128)(2,1)S(1)} %get-tuple-element.31), kind=kOutput, calls=%fused_computation.3 | convolution fusion | flops 68222704 | bytes 630692 | tf_op jit(solution)/shard_map/vqkt,ht->vhqk/dot_general | solution.py:258
  4.7 0.2 copy.155
  5.0 0.7 copy-done.6
  5.9 0.3 copy.76.wdown_ref
  6.3 0.9 copy.74.wp_ref
  7.2 1.1 copy.68
  8.3 14.1 %shard_map.109 = bf16[2,4,256,180]{3,2,1,0:T(8,128)(2,1)S(1)} custom-call(bf16[1,4,256,180]{3,2,1,0:T(8,128)(2,1)S(1)} %bitcast.211, s32[4,256,1]{2,1,0:T(8,128)S(1)} %reshape.815.labq_ref, s32[4,1,256]{2,1,0:T(1,128)S(1)} %reshape.782.labk_ref, f32[2,6,64,64]{3,2,1,0:T(8,128)S(1)} %slice_add_fusion.2.bias_ref, bf16[2,180,540]{2,1,0:T(8,128)(2,1)S(1)} %copy.73.wqkv_ref, ...), custom_call_target="tpu_custom_call" | custom-call | tf_op jit(solution)/shard_map/pallas_call | solution.py:187
  22.6 0.2 broadcast_in_dim.264
  22.8 0.9 pad_maximum_fusion.6
  23.7 2.6 %collective-permute-start = (bf16[2,32,4,181]{3,2,1,0:T(4,128)(2,1)}, bf16[2,32,4,181]{3,2,1,0:T(4,128)(2,1)S(1)}, u32[]{:S(2)}, u32[]{:S(2)}) collective-permute-start(bf16[2,32,4,181]{3,2,1,0:T(4,128)(2,1)} %get-tuple-element.7), channel_id=1, source_target_pairs={{0,1},{1,2},{2,3},{3,4},{4,5},{5,6},{6,7},{8,9},{9,10},{10,11},{11... | collective-permute-start | bytes 278024 | tf_op jit(solution)/shard_map/ppermute | solution.py:30
  26.3 3.9 %collective-permute-start.1 = (bf16[2,32,4,181]{3,2,1,0:T(4,128)(2,1)}, bf16[2,32,4,181]{3,2,1,0:T(4,128)(2,1)}, u32[]{:S(2)}, u32[]{:S(2)}) collective-permute-start(bf16[2,32,4,181]{3,2,1,0:T(4,128)(2,1)} %get-tuple-element.8), channel_id=1, source_target_pairs={{1,0},{2,1},{3,2},{4,3},{5,4},{6,5},{7,6},{9,8},{10,9},{11,10},{12... | collective-permute-start | bytes 278024 | tf_op jit(solution)/shard_map/ppermute | solution.py:32
  30.2 0.6 fusion.75
  30.9 1.8 %fusion.1 = f32[18,2,64,64]{3,0,2,1:T(8,128)S(1)} fusion(s32[2,64,64]{2,1,0:T(8,128)S(1)} %fusion.33, bf16[6,225]{1,0:T(8,128)(2,1)S(1)} %get-tuple-element.12, bf16[6,225]{1,0:T(8,128)(2,1)S(1)} %get-tuple-element.13, bf16[6,225]{1,0:T(8,128)(2,1)S(1)} %get-tuple-element.11), kind=kOutput, calls=%fused_computation.2 | convolution fusion | flops 68222704 | bytes 630692 | tf_op jit(solution)/shard_map/vqkt,ht->vhqk/dot_general | solution.py:258
  32.7 0.2 copy.154
  33.1 0.4 copy-done.12
  33.4 1.0 fusion.12
  34.5 0.7 copy.97
  35.2 0.8 broadcast_compare_fusion
  36.2 1.3 %convolution_convert_fusion = bf16[2,9,180,48]{2,1,3,0:T(8,128)(2,1)S(1)} fusion(bf16[9,180,48]{1,2,0:T(8,128)(2,1)} %param.18, s32[2,9]{1,0:T(2,128)S(1)} %fusion.61), kind=kOutput, calls=%fused_computation.11 | convolution fusion | flops 2955042 | bytes 466632 | tf_op jit(solution)/shard_map/vpq,qcs->vpcs/dot_general | solution.py:286
  37.6 1.1 convolution_convert_fusion.2
  38.7 0.9 pad_maximum_fusion.4
  39.7 2.8 %collective-permute-start.2 = (bf16[2,4,40,181]{3,2,1,0:T(8,128)(2,1)S(1)}, bf16[2,4,40,181]{3,2,1,0:T(8,128)(2,1)S(1)}, u32[]{:S(2)}, u32[]{:S(2)}) collective-permute-start(bf16[2,4,40,181]{3,2,1,0:T(8,128)(2,1)S(1)} %get-tuple-element.5), channel_id=1, source_target_pairs={{0,8},{8,16},{16,24},{24,32},{32,40},{40,48},{48,56},{1,9},{9,17},... | collective-permute-start | bytes 347528 | tf_op jit(solution)/shard_map/ppermute | solution.py:30
  42.5 2.7 %collective-permute-start.3 = (bf16[2,4,40,181]{3,2,1,0:T(8,128)(2,1)S(1)}, bf16[2,4,40,181]{3,2,1,0:T(8,128)(2,1)S(1)}, u32[]{:S(2)}, u32[]{:S(2)}) collective-permute-start(bf16[2,4,40,181]{3,2,1,0:T(8,128)(2,1)S(1)} %get-tuple-element.6), channel_id=1, source_target_pairs={{8,0},{16,8},{24,16},{32,24},{40,32},{48,40},{56,48},{9,1},{17,9},... | collective-permute-start | bytes 347528 | tf_op jit(solution)/shard_map/ppermute | solution.py:32
  45.2 0.5 collective-permute-done.2
  45.7 4.9 %collective-permute-done.3 = bf16[2,4,40,181]{3,2,1,0:T(8,128)(2,1)S(1)} collective-permute-done((bf16[2,4,40,181]{3,2,1,0:T(8,128)(2,1)S(1)}, bf16[2,4,40,181]{3,2,1,0:T(8,128)(2,1)S(1)}, u32[]{:S(2)}, u32[]{:S(2)}) %collective-permute-start.3) | collective-permute-done | bytes 115872 | tf_op jit(solution)/shard_map/ppermute | solution.py:32
  50.6 0.7 copy-done.5
  51.3 1.8 %convert_reduce_fusion = s32[40,40]{1,0:T(8,128)S(1)} fusion(bf16[2,4,40,181]{3,2,1,0:T(8,128)(2,1)S(1)} %collective-permute-done.3, bf16[2,4,40,181]{3,2,1,0:T(8,128)(2,1)S(1)} %collective-permute-done.2, bf16[2,32,4,181]{3,2,1,0:T(4,128)(2,1)} %collective-permute-done.1, bf16[2,32,4,181]{3,2,1,0:T(4,128)(2,1)S(1)} %collective-permute-done, ...), kind=kLoop, calls=%fused_computation.44 | loop fusion | flops 19200 | bytes 1164800 | tf_op jit(solution)/shard_map/transpose | solution.py:228
  53.2 0.7 copy.80
  53.9 0.3 reshape.816.labq_ref
  54.1 1.0 reshape.787.labk_ref
  55.1 2.4 %pad_maximum_fusion = bf16[2,40,40,181]{3,2,1,0:T(8,128)(2,1)S(1)} fusion(bf16[2,4,40,181]{3,2,1,0:T(8,128)(2,1)} %copy-done.5, bf16[2,32,4,181]{3,2,1,0:T(4,128)(2,1)} %collective-permute-done.1, bf16[2,32,32,1]{3,2,1,0:T(8,128)(2,1)S(1)} %broadcast_in_dim.264, bf16[2,32,32,180]{3,2,1,0:T(8,128)(2,1)} %bitcast.215, ...), kind=kLoop, calls=%fused_computation.9 | loop fusion | flops 6950400 | bytes 2316800 | tf_op jit(solution)/shard_map/concatenate | solution.py:28
  57.8 27.9 %shard_map.110 = bf16[2,5,320,180]{3,2,1,0:T(8,128)(2,1)S(1)} custom-call(bf16[2,5,320,180]{3,2,1,0:T(8,128)(2,1)S(1)} %bitcast.208, s32[5,320,1]{2,1,0:T(8,128)S(1)} %reshape.816.labq_ref, s32[5,1,320]{2,1,0:T(1,128)S(1)} %reshape.787.labk_ref, f32[2,6,64,64]{3,2,1,0:T(8,128)S(1)} %slice_add_fusion.bias_ref, bf16[2,180,540]{2,1,0:T(8,128)(2,1)S(1)} %copy.73.wqkv_ref, ...), custom_call_target="tpu_custom_call" | custom-call | tf_op jit(solution)/shard_map/pallas_call | solution.py:187
  85.9 0.4 slice_select_fusion
  86.3 0.6 copy-done.2
  86.9 0.4 fusion.21
  87.3 0.4 convolution_add_fusion.7
  87.7 0.4 convolution_add_fusion.6
  88.2 0.4 convolution_add_fusion.5
  88.6 0.4 convolution_add_fusion.4
  89.0 0.4 convolution_add_fusion.3
  89.4 0.4 convolution_add_fusion.2
  89.9 0.4 convolution_add_fusion.1
  90.3 0.5 fusion.11
  90.8 1.0 convert_element_type.62.part_ref
  91.7 12.7 %shard_map.111 = f32[32,1536]{1,0:T(8,128)} custom-call(bf16[32,1536]{1,0:T(8,128)(2,1)} %convert_element_type.62.part_ref), custom_call_target="tpu_custom_call" | custom-call | tf_op jit(solution)/shard_map/pallas_call | solution.py:82
  104.4 0.9 broadcast_multiply_fusion
  105.4 0.2 div.142
  105.6 0.2 bitcast_reduce_fusion
  105.9 0.4 fusion.24
  106.5 0.5 convolution_convert_fusion.1
  107.0 0.4 copy.93
  107.4 0.3 fusion.10
  107.7 0.7 fusion.83
  108.4 0.2 copy.100
  108.6 0.4 convolution_convert_fusion.3
  109.0 0.3 copy-done.11
  109.3 1.0 convolution_add_fusion.8
  110.3 1.9 %reshape.794 = f32[4,4,8,8,12,4]{3,2,5,4,1,0:T(8,128)S(1)} reshape(f32[16,64,48]{1,2,0:T(8,128)} %convolution_add_fusion.8) | data formatting | bytes 393216 | tf_op jit(solution)/shard_map/reshape | solution.py:401
  112.2 2.9 %copy.101 = f32[12,4,8,4,8,4]{2,1,5,4,3,0:T(4,128)} copy(f32[12,4,8,4,8,4]{4,2,5,0,3,1:T(8,128)S(1)} %bitcast.216) | data formatting | bytes 393216 | tf_op jit(solution)/shard_map/transpose | solution.py:403
  115.1 2.8 %reshape.795 = f32[3,4,32,128]{2,3,1,0:T(8,128)S(1)} reshape(f32[12,4,8,4,8,4]{2,1,5,4,3,0:T(4,128)} %copy.101) | data formatting | bytes 393216 | tf_op jit(solution)/shard_map/reshape | solution.py:404
  117.9 0.9 copy.102
  (59 shorter events, 2.1 us)
Async XLA Ops:
  0.0 106.5 %copy-start = (bf16[48,144]{1,0:T(8,128)(2,1)S(1)}, bf16[48,144]{1,0:T(8,128)(2,1)}, u32[]{:S(2)}) copy-start(bf16[48,144]{1,0:T(8,128)(2,1)} %param.19) | copy-start | bytes 41476
  4.7 1.0 copy-start.6
  4.9 1.0 copy-start.7
  5.0 1.2 %copy-start.8 = (bf16[2,180,360]{2,0,1:T(2,128)(2,1)S(1)}, bf16[2,180,360]{2,0,1:T(2,128)(2,1)}, u32[]{:S(2)}) copy-start(bf16[2,180,360]{2,0,1:T(2,128)(2,1)} %param.15) | copy-start | bytes 777604
  22.5 28.1 %copy-start.1 = (bf16[2,4,4,8,8,180]{5,4,2,3,1,0:T(8,128)(2,1)}, bf16[2,4,4,8,8,180]{5,4,2,3,1,0:T(8,128)(2,1)S(1)}, u32[]{:S(2)}) copy-start(bf16[2,4,4,8,8,180]{5,4,2,3,1,0:T(8,128)(2,1)S(1)} %copy.77) | copy-start | bytes 2211844
  23.7 15.0 %collective-permute-start = (bf16[2,32,4,181]{3,2,1,0:T(4,128)(2,1)}, bf16[2,32,4,181]{3,2,1,0:T(4,128)(2,1)S(1)}, u32[]{:S(2)}, u32[]{:S(2)}) collective-permute-start(bf16[2,32,4,181]{3,2,1,0:T(4,128)(2,1)} %get-tuple-element.7), channel_id=1, source_target_pairs={{0,1},{1,2},{2,3},{3,4},{4,5},{5,6},{6,7},{8,9},{9,10},{10,11},{11... | collective-permute-start | bytes 278024 | tf_op jit(solution)/shard_map/ppermute | solution.py:30
  26.3 12.4 %collective-permute-start.1 = (bf16[2,32,4,181]{3,2,1,0:T(4,128)(2,1)}, bf16[2,32,4,181]{3,2,1,0:T(4,128)(2,1)}, u32[]{:S(2)}, u32[]{:S(2)}) collective-permute-start(bf16[2,32,4,181]{3,2,1,0:T(4,128)(2,1)} %get-tuple-element.8), channel_id=1, source_target_pairs={{1,0},{2,1},{3,2},{4,3},{5,4},{6,5},{7,6},{9,8},{10,9},{11,10},{12... | collective-permute-start | bytes 278024 | tf_op jit(solution)/shard_map/ppermute | solution.py:32
  32.7 0.7 copy-start.12
  33.0 3.1 %copy-start.13 = (s32[9]{0:T(128)S(1)}, s32[9]{0:T(128)}, u32[]{:S(2)}) copy-start(s32[9]{0:T(128)} %get-tuple-element.37) | copy-start | bytes 112
  39.7 6.1 %collective-permute-start.2 = (bf16[2,4,40,181]{3,2,1,0:T(8,128)(2,1)S(1)}, bf16[2,4,40,181]{3,2,1,0:T(8,128)(2,1)S(1)}, u32[]{:S(2)}, u32[]{:S(2)}) collective-permute-start(bf16[2,4,40,181]{3,2,1,0:T(8,128)(2,1)S(1)} %get-tuple-element.5), channel_id=1, source_target_pairs={{0,8},{8,16},{16,24},{24,32},{32,40},{40,48},{48,56},{1,9},{9,17},... | collective-permute-start | bytes 347528 | tf_op jit(solution)/shard_map/ppermute | solution.py:30
  42.5 8.2 %collective-permute-start.3 = (bf16[2,4,40,181]{3,2,1,0:T(8,128)(2,1)S(1)}, bf16[2,4,40,181]{3,2,1,0:T(8,128)(2,1)S(1)}, u32[]{:S(2)}, u32[]{:S(2)}) collective-permute-start(bf16[2,4,40,181]{3,2,1,0:T(8,128)(2,1)S(1)} %get-tuple-element.6), channel_id=1, source_target_pairs={{8,0},{16,8},{24,16},{32,24},{40,32},{48,40},{56,48},{9,1},{17,9},... | collective-permute-start | bytes 347528 | tf_op jit(solution)/shard_map/ppermute | solution.py:32
  45.7 4.9 %copy-start.3 = (bf16[2,4,40,181]{3,2,1,0:T(8,128)(2,1)}, bf16[2,4,40,181]{3,2,1,0:T(8,128)(2,1)S(1)}, u32[]{:S(2)}) copy-start(bf16[2,4,40,181]{3,2,1,0:T(8,128)(2,1)S(1)} %collective-permute-done.2) | copy-start | bytes 347524
  50.6 0.7 copy-start.5
  53.1 2.1 %copy-start.4 = (bf16[2,4,40,181]{3,2,1,0:T(8,128)(2,1)S(1)}, bf16[2,4,40,181]{3,2,1,0:T(8,128)(2,1)}, u32[]{:S(2)}) copy-start(bf16[2,4,40,181]{3,2,1,0:T(8,128)(2,1)} %copy-done.3) | copy-start | bytes 347524
  85.9 1.0 copy-start.2
  105.9 1.5 %copy-start.9 = (pred[16,64,64]{1,2,0:T(8,128)(4,1)S(1)}, pred[16,64,64]{1,2,0:T(8,128)(4,1)}, u32[]{:S(2)}) copy-start(pred[16,64,64]{1,2,0:T(8,128)(4,1)} %broadcast_compare_fusion) | copy-start | bytes 196612
  105.9 1.5 %copy-start.10 = (f32[2,64,64]{1,2,0:T(8,128)S(1)}, f32[2,64,64]{1,2,0:T(8,128)}, u32[]{:S(2)}) copy-start(f32[2,64,64]{1,2,0:T(8,128)} %copy.97) | copy-start | bytes 98308
  108.6 0.7 copy-start.11

commit v7 on v6

--- a/solution.py
+++ b/solution.py
@@ -214,6 +214,28 @@
     return from_windows(out, height, breadth)
 
 
+def halo(cells, width):
+    rows_of, cols_of = lax.axis_size("ty"), lax.axis_size("tx")
+    height, breadth = cells.shape[1], cells.shape[2]
+    rows = {-1: slice(height - width, height), 0: slice(0, height), 1: slice(0, width)}
+    cols = {-1: slice(breadth - width, breadth), 0: slice(0, breadth), 1: slice(0, width)}
+    pieces = {}
+    for dy in (-1, 0, 1):
+        for dx in (-1, 0, 1):
+            if dy == 0 and dx == 0:
+                pieces[(dy, dx)] = cells
+                continue
+            pairs = [
+                ((y + dy) * cols_of + x + dx, y * cols_of + x)
+                for y in range(rows_of)
+                for x in range(cols_of)
+                if 0 <= y + dy < rows_of and 0 <= x + dx < cols_of
+            ]
+            pieces[(dy, dx)] = lax.ppermute(cells[:, rows[dy], cols[dx]], ("ty", "tx"), pairs)
+    bands = [jnp.concatenate([pieces[(dy, dx)] for dx in (-1, 0, 1)], axis=2) for dy in (-1, 0, 1)]
+    return jnp.concatenate(bands, axis=1)
+
+
 def normalize(values):
     values = values.astype(jnp.float32)
     average = jnp.mean(values, axis=-1, keepdims=True)
@@ -374,7 +396,7 @@
         features[None], labels, 0, qkv_weight, proj_weight, up_weight, down_weight, first_bias
     )
     tagged = jnp.broadcast_to(labels.astype(jnp.bfloat16)[None, :, :, None], block_one.shape[:3] + (1,))
-    carried = extended(jnp.concatenate([block_one, tagged], axis=-1), (("tx", 2), ("ty", 1)), SHIFT)
+    carried = halo(jnp.concatenate([block_one, tagged], axis=-1), SHIFT)
     shifted = carried[..., :channels]
     region = carried[0, :, :, channels].astype(jnp.int32)
     block_two = block_on_grid(

time: 120 us -> 143 us (1.19)
  the two profiles are of different devices: /device:TPU:153 before, /device:TPU:99 now
where the time goes in v7:
time: 143 us; the launch traced here: 140 us
  Pallas kernels  55.3 us (39%)
  starting transfers between devices  31.3 us (22%)
  local copies, waits for them, and re-layouts  21.6 us (15%)
  other arithmetic  17.5 us (12%)
  matrix products  12.9 us (9%)
    pallas_call x2, Pallas kernels, swin_block(): pl.pallas_call(functools.partial(block_kernel, variants, heads, scale), o...  42 us
    ppermute x8, starting transfers between devices, halo(): lax.ppermute(cells[:, rows[dy], cols[dx]], ('ty', 'tx'), pairs)  31.3 us
    pallas_call x1, Pallas kernels, var_sum(): pl.pallas_call(functools.partial(var_sum_kernel, count), out_shape=jax.Sh...  13.3 us
    dot_general x3, matrix products, bias_table(): jnp.einsum('vqkt,ht->vhqk', one_hot, parts, preferred_element_type=jnp.fl...  5.38 us
    transpose x1, local copies, waits for them, and re-layouts, local(): picture = refined.reshape(height // WIN, breadth // WIN, WIN, WIN, colour...  4.96 us
    dot_general x9, matrix products, reconstruct(): jnp.einsum('vrcd,vde->vrce', window, kernels[:, kernel_spot], preferred_e...  3.86 us
    unnamed x28, local copies, waits for them, and re-layouts  3.85 us
  transfers between devices with their start and end apart: 8, of which 1 were waited for; matrix products, arithmetic and copies ran while one was open for 11% of the time, Pallas kernels for 0%

profile of v7, /device:TPU:99, one launch (start us, length us, event | category | flops | bytes accessed | tf_op | source)
XLA Modules:
  0.0 140.2 jit_solution(11658988344355767219)
XLA Ops:
  0.1 0.8 reshape_broadcast_in_dim.9
  1.2 0.7 convert_element_type.57
  1.9 0.8 fusion.82
  2.7 0.7 add_add_fusion
  3.5 1.8 %fusion.2 = f32[18,2,64,64]{3,0,2,1:T(8,128)S(1)} fusion(s32[2,64,64]{2,1,0:T(8,128)S(1)} %fusion.33, bf16[6,225]{1,0:T(8,128)(2,1)S(1)} %get-tuple-element.34, bf16[6,225]{1,0:T(8,128)(2,1)S(1)} %get-tuple-element.33, bf16[6,225]{1,0:T(8,128)(2,1)S(1)} %get-tuple-element.35), kind=kOutput, calls=%fused_computation.3 | convolution fusion | flops 68222704 | bytes 630692 | tf_op jit(solution)/shard_map/vqkt,ht->vhqk/dot_general | solution.py:280
  5.7 0.7 copy-done.5
  6.4 1.2 copy.76.wdown_ref
  7.6 1.0 copy.75.wup_ref
  8.7 14.1 %shard_map.109 = bf16[2,4,256,180]{3,2,1,0:T(8,128)(2,1)S(1)} custom-call(bf16[1,4,256,180]{3,2,1,0:T(8,128)(2,1)S(1)} %bitcast.211, s32[4,256,1]{2,1,0:T(8,128)S(1)} %reshape.815.labq_ref, s32[4,1,256]{2,1,0:T(1,128)S(1)} %reshape.782.labk_ref, f32[2,6,64,64]{3,2,1,0:T(8,128)S(1)} %slice_add_fusion.2.bias_ref, bf16[2,180,540]{2,1,0:T(8,128)(2,1)S(1)} %copy.73.wqkv_ref, ...), custom_call_target="tpu_custom_call" | custom-call | tf_op jit(solution)/shard_map/pallas_call | solution.py:187
  23.2 0.8 pad_maximum_fusion.7
  24.0 5.8 %collective-permute-start = (bf16[2,4,4,181]{3,2,1,0:T(4,128)(2,1)}, bf16[2,4,4,181]{3,2,1,0:T(4,128)(2,1)S(1)}, u32[]{:S(2)}, u32[]{:S(2)}) collective-permute-start(bf16[2,4,4,181]{3,2,1,0:T(4,128)(2,1)} %get-tuple-element.5), channel_id=1, source_target_pairs={{0,9},{1,10},{2,11},{3,12},{4,13},{5,14},{6,15},{8,17},{9,18},{10,... | collective-permute-start | bytes 34760 | tf_op jit(solution)/shard_map/ppermute | solution.py:234
  29.7 1.9 %collective-permute-start.2 = (bf16[2,4,4,181]{3,2,1,0:T(4,128)(2,1)}, bf16[2,4,4,181]{3,2,1,0:T(4,128)(2,1)}, u32[]{:S(2)}, u32[]{:S(2)}) collective-permute-start(bf16[2,4,4,181]{3,2,1,0:T(4,128)(2,1)} %get-tuple-element.8), channel_id=1, source_target_pairs={{1,8},{2,9},{3,10},{4,11},{5,12},{6,13},{7,14},{9,16},{10,17},{11,... | collective-permute-start | bytes 34760 | tf_op jit(solution)/shard_map/ppermute | solution.py:234
  31.7 7.6 %collective-permute-start.5 = (bf16[2,4,4,181]{3,2,1,0:T(4,128)(2,1)}, bf16[2,4,4,181]{3,2,1,0:T(4,128)(2,1)}, u32[]{:S(2)}, u32[]{:S(2)}) collective-permute-start(bf16[2,4,4,181]{3,2,1,0:T(4,128)(2,1)} %get-tuple-element.7), channel_id=1, source_target_pairs={{8,1},{9,2},{10,3},{11,4},{12,5},{13,6},{14,7},{16,9},{17,10},{18,... | collective-permute-start | bytes 34760 | tf_op jit(solution)/shard_map/ppermute | solution.py:234
  39.3 2.1 %collective-permute-start.7 = (bf16[2,4,4,181]{3,2,1,0:T(4,128)(2,1)}, bf16[2,4,4,181]{3,2,1,0:T(4,128)(2,1)}, u32[]{:S(2)}, u32[]{:S(2)}) collective-permute-start(bf16[2,4,4,181]{3,2,1,0:T(4,128)(2,1)} %get-tuple-element.6), channel_id=1, source_target_pairs={{9,0},{10,1},{11,2},{12,3},{13,4},{14,5},{15,6},{17,8},{18,9},{19,... | collective-permute-start | bytes 34760 | tf_op jit(solution)/shard_map/ppermute | solution.py:234
  41.3 0.9 pad_maximum_fusion.2
  42.3 4.4 %collective-permute-start.3 = (bf16[2,32,4,181]{3,2,1,0:T(4,128)(2,1)}, bf16[2,32,4,181]{3,2,1,0:T(4,128)(2,1)}, u32[]{:S(2)}, u32[]{:S(2)}) collective-permute-start(bf16[2,32,4,181]{3,2,1,0:T(4,128)(2,1)} %get-tuple-element.11), channel_id=1, source_target_pairs={{0,1},{1,2},{2,3},{3,4},{4,5},{5,6},{6,7},{8,9},{9,10},{10,11},{11... | collective-permute-start | bytes 278024 | tf_op jit(solution)/shard_map/ppermute | solution.py:234
  46.7 0.8 pad_maximum_fusion.3
  47.5 0.6 fusion.68
  48.1 0.6 fusion.75
  48.7 0.5 and_select_fusion
  49.3 0.6 fusion.65
  49.8 0.5 broadcast_subtract_fusion.3
  50.5 1.8 %fusion.1 = f32[18,2,64,64]{3,0,2,1:T(8,128)S(1)} fusion(s32[2,64,64]{2,1,0:T(8,128)S(1)} %copy-done.9, bf16[6,225]{1,0:T(8,128)(2,1)S(1)} %get-tuple-element.16, bf16[6,225]{1,0:T(8,128)(2,1)S(1)} %get-tuple-element.17, bf16[6,225]{1,0:T(8,128)(2,1)S(1)} %get-tuple-element.15), kind=kOutput, calls=%fused_computation.2 | convolution fusion | flops 68222704 | bytes 630692 | tf_op jit(solution)/shard_map/vqkt,ht->vhqk/dot_general | solution.py:280
  52.6 0.7 reduce-precision_convert_fusion.5
  53.3 1.7 %fusion.12 = f32[1,6,64,64]{3,1,2,0:T(8,128)S(1)} fusion(s32[64,64]{1,0:T(8,128)} %get-tuple-element.24, bf16[2,225]{1,0:T(2,128)(2,1)S(1)} %get-tuple-element.22, bf16[2,225]{1,0:T(2,128)(2,1)S(1)} %get-tuple-element.23, bf16[2,225]{1,0:T(2,128)(2,1)S(1)} %get-tuple-element.21), kind=kOutput, calls=%fused_computation.32 | convolution fusion | flops 11988900 | bytes 117388 | tf_op jit(solution)/shard_map/vqkt,ht->vhqk/dot_general | solution.py:280
  55.1 0.7 fusion.34
  55.8 0.9 broadcast_compare_fusion
  56.6 0.8 fusion.61
  57.4 0.4 convolution_convert_fusion
  57.8 0.8 fusion.64
  58.6 1.1 convolution_convert_fusion.2
  59.7 1.9 %collective-permute-start.4 = (bf16[2,32,4,181]{3,2,1,0:T(4,128)(2,1)}, bf16[2,32,4,181]{3,2,1,0:T(4,128)(2,1)S(1)}, u32[]{:S(2)}, u32[]{:S(2)}) collective-permute-start(bf16[2,32,4,181]{3,2,1,0:T(4,128)(2,1)} %get-tuple-element.12), channel_id=1, source_target_pairs={{1,0},{2,1},{3,2},{4,3},{5,4},{6,5},{7,6},{9,8},{10,9},{11,10},{12... | collective-permute-start | bytes 278024 | tf_op jit(solution)/shard_map/ppermute | solution.py:234
  61.6 3.2 %collective-permute-start.1 = (bf16[2,4,32,181]{3,2,1,0:T(8,128)(2,1)}, bf16[2,4,32,181]{3,2,1,0:T(8,128)(2,1)}, u32[]{:S(2)}, u32[]{:S(2)}) collective-permute-start(bf16[2,4,32,181]{3,2,1,0:T(8,128)(2,1)} %get-tuple-element.9), channel_id=1, source_target_pairs={{0,8},{1,9},{2,10},{3,11},{4,12},{5,13},{6,14},{7,15},{8,16},{9,17... | collective-permute-start | bytes 278024 | tf_op jit(solution)/shard_map/ppermute | solution.py:234
  64.9 4.4 %collective-permute-start.6 = (bf16[2,4,32,181]{3,2,1,0:T(8,128)(2,1)}, bf16[2,4,32,181]{3,2,1,0:T(8,128)(2,1)}, u32[]{:S(2)}, u32[]{:S(2)}) collective-permute-start(bf16[2,4,32,181]{3,2,1,0:T(8,128)(2,1)} %get-tuple-element.10), channel_id=1, source_target_pairs={{8,0},{9,1},{10,2},{11,3},{12,4},{13,5},{14,6},{15,7},{16,8},{17,9... | collective-permute-start | bytes 278024 | tf_op jit(solution)/shard_map/ppermute | solution.py:234
  69.3 0.9 copy.97
  70.3 1.0 collective-permute-done.6
  71.3 1.9 %convert_reduce_fusion = s32[40,40]{1,0:T(8,128)S(1)} fusion(bf16[2,4,4,181]{3,2,1,0:T(4,128)(2,1)} %collective-permute-done.7, bf16[2,4,32,181]{3,2,1,0:T(8,128)(2,1)} %collective-permute-done.6, bf16[2,4,4,181]{3,2,1,0:T(4,128)(2,1)} %collective-permute-done.5, bf16[2,32,4,181]{3,2,1,0:T(4,128)(2,1)S(1)} %collective-permute-done.4, ...), kind=kLoop, calls=%fused_computation.44 | loop fusion | flops 32000 | bytes 1164800 | tf_op jit(solution)/shard_map/transpose | solution.py:250
  73.7 2.7 %maximum_maximum_fusion = bf16[2,40,40,181]{3,2,1,0:T(8,128)(2,1)S(1)} fusion(bf16[2,4,4,181]{3,2,1,0:T(4,128)(2,1)} %collective-permute-done.7, bf16[2,4,32,181]{3,2,1,0:T(8,128)(2,1)} %collective-permute-done.6, bf16[2,4,4,181]{3,2,1,0:T(4,128)(2,1)} %collective-permute-done.5, bf16[2,32,4,181]{3,2,1,0:T(4,128)(2,1)S(1)} %collective-permute-done.4, ...), kind=kLoop, calls=%fused_computation.9 | loop fusion | flops 11584000 | bytes 2316800 | tf_op jit(solution)/shard_map/concatenate | solution.py:236
  76.6 27.9 %shard_map.110 = bf16[2,5,320,180]{3,2,1,0:T(8,128)(2,1)S(1)} custom-call(bf16[2,5,320,180]{3,2,1,0:T(8,128)(2,1)S(1)} %bitcast.208, s32[5,320,1]{2,1,0:T(8,128)S(1)} %reshape.816.labq_ref, s32[5,1,320]{2,1,0:T(1,128)S(1)} %reshape.787.labk_ref, f32[2,6,64,64]{3,2,1,0:T(8,128)S(1)} %slice_add_fusion.bias_ref, bf16[2,180,540]{2,1,0:T(8,128)(2,1)S(1)} %copy.73.wqkv_ref, ...), custom_call_target="tpu_custom_call" | custom-call | tf_op jit(solution)/shard_map/pallas_call | solution.py:187
  104.6 0.4 slice_select_fusion
  105.1 0.6 copy-done.2
  105.6 0.4 fusion.21
  106.0 0.4 convolution_add_fusion.7
  106.5 0.4 convolution_add_fusion.6
  106.9 0.4 convolution_add_fusion.5
  107.3 0.4 convolution_add_fusion.4
  107.8 0.4 convolution_add_fusion.3
  108.2 0.4 convolution_add_fusion.2
  108.6 0.4 convolution_add_fusion.1
  109.1 0.5 fusion.11
  109.5 1.0 convert_element_type.62.part_ref
  110.5 13.3 %shard_map.111 = f32[32,1536]{1,0:T(8,128)} custom-call(bf16[32,1536]{1,0:T(8,128)(2,1)} %convert_element_type.62.part_ref), custom_call_target="tpu_custom_call" | custom-call | tf_op jit(solution)/shard_map/pallas_call | solution.py:82
  123.8 0.9 broadcast_multiply_fusion
  125.3 0.4 fusion.24
  125.9 0.5 convolution_convert_fusion.1
  126.3 0.4 copy.93
  126.7 0.3 fusion.10
  127.1 0.7 fusion.83
  127.9 0.4 convolution_convert_fusion.3
  128.3 0.3 copy-done.10
  128.9 2.6 %reshape.794 = f32[4,4,8,8,12,4]{3,2,5,4,1,0:T(8,128)} reshape(f32[16,64,48]{1,2,0:T(8,128)S(1)} %convolution_add_fusion.8) | data formatting | bytes 393216 | tf_op jit(solution)/shard_map/reshape | solution.py:423
  131.5 5.0 %copy.101 = f32[12,4,8,4,8,4]{2,1,5,4,3,0:T(4,128)} copy(f32[12,4,8,4,8,4]{4,2,5,0,3,1:T(8,128)} %bitcast.217) | data formatting | bytes 393216 | tf_op jit(solution)/shard_map/transpose | solution.py:425
  136.4 2.8 %reshape.795 = f32[3,4,32,128]{2,3,1,0:T(8,128)S(1)} reshape(f32[12,4,8,4,8,4]{2,1,5,4,3,0:T(4,128)} %copy.101) | data formatting | bytes 393216 | tf_op jit(solution)/shard_map/reshape | solution.py:426
  139.3 0.9 copy.102
  (64 shorter events, 3.6 us)
Async XLA Ops:
  0.0 125.9 %copy-start = (bf16[48,144]{1,0:T(8,128)(2,1)S(1)}, bf16[48,144]{1,0:T(8,128)(2,1)}, u32[]{:S(2)}) copy-start(bf16[48,144]{1,0:T(8,128)(2,1)} %param.19) | copy-start | bytes 41476
  0.0 5.3 %copy-start.11 = (pred[2]{0:T(512)(128)(4,1)}, pred[2]{0:T(512)(128)(4,1)S(1)}, u32[]{:S(2)}) copy-start(pred[2]{0:T(512)(128)(4,1)S(1)} %fusion.74) | copy-start | bytes 10
  3.5 2.1 %copy-start.8 = (s32[2,64,64]{2,1,0:T(8,128)}, s32[2,64,64]{2,1,0:T(8,128)S(1)}, u32[]{:S(2)}) copy-start(s32[2,64,64]{2,1,0:T(8,128)S(1)} %fusion.33) | copy-start | bytes 98308
  5.3 1.0 copy-start.5
  5.6 3.0 %copy-start.6 = (bf16[2,180,180]{2,0,1:T(2,128)(2,1)S(1)}, bf16[2,180,180]{2,0,1:T(2,128)(2,1)}, u32[]{:S(2)}) copy-start(bf16[2,180,180]{2,0,1:T(2,128)(2,1)} %param.14) | copy-start | bytes 388804
  6.4 2.3 %copy-start.4 = (bf16[32,32,180]{2,1,0:T(8,128)(2,1)S(1)}, bf16[32,32,180]{2,1,0:T(8,128)(2,1)}, u32[]{:S(2)}) copy-start(bf16[32,32,180]{2,1,0:T(8,128)(2,1)} %param.11) | copy-start | bytes 1105924
  23.0 48.4 %copy-start.1 = (bf16[2,4,4,8,8,180]{5,4,2,3,1,0:T(8,128)(2,1)}, bf16[2,4,4,8,8,180]{5,4,2,3,1,0:T(8,128)(2,1)S(1)}, u32[]{:S(2)}) copy-start(bf16[2,4,4,8,8,180]{5,4,2,3,1,0:T(8,128)(2,1)S(1)} %copy.77) | copy-start | bytes 2211844
  24.0 35.7 %collective-permute-start = (bf16[2,4,4,181]{3,2,1,0:T(4,128)(2,1)}, bf16[2,4,4,181]{3,2,1,0:T(4,128)(2,1)S(1)}, u32[]{:S(2)}, u32[]{:S(2)}) collective-permute-start(bf16[2,4,4,181]{3,2,1,0:T(4,128)(2,1)} %get-tuple-element.5), channel_id=1, source_target_pairs={{0,9},{1,10},{2,11},{3,12},{4,13},{5,14},{6,15},{8,17},{9,18},{10,... | collective-permute-start | bytes 34760 | tf_op jit(solution)/shard_map/ppermute | solution.py:234
  29.7 31.9 %collective-permute-start.2 = (bf16[2,4,4,181]{3,2,1,0:T(4,128)(2,1)}, bf16[2,4,4,181]{3,2,1,0:T(4,128)(2,1)}, u32[]{:S(2)}, u32[]{:S(2)}) collective-permute-start(bf16[2,4,4,181]{3,2,1,0:T(4,128)(2,1)} %get-tuple-element.8), channel_id=1, source_target_pairs={{1,8},{2,9},{3,10},{4,11},{5,12},{6,13},{7,14},{9,16},{10,17},{11,... | collective-permute-start | bytes 34760 | tf_op jit(solution)/shard_map/ppermute | solution.py:234
  31.7 33.2 %collective-permute-start.5 = (bf16[2,4,4,181]{3,2,1,0:T(4,128)(2,1)}, bf16[2,4,4,181]{3,2,1,0:T(4,128)(2,1)}, u32[]{:S(2)}, u32[]{:S(2)}) collective-permute-start(bf16[2,4,4,181]{3,2,1,0:T(4,128)(2,1)} %get-tuple-element.7), channel_id=1, source_target_pairs={{8,1},{9,2},{10,3},{11,4},{12,5},{13,6},{14,7},{16,9},{17,10},{18,... | collective-permute-start | bytes 34760 | tf_op jit(solution)/shard_map/ppermute | solution.py:234
  39.3 11.2 %copy-start.9 = (s32[2,64,64]{2,1,0:T(8,128)S(1)}, s32[2,64,64]{2,1,0:T(8,128)}, u32[]{:S(2)}) copy-start(s32[2,64,64]{2,1,0:T(8,128)} %copy-done.8) | copy-start | bytes 98308
  39.3 31.0 %collective-permute-start.7 = (bf16[2,4,4,181]{3,2,1,0:T(4,128)(2,1)}, bf16[2,4,4,181]{3,2,1,0:T(4,128)(2,1)}, u32[]{:S(2)}, u32[]{:S(2)}) collective-permute-start(bf16[2,4,4,181]{3,2,1,0:T(4,128)(2,1)} %get-tuple-element.6), channel_id=1, source_target_pairs={{9,0},{10,1},{11,2},{12,3},{13,4},{14,5},{15,6},{17,8},{18,9},{19,... | collective-permute-start | bytes 34760 | tf_op jit(solution)/shard_map/ppermute | solution.py:234
  42.3 28.0 %collective-permute-start.3 = (bf16[2,32,4,181]{3,2,1,0:T(4,128)(2,1)}, bf16[2,32,4,181]{3,2,1,0:T(4,128)(2,1)}, u32[]{:S(2)}, u32[]{:S(2)}) collective-permute-start(bf16[2,32,4,181]{3,2,1,0:T(4,128)(2,1)} %get-tuple-element.11), channel_id=1, source_target_pairs={{0,1},{1,2},{2,3},{3,4},{4,5},{5,6},{6,7},{8,9},{9,10},{10,11},{11... | collective-permute-start | bytes 278024 | tf_op jit(solution)/shard_map/ppermute | solution.py:234
  52.5 4.9 %copy-start.3 = (bf16[9,180,48]{1,2,0:T(8,128)(2,1)S(1)}, bf16[9,180,48]{1,2,0:T(8,128)(2,1)}, u32[]{:S(2)}) copy-start(bf16[9,180,48]{1,2,0:T(8,128)(2,1)} %param.18) | copy-start | bytes 466564
  59.7 10.6 %collective-permute-start.4 = (bf16[2,32,4,181]{3,2,1,0:T(4,128)(2,1)}, bf16[2,32,4,181]{3,2,1,0:T(4,128)(2,1)S(1)}, u32[]{:S(2)}, u32[]{:S(2)}) collective-permute-start(bf16[2,32,4,181]{3,2,1,0:T(4,128)(2,1)} %get-tuple-element.12), channel_id=1, source_target_pairs={{1,0},{2,1},{3,2},{4,3},{5,4},{6,5},{7,6},{9,8},{10,9},{11,10},{12... | collective-permute-start | bytes 278024 | tf_op jit(solution)/shard_map/ppermute | solution.py:234
  61.6 8.6 %collective-permute-start.1 = (bf16[2,4,32,181]{3,2,1,0:T(8,128)(2,1)}, bf16[2,4,32,181]{3,2,1,0:T(8,128)(2,1)}, u32[]{:S(2)}, u32[]{:S(2)}) collective-permute-start(bf16[2,4,32,181]{3,2,1,0:T(8,128)(2,1)} %get-tuple-element.9), channel_id=1, source_target_pairs={{0,8},{1,9},{2,10},{3,11},{4,12},{5,13},{6,14},{7,15},{8,16},{9,17... | collective-permute-start | bytes 278024 | tf_op jit(solution)/shard_map/ppermute | solution.py:234
  64.9 6.4 %collective-permute-start.6 = (bf16[2,4,32,181]{3,2,1,0:T(8,128)(2,1)}, bf16[2,4,32,181]{3,2,1,0:T(8,128)(2,1)}, u32[]{:S(2)}, u32[]{:S(2)}) collective-permute-start(bf16[2,4,32,181]{3,2,1,0:T(8,128)(2,1)} %get-tuple-element.10), channel_id=1, source_target_pairs={{8,0},{9,1},{10,2},{11,3},{12,4},{13,5},{14,6},{15,7},{16,8},{17,9... | collective-permute-start | bytes 278024 | tf_op jit(solution)/shard_map/ppermute | solution.py:234
  104.6 1.0 copy-start.2
  125.2 1.5 %copy-start.7 = (pred[16,64,64]{1,2,0:T(8,128)(4,1)S(1)}, pred[16,64,64]{1,2,0:T(8,128)(4,1)}, u32[]{:S(2)}) copy-start(pred[16,64,64]{1,2,0:T(8,128)(4,1)} %broadcast_compare_fusion) | copy-start | bytes 196612
  127.9 0.7 copy-start.10

commit v8 on v6

--- a/solution.py
+++ b/solution.py
@@ -36,15 +36,13 @@
     return cells
 
 
-def var_sum_kernel(count, part_ref, out_ref, held, send_sem, recv_sem, own_sem):
+def var_sum_kernel(count, part_ref, out_ref, held, send_sem, recv_sem):
     me = lax.axis_index("var")
     barrier = pltpu.get_barrier_semaphore()
     for step in range(1, count):
         peer = lax.rem(me + step, count)
         pl.semaphore_signal(barrier, inc=1, device_id={"var": peer}, device_id_type=MESH)
     pl.semaphore_wait(barrier, count - 1)
-    own = pltpu.make_async_copy(part_ref, held.at[me], own_sem)
-    own.start()
     sends = []
     for step in range(1, count):
         peer = lax.rem(me + step, count)
@@ -58,7 +56,7 @@
         )
         copy.start()
         sends.append(copy)
-    own.wait()
+    held[me] = part_ref[...]
     for copy in sends:
         copy.wait_send()
     for step in range(1, count):
@@ -88,7 +86,6 @@
             pltpu.VMEM((count,) + part.shape, part.dtype),
             pltpu.SemaphoreType.DMA((count - 1,)),
             pltpu.SemaphoreType.DMA((count,)),
-            pltpu.SemaphoreType.DMA(()),
         ],
         compiler_params=pltpu.CompilerParams(collective_id=0, has_side_effects=True),
     )(part)

time: 120 us -> 120 us (level)
  no operation moved by 1% of the time
where the time goes in v8:
time: 120 us; the launch traced here: 119 us
  Pallas kernels  54.6 us (46%)
  local copies, waits for them, and re-layouts  21.4 us (18%)
  matrix products  13.8 us (12%)
  starting transfers between devices  11.9 us (10%)
  other arithmetic  11 us (9%)
  waiting for transfers between devices  5.4 us (4%)
    pallas_call x2, Pallas kernels, swin_block(): pl.pallas_call(functools.partial(block_kernel, variants, heads, scale), o...  42.3 us
    pallas_call x1, Pallas kernels, var_sum(): pl.pallas_call(functools.partial(var_sum_kernel, count), out_shape=jax.Sh...  12.4 us
    ppermute x2, starting transfers between devices, extended(): lax.ppermute(head, axis, [((i + 1) % count, i) for i in range(ends)])  6.54 us
    ppermute x2, starting transfers between devices, extended(): lax.ppermute(tail, axis, [(i, (i + 1) % count) for i in range(ends)])  5.41 us
    ppermute x2, waiting for transfers between devices, extended(): lax.ppermute(head, axis, [((i + 1) % count, i) for i in range(ends)])  4.89 us
    dot_general x3, matrix products, bias_table(): jnp.einsum('vqkt,ht->vhqk', one_hot, parts, preferred_element_type=jnp.fl...  4.62 us
    unnamed x32, local copies, waits for them, and re-layouts  4.04 us
    dot_general x9, matrix products, reconstruct(): jnp.einsum('vrcd,vde->vrce', window, kernels[:, kernel_spot], preferred_e...  3.84 us
  transfers between devices with their start and end apart: 4, of which 2 were waited for; matrix products, arithmetic and copies ran while one was open for 7% of the time, Pallas kernels for 0%

profile of v8, /device:TPU:153, one launch (start us, length us, event | category | flops | bytes accessed | tf_op | source)
XLA Modules:
  0.0 118.7 jit_solution(5898820796916693232)
XLA Ops:
  0.0 0.8 reshape_broadcast_in_dim.9
  1.2 0.7 convert_element_type.57
  1.9 0.8 fusion.82
  2.9 1.8 %fusion.2 = f32[18,2,64,64]{3,0,2,1:T(8,128)S(1)} fusion(s32[2,64,64]{2,1,0:T(8,128)S(1)} %fusion.33, bf16[6,225]{1,0:T(8,128)(2,1)S(1)} %get-tuple-element.30, bf16[6,225]{1,0:T(8,128)(2,1)S(1)} %get-tuple-element.29, bf16[6,225]{1,0:T(8,128)(2,1)S(1)} %get-tuple-element.31), kind=kOutput, calls=%fused_computation.3 | convolution fusion | flops 68222704 | bytes 630692 | tf_op jit(solution)/shard_map/vqkt,ht->vhqk/dot_general | solution.py:255
  4.7 0.2 copy.155
  5.0 0.7 copy-done.6
  5.9 0.3 copy.76.wdown_ref
  6.3 0.9 copy.74.wp_ref
  7.2 1.1 copy.68
  8.3 14.1 %shard_map.109 = bf16[2,4,256,180]{3,2,1,0:T(8,128)(2,1)S(1)} custom-call(bf16[1,4,256,180]{3,2,1,0:T(8,128)(2,1)S(1)} %bitcast.211, s32[4,256,1]{2,1,0:T(8,128)S(1)} %reshape.815.labq_ref, s32[4,1,256]{2,1,0:T(1,128)S(1)} %reshape.782.labk_ref, f32[2,6,64,64]{3,2,1,0:T(8,128)S(1)} %slice_add_fusion.2.bias_ref, bf16[2,180,540]{2,1,0:T(8,128)(2,1)S(1)} %copy.73.wqkv_ref, ...), custom_call_target="tpu_custom_call" | custom-call | tf_op jit(solution)/shard_map/pallas_call | solution.py:184
  22.6 0.2 broadcast_in_dim.264
  22.8 0.9 pad_maximum_fusion.6
  23.7 2.6 %collective-permute-start = (bf16[2,32,4,181]{3,2,1,0:T(4,128)(2,1)}, bf16[2,32,4,181]{3,2,1,0:T(4,128)(2,1)S(1)}, u32[]{:S(2)}, u32[]{:S(2)}) collective-permute-start(bf16[2,32,4,181]{3,2,1,0:T(4,128)(2,1)} %get-tuple-element.7), channel_id=1, source_target_pairs={{0,1},{1,2},{2,3},{3,4},{4,5},{5,6},{6,7},{8,9},{9,10},{10,11},{11... | collective-permute-start | bytes 278024 | tf_op jit(solution)/shard_map/ppermute | solution.py:30
  26.3 3.9 %collective-permute-start.1 = (bf16[2,32,4,181]{3,2,1,0:T(4,128)(2,1)}, bf16[2,32,4,181]{3,2,1,0:T(4,128)(2,1)}, u32[]{:S(2)}, u32[]{:S(2)}) collective-permute-start(bf16[2,32,4,181]{3,2,1,0:T(4,128)(2,1)} %get-tuple-element.8), channel_id=1, source_target_pairs={{1,0},{2,1},{3,2},{4,3},{5,4},{6,5},{7,6},{9,8},{10,9},{11,10},{12... | collective-permute-start | bytes 278024 | tf_op jit(solution)/shard_map/ppermute | solution.py:32
  30.2 0.6 fusion.75
  30.9 1.8 %fusion.1 = f32[18,2,64,64]{3,0,2,1:T(8,128)S(1)} fusion(s32[2,64,64]{2,1,0:T(8,128)S(1)} %fusion.33, bf16[6,225]{1,0:T(8,128)(2,1)S(1)} %get-tuple-element.12, bf16[6,225]{1,0:T(8,128)(2,1)S(1)} %get-tuple-element.13, bf16[6,225]{1,0:T(8,128)(2,1)S(1)} %get-tuple-element.11), kind=kOutput, calls=%fused_computation.2 | convolution fusion | flops 68222704 | bytes 630692 | tf_op jit(solution)/shard_map/vqkt,ht->vhqk/dot_general | solution.py:255
  32.7 0.2 copy.154
  33.1 0.4 copy-done.12
  33.4 1.0 fusion.12
  34.5 0.7 copy.97
  35.2 0.8 broadcast_compare_fusion
  36.2 1.3 %convolution_convert_fusion = bf16[2,9,180,48]{2,1,3,0:T(8,128)(2,1)S(1)} fusion(bf16[9,180,48]{1,2,0:T(8,128)(2,1)} %param.18, s32[2,9]{1,0:T(2,128)S(1)} %fusion.61), kind=kOutput, calls=%fused_computation.11 | convolution fusion | flops 2955042 | bytes 466632 | tf_op jit(solution)/shard_map/vpq,qcs->vpcs/dot_general | solution.py:283
  37.6 1.1 convolution_convert_fusion.2
  38.7 0.9 pad_maximum_fusion.4
  39.7 2.8 %collective-permute-start.2 = (bf16[2,4,40,181]{3,2,1,0:T(8,128)(2,1)S(1)}, bf16[2,4,40,181]{3,2,1,0:T(8,128)(2,1)S(1)}, u32[]{:S(2)}, u32[]{:S(2)}) collective-permute-start(bf16[2,4,40,181]{3,2,1,0:T(8,128)(2,1)S(1)} %get-tuple-element.5), channel_id=1, source_target_pairs={{0,8},{8,16},{16,24},{24,32},{32,40},{40,48},{48,56},{1,9},{9,17},... | collective-permute-start | bytes 347528 | tf_op jit(solution)/shard_map/ppermute | solution.py:30
  42.5 2.7 %collective-permute-start.3 = (bf16[2,4,40,181]{3,2,1,0:T(8,128)(2,1)S(1)}, bf16[2,4,40,181]{3,2,1,0:T(8,128)(2,1)S(1)}, u32[]{:S(2)}, u32[]{:S(2)}) collective-permute-start(bf16[2,4,40,181]{3,2,1,0:T(8,128)(2,1)S(1)} %get-tuple-element.6), channel_id=1, source_target_pairs={{8,0},{16,8},{24,16},{32,24},{40,32},{48,40},{56,48},{9,1},{17,9},... | collective-permute-start | bytes 347528 | tf_op jit(solution)/shard_map/ppermute | solution.py:32
  45.2 0.5 collective-permute-done.2
  45.7 4.9 %collective-permute-done.3 = bf16[2,4,40,181]{3,2,1,0:T(8,128)(2,1)S(1)} collective-permute-done((bf16[2,4,40,181]{3,2,1,0:T(8,128)(2,1)S(1)}, bf16[2,4,40,181]{3,2,1,0:T(8,128)(2,1)S(1)}, u32[]{:S(2)}, u32[]{:S(2)}) %collective-permute-start.3) | collective-permute-done | bytes 115872 | tf_op jit(solution)/shard_map/ppermute | solution.py:32
  50.6 0.7 copy-done.5
  51.3 1.8 %convert_reduce_fusion = s32[40,40]{1,0:T(8,128)S(1)} fusion(bf16[2,4,40,181]{3,2,1,0:T(8,128)(2,1)S(1)} %collective-permute-done.3, bf16[2,4,40,181]{3,2,1,0:T(8,128)(2,1)S(1)} %collective-permute-done.2, bf16[2,32,4,181]{3,2,1,0:T(4,128)(2,1)} %collective-permute-done.1, bf16[2,32,4,181]{3,2,1,0:T(4,128)(2,1)S(1)} %collective-permute-done, ...), kind=kLoop, calls=%fused_computation.44 | loop fusion | flops 19200 | bytes 1164800 | tf_op jit(solution)/shard_map/transpose | solution.py:225
  53.2 0.7 copy.80
  53.9 0.3 reshape.816.labq_ref
  54.1 1.0 reshape.787.labk_ref
  55.1 2.4 %pad_maximum_fusion = bf16[2,40,40,181]{3,2,1,0:T(8,128)(2,1)S(1)} fusion(bf16[2,4,40,181]{3,2,1,0:T(8,128)(2,1)} %copy-done.5, bf16[2,32,4,181]{3,2,1,0:T(4,128)(2,1)} %collective-permute-done.1, bf16[2,32,32,1]{3,2,1,0:T(8,128)(2,1)S(1)} %broadcast_in_dim.264, bf16[2,32,32,180]{3,2,1,0:T(8,128)(2,1)} %bitcast.215, ...), kind=kLoop, calls=%fused_computation.9 | loop fusion | flops 6950400 | bytes 2316800 | tf_op jit(solution)/shard_map/concatenate | solution.py:28
  57.8 28.2 %shard_map.110 = bf16[2,5,320,180]{3,2,1,0:T(8,128)(2,1)S(1)} custom-call(bf16[2,5,320,180]{3,2,1,0:T(8,128)(2,1)S(1)} %bitcast.208, s32[5,320,1]{2,1,0:T(8,128)S(1)} %reshape.816.labq_ref, s32[5,1,320]{2,1,0:T(1,128)S(1)} %reshape.787.labk_ref, f32[2,6,64,64]{3,2,1,0:T(8,128)S(1)} %slice_add_fusion.bias_ref, bf16[2,180,540]{2,1,0:T(8,128)(2,1)S(1)} %copy.73.wqkv_ref, ...), custom_call_target="tpu_custom_call" | custom-call | tf_op jit(solution)/shard_map/pallas_call | solution.py:184
  86.1 0.4 slice_select_fusion
  86.5 0.6 copy-done.2
  87.1 0.4 fusion.21
  87.5 0.4 convolution_add_fusion.7
  87.9 0.4 convolution_add_fusion.6
  88.4 0.4 convolution_add_fusion.5
  88.8 0.4 convolution_add_fusion.4
  89.2 0.4 convolution_add_fusion.3
  89.7 0.4 convolution_add_fusion.2
  90.1 0.4 convolution_add_fusion.1
  90.5 0.5 fusion.11
  91.0 1.0 convert_element_type.62.part_ref
  92.0 12.4 %shard_map.111 = f32[32,1536]{1,0:T(8,128)} custom-call(bf16[32,1536]{1,0:T(8,128)(2,1)} %convert_element_type.62.part_ref), custom_call_target="tpu_custom_call" | custom-call | tf_op jit(solution)/shard_map/pallas_call | solution.py:80
  104.3 0.9 broadcast_multiply_fusion
  105.3 0.2 div.142
  105.5 0.2 bitcast_reduce_fusion
  105.8 0.4 fusion.24
  106.4 0.5 convolution_convert_fusion.1
  106.9 0.4 copy.93
  107.3 0.3 fusion.10
  107.6 0.7 fusion.83
  108.3 0.2 copy.100
  108.5 0.4 convolution_convert_fusion.3
  108.9 0.3 copy-done.11
  109.2 1.0 convolution_add_fusion.8
  110.2 1.9 %reshape.794 = f32[4,4,8,8,12,4]{3,2,5,4,1,0:T(8,128)S(1)} reshape(f32[16,64,48]{1,2,0:T(8,128)} %convolution_add_fusion.8) | data formatting | bytes 393216 | tf_op jit(solution)/shard_map/reshape | solution.py:398
  112.1 2.9 %copy.101 = f32[12,4,8,4,8,4]{2,1,5,4,3,0:T(4,128)} copy(f32[12,4,8,4,8,4]{4,2,5,0,3,1:T(8,128)S(1)} %bitcast.216) | data formatting | bytes 393216 | tf_op jit(solution)/shard_map/transpose | solution.py:400
  115.0 2.8 %reshape.795 = f32[3,4,32,128]{2,3,1,0:T(8,128)S(1)} reshape(f32[12,4,8,4,8,4]{2,1,5,4,3,0:T(4,128)} %copy.101) | data formatting | bytes 393216 | tf_op jit(solution)/shard_map/reshape | solution.py:401
  117.8 0.9 copy.102
  (59 shorter events, 2.1 us)
Async XLA Ops:
  0.0 106.4 %copy-start = (bf16[48,144]{1,0:T(8,128)(2,1)S(1)}, bf16[48,144]{1,0:T(8,128)(2,1)}, u32[]{:S(2)}) copy-start(bf16[48,144]{1,0:T(8,128)(2,1)} %param.19) | copy-start | bytes 41476
  4.7 1.0 copy-start.6
  4.9 1.0 copy-start.7
  5.0 1.2 %copy-start.8 = (bf16[2,180,360]{2,0,1:T(2,128)(2,1)S(1)}, bf16[2,180,360]{2,0,1:T(2,128)(2,1)}, u32[]{:S(2)}) copy-start(bf16[2,180,360]{2,0,1:T(2,128)(2,1)} %param.15) | copy-start | bytes 777604
  22.5 28.1 %copy-start.1 = (bf16[2,4,4,8,8,180]{5,4,2,3,1,0:T(8,128)(2,1)}, bf16[2,4,4,8,8,180]{5,4,2,3,1,0:T(8,128)(2,1)S(1)}, u32[]{:S(2)}) copy-start(bf16[2,4,4,8,8,180]{5,4,2,3,1,0:T(8,128)(2,1)S(1)} %copy.77) | copy-start | bytes 2211844
  23.7 15.0 %collective-permute-start = (bf16[2,32,4,181]{3,2,1,0:T(4,128)(2,1)}, bf16[2,32,4,181]{3,2,1,0:T(4,128)(2,1)S(1)}, u32[]{:S(2)}, u32[]{:S(2)}) collective-permute-start(bf16[2,32,4,181]{3,2,1,0:T(4,128)(2,1)} %get-tuple-element.7), channel_id=1, source_target_pairs={{0,1},{1,2},{2,3},{3,4},{4,5},{5,6},{6,7},{8,9},{9,10},{10,11},{11... | collective-permute-start | bytes 278024 | tf_op jit(solution)/shard_map/ppermute | solution.py:30
  26.3 12.4 %collective-permute-start.1 = (bf16[2,32,4,181]{3,2,1,0:T(4,128)(2,1)}, bf16[2,32,4,181]{3,2,1,0:T(4,128)(2,1)}, u32[]{:S(2)}, u32[]{:S(2)}) collective-permute-start(bf16[2,32,4,181]{3,2,1,0:T(4,128)(2,1)} %get-tuple-element.8), channel_id=1, source_target_pairs={{1,0},{2,1},{3,2},{4,3},{5,4},{6,5},{7,6},{9,8},{10,9},{11,10},{12... | collective-permute-start | bytes 278024 | tf_op jit(solution)/shard_map/ppermute | solution.py:32
  32.7 0.7 copy-start.12
  33.0 3.1 %copy-start.13 = (s32[9]{0:T(128)S(1)}, s32[9]{0:T(128)}, u32[]{:S(2)}) copy-start(s32[9]{0:T(128)} %get-tuple-element.37) | copy-start | bytes 112
  39.7 6.1 %collective-permute-start.2 = (bf16[2,4,40,181]{3,2,1,0:T(8,128)(2,1)S(1)}, bf16[2,4,40,181]{3,2,1,0:T(8,128)(2,1)S(1)}, u32[]{:S(2)}, u32[]{:S(2)}) collective-permute-start(bf16[2,4,40,181]{3,2,1,0:T(8,128)(2,1)S(1)} %get-tuple-element.5), channel_id=1, source_target_pairs={{0,8},{8,16},{16,24},{24,32},{32,40},{40,48},{48,56},{1,9},{9,17},... | collective-permute-start | bytes 347528 | tf_op jit(solution)/shard_map/ppermute | solution.py:30
  42.5 8.2 %collective-permute-start.3 = (bf16[2,4,40,181]{3,2,1,0:T(8,128)(2,1)S(1)}, bf16[2,4,40,181]{3,2,1,0:T(8,128)(2,1)S(1)}, u32[]{:S(2)}, u32[]{:S(2)}) collective-permute-start(bf16[2,4,40,181]{3,2,1,0:T(8,128)(2,1)S(1)} %get-tuple-element.6), channel_id=1, source_target_pairs={{8,0},{16,8},{24,16},{32,24},{40,32},{48,40},{56,48},{9,1},{17,9},... | collective-permute-start | bytes 347528 | tf_op jit(solution)/shard_map/ppermute | solution.py:32
  45.7 4.9 %copy-start.3 = (bf16[2,4,40,181]{3,2,1,0:T(8,128)(2,1)}, bf16[2,4,40,181]{3,2,1,0:T(8,128)(2,1)S(1)}, u32[]{:S(2)}) copy-start(bf16[2,4,40,181]{3,2,1,0:T(8,128)(2,1)S(1)} %collective-permute-done.2) | copy-start | bytes 347524
  50.6 0.7 copy-start.5
  53.1 2.1 %copy-start.4 = (bf16[2,4,40,181]{3,2,1,0:T(8,128)(2,1)S(1)}, bf16[2,4,40,181]{3,2,1,0:T(8,128)(2,1)}, u32[]{:S(2)}) copy-start(bf16[2,4,40,181]{3,2,1,0:T(8,128)(2,1)} %copy-done.3) | copy-start | bytes 347524
  86.1 1.0 copy-start.2
  105.8 1.5 %copy-start.9 = (pred[16,64,64]{1,2,0:T(8,128)(4,1)S(1)}, pred[16,64,64]{1,2,0:T(8,128)(4,1)}, u32[]{:S(2)}) copy-start(pred[16,64,64]{1,2,0:T(8,128)(4,1)} %broadcast_compare_fusion) | copy-start | bytes 196612
  105.8 1.5 %copy-start.10 = (f32[2,64,64]{1,2,0:T(8,128)S(1)}, f32[2,64,64]{1,2,0:T(8,128)}, u32[]{:S(2)}) copy-start(f32[2,64,64]{1,2,0:T(8,128)} %copy.97) | copy-start | bytes 98308
  108.5 0.7 copy-start.11
